TPU v7x, 32 devices: a whole 2x2x4 slice. The times are simulated.
32 devices in a mesh: req: 8 (over z, y), tp: 4 (over x, core).
Axes of the slice: x: 2, y: 2, z: 4, core: 2. Of those that a mesh axis runs over, the one named last changes fastest.
Arguments:
- tokens: bfloat16 [16, 256, 2048], P('req'), may hold values from -6 to 6
- attn_gain: float32 [2048], replicated, may hold values from 0.25 to 1.75
- w_query: bfloat16 [2048, 1280], P(None, 'tp'), may hold values from -0.125 to 0.125
- key_value_weight: bfloat16 [2048, 640], replicated, may hold values from -0.125 to 0.125
- w_out: bfloat16 [1280, 2048], P('tp'), may hold values from -0.15625 to 0.15625
- q_gain: float32 [64], replicated, as said below
- k_gain: float32 [64], replicated, as said below
- stored: bfloat16 [8, 5, 2048, 128], P('req'), may hold values from -6 to 6
- continuing: int32 [16], replicated, may hold values from 0 to 1, as said below
- cache_row: int32 [16], replicated, may hold values from -1 to 7, as said below
- cache_len: int32 [16], replicated, may hold values from 0 to 2048, as said below
Outputs:
- layer: bfloat16 [16, 256, 2048], P('req')
- decoding_group_cache: bfloat16 [32, 5, 1152, 128], P('req', None, 'tp')
Inputs may be any that keep to these rules, and one draw needn't show every extreme that they name: `continuing`: exactly 8 requests have 1. `cache_row`: a continuing request's row of stored; every row belongs to exactly one continuing request; -1 for the others. `cache_len`: 1 to 2048 for a continuing request, 2048 for at least one; 0 for the others. `q_gain`: positive. `k_gain`: positive.
All inputs are finite; a program needn't handle non-finite values.
Results may differ from a plain program's by a relative error of at most 0.005.
The roundings to bfloat16 on the way count: a program that leaves them out, or rounds other values in their place, can miss the bound.
Values may be sent and summed in bfloat16 or wider, within the bound.
No kernel may reach another device: no remote copies, remote signals or barrier semaphores. Data moves between devices by JAX's collectives and lax.ppermute only.
A program may use at most 128 MiB of HBM per device.

v0:
```python
import math

import jax
import jax.numpy as jnp
from jax import lax
from jax.sharding import PartitionSpec as P


def swapped(value, axis, apart):
    mask = 2**apart
    pairs = [(source, source ^ mask) for source in range(lax.axis_size(axis))]
    return lax.ppermute(value, axis, pairs)


def normalize(values, gain):
    return values * lax.rsqrt(jnp.mean(values * values, axis=-1, keepdims=True) + 1e-06) * gain


def rotary(values, positions):
    half_dim = values.shape[-1] // 2
    freq = jnp.exp(
        -math.log(10000.0) * jnp.arange(half_dim).astype(jnp.float32) * 2.0 / values.shape[-1]
    )
    angle = positions.astype(jnp.float32)[..., None] * freq
    cosine = jnp.cos(angle)[..., None, :]
    sine = jnp.sin(angle)[..., None, :]
    first_half = values[..., :half_dim]
    second_half = values[..., half_dim:]
    return jnp.concatenate(
        [first_half * cosine - second_half * sine, second_half * cosine + first_half * sine],
        axis=-1,
    )


def attend(query_one, keys_one, allowed, head_dim, new_count, scale):
    scores = (
        jnp.einsum(
            "hqd,hkd->hqk", query_one, keys_one[..., :head_dim], preferred_element_type=jnp.float32
        )
        * scale
    )
    scores = jnp.where(allowed[None], scores, -jnp.inf)
    row_max = jnp.max(scores, axis=-1, keepdims=True)
    weights = jnp.exp(scores - row_max)
    probs = (weights / jnp.sum(weights, axis=-1, keepdims=True)).astype(jnp.bfloat16)
    mixed = jnp.einsum(
        "hqk,hkd->qhd", probs, keys_one[..., head_dim:], preferred_element_type=jnp.float32
    )
    return mixed.astype(jnp.bfloat16).reshape(new_count, query_one.shape[0] * head_dim)


def on_device(
    tokens,
    attn_gain,
    w_query,
    key_value_weight,
    w_out,
    q_gain,
    k_gain,
    stored,
    continuing,
    cache_row,
    cache_len,
):
    tp_count = lax.axis_size("tp")
    req_place = lax.axis_index("req")
    tp_place = lax.axis_index("tp")
    req_dev, new_count, width = tokens.shape
    head_dim = q_gain.shape[0]
    kv_heads = key_value_weight.shape[1] // (2 * head_dim)
    local_heads = w_query.shape[1] // head_dim
    query_group_ratio = local_heads * tp_count // kv_heads
    cache_span = stored.shape[2]
    total_length = cache_span + new_count
    scale = 1.0 / math.sqrt(head_dim)
    relayed = lax.all_to_all(stored, "req", split_axis=2, concat_axis=0, tiled=True)
    live_all = continuing == 1
    rows_all = jnp.where(live_all, cache_row, 0)
    select_chosen = jnp.take(relayed, rows_all, axis=0)
    stored_entries = lax.all_to_all(
        jnp.where(live_all[:, None, None, None], select_chosen, jnp.zeros_like(select_chosen)),
        "req",
        split_axis=0,
        concat_axis=2,
        tiled=True,
    )
    first = req_place * req_dev
    my_live = lax.dynamic_slice_in_dim(continuing, first, req_dev) == 1
    my_len = jnp.where(my_live, lax.dynamic_slice_in_dim(cache_len, first, req_dev), 0)
    position = jnp.arange(cache_span, dtype=jnp.int32)
    stored_entries = jnp.where(
        (position[None, :] < my_len[:, None])[:, None, :, None],
        stored_entries,
        jnp.zeros_like(stored_entries),
    )
    token_rows = tokens.reshape(req_dev * new_count, width)
    normalized_input = normalize(token_rows.astype(jnp.float32), attn_gain).astype(jnp.bfloat16)
    positions = my_len[:, None] + jnp.arange(new_count, dtype=jnp.int32)[None, :]
    query = jnp.dot(normalized_input, w_query, preferred_element_type=jnp.float32).reshape(
        req_dev, new_count, local_heads, head_dim
    )
    query = rotary(normalize(query, q_gain), positions).astype(jnp.bfloat16)
    key_value_rows = jnp.dot(
        normalized_input, key_value_weight, preferred_element_type=jnp.float32
    ).reshape(req_dev, new_count, kv_heads, 2 * head_dim)
    keys_new = rotary(normalize(key_value_rows[..., :head_dim], k_gain), positions)
    fresh = jnp.concatenate([keys_new, key_value_rows[..., head_dim:]], axis=-1).astype(
        jnp.bfloat16
    )
    fresh = jnp.transpose(fresh, (0, 2, 1, 3))
    keys_all = jnp.concatenate([stored_entries, fresh], axis=2)
    head_select = (
        tp_place * local_heads + jnp.arange(local_heads, dtype=jnp.int32)
    ) // query_group_ratio
    query_index = jnp.arange(new_count, dtype=jnp.int32)[:, None]
    key_index = jnp.arange(total_length, dtype=jnp.int32)[None, :]
    outputs = []
    for number in range(req_dev):
        query_one = jnp.transpose(query[number], (1, 0, 2))
        chosen = jnp.take(keys_all[number], head_select, axis=0)
        allowed = jnp.where(
            key_index < cache_span,
            key_index < my_len[number],
            key_index - cache_span <= query_index,
        )
        mixed = attend(query_one, chosen, allowed, head_dim, new_count, scale)
        outputs.append(mixed)
    mixed_all = jnp.concatenate(outputs, axis=0)
    summed = lax.psum(jnp.dot(mixed_all, w_out, preferred_element_type=jnp.float32), "tp")
    layer = (token_rows.astype(jnp.float32) + summed).astype(jnp.bfloat16)
    layer = layer.reshape(req_dev, new_count, width)
    padded_tokens = jnp.concatenate(
        [stored_entries, jnp.zeros((req_dev, kv_heads, new_count, 2 * head_dim), jnp.bfloat16)],
        axis=2,
    )
    whole = jax.vmap(
        lambda padded_one, fresh_one, offset: lax.dynamic_update_slice_in_dim(
            padded_one, fresh_one, offset, 1
        )
    )(padded_tokens, fresh, my_len)
    half_span = total_length // 2
    segment = half_span // tp_count
    pair_side = req_place % 2
    kept_half = lax.dynamic_slice_in_dim(
        whole, pair_side * half_span + tp_place * segment, segment, 2
    )
    sent_half = lax.dynamic_slice_in_dim(
        whole, (1 - pair_side) * half_span + tp_place * segment, segment, 2
    )
    partner = swapped(sent_half, "req", 0)
    decoding_group_cache = jnp.where(
        pair_side == 0,
        jnp.concatenate([kept_half, partner], axis=0),
        jnp.concatenate([partner, kept_half], axis=0),
    )
    return (layer, decoding_group_cache)


def solution(mesh):
    return jax.shard_map(
        on_device,
        mesh=mesh,
        in_specs=(
            P("req", None, None),
            P(),
            P(None, "tp"),
            P(),
            P("tp", None),
            P(),
            P(),
            P("req", None, None, None),
            P(),
            P(),
            P(),
        ),
        out_specs=(P("req", None, None), P("req", None, "tp", None)),
        check_vma=False,
    )
```

profile of v0, /device:TPU:0, one launch (start us, length us, event | category | flops | bytes accessed | tf_op | source)
XLA Modules:
  0.0 405.0 jit_solution(1439324511392412007)
XLA Ops:
  7.2 5.2 %copy.40 = bf16[1,5,2048,128]{3,1,0,2:T(8,128)(2,1)} copy(bf16[1,5,2048,128]{3,2,1,0:T(8,128)(2,1)} %param.20) | data formatting | bytes 5242880 | tf_op args[7]
  12.4 7.4 %all-to-all-start = ((bf16[1,5,2048,128]{3,1,0,2:T(8,128)(2,1)}), bf16[1,5,2048,128]{3,1,0,2:T(8,128)(2,1)}, u32[]{:S(2)}, u32[]{:S(2)}) async-start(bf16[1,5,2048,128]{3,1,0,2:T(8,128)(2,1)} %copy.40), calls=%async_computation | async-start | bytes 8388608 | tf_op jit(solution)/shard_map/all_to_all | solution.py:76
  19.9 93.2 %all-to-all-done = bf16[1,5,2048,128]{3,1,0,2:T(8,128)(2,1)} async-done(((bf16[1,5,2048,128]{3,1,0,2:T(8,128)(2,1)}), bf16[1,5,2048,128]{3,1,0,2:T(8,128)(2,1)}, u32[]{:S(2)}, u32[]{:S(2)}) %all-to-all-start) | async-done | bytes 2621472 | tf_op jit(solution)/shard_map/all_to_all | solution.py:76
  113.1 4.4 %copy.54 = bf16[1,5,8,256,128]{4,3,1,2,0:T(8,128)(2,1)} copy(bf16[1,5,8,256,128]{4,1,3,2,0:T(8,128)(2,1)} %bitcast.1) | data formatting | bytes 5242880 | tf_op jit(solution)/shard_map/all_to_all | solution.py:76
  117.6 5.3 %gather_fusion = bf16[16,5,256,128]{3,2,1,0:T(8,128)(2,1)} fusion(bf16[8,5,256,128]{3,2,1,0:T(8,128)(2,1)} %bitcast.95, s32[1024]{0:T(1024)S(1)} %pad_clamp_fusion.1), kind=kCustom, calls=%fused_computation.2 | custom fusion | bytes 10485824 | tf_op jit(solution)/shard_map/jit(_take)/gather | solution.py:79
  122.9 5.5 %select_select_fusion = bf16[16,5,256,128]{3,2,1,0:T(8,128)(2,1)} fusion(bf16[16,5,256,128]{3,2,1,0:T(8,128)(2,1)} %gather_fusion, pred[16]{0:T(512)(128)(4,1)S(1)} %get-tuple-element.41, pred[16]{0:T(512)(128)(4,1)S(1)} %get-tuple-element.65), kind=kLoop, calls=%fused_computation.27 | loop fusion | flops 5242880 | bytes 10485792 | tf_op jit(solution)/shard_map/jit(_where)/select_n | solution.py:81
  128.3 4.6 %all-to-all-start.1 = ((bf16[16,5,256,128]{3,2,1,0:T(8,128)(2,1)}), bf16[16,5,256,128]{3,2,1,0:T(8,128)(2,1)}, u32[]{:S(2)}, u32[]{:S(2)}) async-start(bf16[16,5,256,128]{3,2,1,0:T(8,128)(2,1)} %select_select_fusion), calls=%async_computation.1 | async-start | bytes 10485760 | tf_op jit(solution)/shard_map/all_to_all | solution.py:80
  133.2 4.6 %copy.44 = bf16[2048,640]{0,1:T(8,128)(2,1)} copy(bf16[2048,640]{1,0:T(8,128)(2,1)} %param.16) | data formatting | bytes 5242880 | tf_op args[3]
  138.3 3.4 fusion.45
  151.3 96.6 %all-to-all-done.1 = bf16[16,5,256,128]{3,2,1,0:T(8,128)(2,1)} async-done(((bf16[16,5,256,128]{3,2,1,0:T(8,128)(2,1)}), bf16[16,5,256,128]{3,2,1,0:T(8,128)(2,1)}, u32[]{:S(2)}, u32[]{:S(2)}) %all-to-all-start.1) | async-done | bytes 5242912 | tf_op jit(solution)/shard_map/all_to_all | solution.py:80
  252.0 4.1 %fusion.14 = (bf16[5,2304,128]{2,1,0:T(8,128)(2,1)}, bf16[5,2304,128]{2,1,0:T(8,128)(2,1)}) fusion(bf16[2,5,2048,128]{3,2,1,0:T(8,128)(2,1)S(1)} %bitcast_select_fusion, bf16[2,5,256,128]{3,2,1,0:T(8,128)(2,1)S(1)} %copy.45), kind=kLoop, calls=%fused_computation.33 | loop fusion | flops 11796480 | bytes 11796480 | tf_op jit(solution)/shard_map/squeeze | solution.py:120
  256.1 4.6 %gather_fusion.1 = bf16[5,2304,128]{2,1,0:T(8,128)(2,1)} fusion(bf16[5,2304,128]{2,1,0:T(8,128)(2,1)} %get-tuple-element.49, s32[1024]{0:T(1024)S(1)} %pad_clamp_fusion), kind=kCustom, calls=%fused_computation.clone | custom fusion | bytes 5898260 | tf_op jit(solution)/shard_map/jit(_take)/gather | solution.py:120
  260.7 5.4 %copy.46 = bf16[5,2304,128]{1,2,0:T(8,128)(2,1)} copy(bf16[5,2304,128]{2,1,0:T(8,128)(2,1)} %gather_fusion.1) | data formatting | bytes 5898240 | tf_op jit(solution)/shard_map/jit(_take)/gather | solution.py:120
  266.1 4.6 %gather_fusion.2 = bf16[5,2304,128]{2,1,0:T(8,128)(2,1)} fusion(bf16[5,2304,128]{2,1,0:T(8,128)(2,1)} %get-tuple-element.50, s32[1024]{0:T(1024)S(1)} %pad_clamp_fusion), kind=kCustom, calls=%fused_computation.1.clone | custom fusion | bytes 5898260 | tf_op jit(solution)/shard_map/jit(_take)/gather | solution.py:120
  270.8 5.4 %copy.47 = bf16[5,2304,128]{1,2,0:T(8,128)(2,1)} copy(bf16[5,2304,128]{2,1,0:T(8,128)(2,1)} %gather_fusion.2) | data formatting | bytes 5898240 | tf_op jit(solution)/shard_map/jit(_take)/gather | solution.py:120
  276.2 5.8 %broadcast_select_fusion.1 = (bf16[5,2304,128]{1,2,0:T(8,128)(2,1)}, bf16[5,2304,128]{1,2,0:T(8,128)(2,1)}) fusion(bf16[5,2304,128]{1,2,0:T(8,128)(2,1)} %copy.46, pred[5]{0:T(512)(128)(4,1)S(1)} %compare_and_fusion, bf16[5,2304,128]{1,2,0:T(8,128)(2,1)} %copy.47), kind=kLoop, calls=%fused_computation.37 | loop fusion | flops 2949120 | bytes 11796485 | tf_op jit(solution)/shard_map/jit(_take)/select_n | solution.py:120
  282.0 5.2 %fusion.90 = f32[5,256]{1,0:T(8,128)S(1)} fusion(pred[256,2304]{1,0:T(8,128)(4,1)S(1)} %get-tuple-element.58, bf16[5,2304,128]{1,2,0:T(8,128)(2,1)} %get-tuple-element.62, bf16[2,256,5,32]{1,3,2,0:T(8,128)(2,1)S(1)} %get-tuple-element.52, bf16[2,256,5,32]{1,3,2,0:T(8,128)(2,1)S(1)} %get-tuple-element.51), kind=kOutput, calls=%fused_computation.119 | convolution fusion | flops 389613824 | bytes 2397184 | tf_op jit(solution)/shard_map/sub | solution.py:44
  287.2 7.0 %fusion.37 = bf16[5,64,256]{2,1,0:T(8,128)(2,1)} fusion(f32[5,256]{1,0:T(8,128)S(1)} %fusion.90, bf16[5,2304,128]{1,2,0:T(8,128)(2,1)} %get-tuple-element.62, pred[256,2304]{1,0:T(8,128)(4,1)S(1)} %get-tuple-element.58, bf16[2,256,5,32]{1,3,2,0:T(8,128)(2,1)S(1)} %get-tuple-element.52, bf16[2,256,5,32]{1,3,2,0:T(8,128)(2,1)S(1)} %get-tuple-element.51), kind=kOutput, calls=%fused_computation.54 | convolution fusion | flops 770133504 | bytes 4035584 | tf_op jit(solution)/shard_map/hqk,hkd->qhd/dot_general | solution.py:46
  294.2 5.5 %fusion.95 = f32[5,256]{1,0:T(8,128)S(1)} fusion(pred[256,2304]{1,0:T(8,128)(4,1)S(1)} %get-tuple-element.57, bf16[5,2304,128]{1,2,0:T(8,128)(2,1)} %get-tuple-element.61, bf16[2,256,5,32]{1,3,2,0:T(8,128)(2,1)S(1)} %get-tuple-element.51, bf16[2,256,5,32]{1,3,2,0:T(8,128)(2,1)S(1)} %get-tuple-element.52), kind=kOutput, calls=%fused_computation.120 | convolution fusion | flops 389613824 | bytes 2397184 | tf_op jit(solution)/shard_map/sub | solution.py:44
  299.6 6.3 %fusion.40 = bf16[5,64,256]{2,1,0:T(8,128)(2,1)S(1)} fusion(f32[5,256]{1,0:T(8,128)S(1)} %fusion.95, bf16[5,2304,128]{1,2,0:T(8,128)(2,1)} %get-tuple-element.61, pred[256,2304]{1,0:T(8,128)(4,1)S(1)} %get-tuple-element.57, bf16[2,256,5,32]{1,3,2,0:T(8,128)(2,1)S(1)} %get-tuple-element.51, bf16[2,256,5,32]{1,3,2,0:T(8,128)(2,1)S(1)} %get-tuple-element.52), kind=kOutput, calls=%fused_computation.55 | convolution fusion | flops 770133504 | bytes 4035584 | tf_op jit(solution)/shard_map/hqk,hkd->qhd/dot_general | solution.py:46
  306.0 3.3 fusion.47
  310.1 5.6 %concatenate.30 = bf16[2,5,2304,128]{3,2,1,0:T(8,128)(2,1)} pad(bf16[2,5,2048,128]{3,2,1,0:T(8,128)(2,1)} %copy-done.1, bf16[]{:T(256)} %constant.52.clone.1), padding=0_0x0_0x0_256x0_0 | pad | bytes 11141122 | tf_op jit(solution)/shard_map/concatenate | solution.py:132
  315.7 24.9 %while.1 = (s32[]{:T(128)}, bf16[2,5,2304,128]{3,2,1,0:T(8,128)(2,1)}, s32[2,4]{1,0:T(2,128)S(1)}, bf16[2,5,256,128]{3,2,1,0:T(8,128)(2,1)S(1)}, s32[]{:T(128)}, /*index=5*/s32[4]{0:T(128)S(1)}, s32[]{:T(128)}) while((s32[]{:T(128)}, bf16[2,5,2304,128]{3,2,1,0:T(8,128)(2,1)}, s32[2,4]{1,0:T(2,128)S(1)}, bf16[2,5,256,128]{3,2,1,0:T(8,128)(2,1)S(1)}, ...), condition=%wide.while_cond, body=%wide.while_body.sunk | while | flops 163869 | bytes 1638603 | solution.py:137
  316.3 3.2 and_reduce_fusion.2
  322.5 5.6 %dynamic-update-slice.3 = bf16[2,5,2304,128]{3,2,1,0:T(8,128)(2,1)} dynamic-update-slice(bf16[2,5,2304,128]{3,2,1,0:T(8,128)(2,1)} %get-tuple-element.113, bf16[1,5,256,128]{3,2,1,0:T(8,128)(2,1)S(1)} %dynamic-slice_select_fusion.2, s32[]{:T(128)} %bitcast.89, s32[]{:T(128)} %constant.38.clone.1..sunk, s32[]{:T(128)} %bitcast.90, s32[]{:T(128)} %constant.38.clone.1..sunk) | dynamic-update-slice | bytes 655364 | tf_op jit(solution)/shard_map/vmap(vmap())/scatter
  328.7 3.2 and_reduce_fusion.2
  332.0 3.0 dynamic-slice_select_fusion.2
  335.0 5.6 %dynamic-update-slice.3 = bf16[2,5,2304,128]{3,2,1,0:T(8,128)(2,1)} dynamic-update-slice(bf16[2,5,2304,128]{3,2,1,0:T(8,128)(2,1)} %get-tuple-element.113, bf16[1,5,256,128]{3,2,1,0:T(8,128)(2,1)S(1)} %dynamic-slice_select_fusion.2, s32[]{:T(128)} %bitcast.89, s32[]{:T(128)} %constant.38.clone.1..sunk, s32[]{:T(128)} %bitcast.90, s32[]{:T(128)} %constant.38.clone.1..sunk) | dynamic-update-slice | bytes 655364 | tf_op jit(solution)/shard_map/vmap(vmap())/scatter
  344.9 15.9 %collective-permute-done = bf16[2,5,288,128]{3,2,1,0:T(8,128)(2,1)} collective-permute-done((bf16[2,5,288,128]{3,2,1,0:T(8,128)(2,1)}, bf16[2,5,288,128]{3,2,1,0:T(8,128)(2,1)}, u32[]{:S(2)}, u32[]{:S(2)}) %collective-permute-start) | collective-permute-done | bytes 737312 | tf_op jit(solution)/shard_map/ppermute | solution.py:12
  360.8 3.2 maximum_select_fusion
  364.0 30.0 %all-reduce.3.cloned.1.call-done = f32[512,2048]{1,0:T(8,128)} async-done(((f32[512,2048]{1,0:T(8,128)}), f32[512,2048]{1,0:T(8,128)}) %all-reduce.3.cloned.1.call-update) | async-done | bytes 4194320 | tf_op jit(solution)/shard_map/psum | solution.py:129
  394.0 4.2 %fusion.12 = bf16[512,2048]{1,0:T(8,128)(2,1)} fusion(f32[512,2048]{1,0:T(8,128)} %all-reduce.3.cloned.1.call-done, bf16[2,256,2048]{2,1,0:T(8,128)(2,1)S(1)} %copy-done.3), kind=kLoop, calls=%fused_computation.29 | loop fusion | flops 3145728 | bytes 8388608 | tf_op jit(solution)/shard_map/convert_element_type | solution.py:130
  (74 shorter events, 23.7 us)
Async XLA Ops:
  7.2 298.8 %copy-start = (bf16[320,2048]{1,0:T(8,128)(2,1)S(1)}, bf16[320,2048]{1,0:T(8,128)(2,1)}, u32[]{:S(2)}) copy-start(bf16[320,2048]{1,0:T(8,128)(2,1)} %param.17) | copy-start | bytes 3932164
  12.4 7.4 %copy-start.9 = (s32[16]{0:T(128)S(1)}, s32[16]{0:T(128)}, u32[]{:S(2)}) copy-start(s32[16]{0:T(128)} %param.21) | copy-start | bytes 196
  12.4 7.4 %copy-start.12 = (s32[16]{0:T(128)S(1)}, s32[16]{0:T(128)}, u32[]{:S(2)}) copy-start(s32[16]{0:T(128)} %param.22) | copy-start | bytes 196
  12.4 100.7 %all-to-all-start = ((bf16[1,5,2048,128]{3,1,0,2:T(8,128)(2,1)}), bf16[1,5,2048,128]{3,1,0,2:T(8,128)(2,1)}, u32[]{:S(2)}, u32[]{:S(2)}) async-start(bf16[1,5,2048,128]{3,1,0,2:T(8,128)(2,1)} %copy.40), calls=%async_computation | async-start | bytes 8388608 | tf_op jit(solution)/shard_map/all_to_all | solution.py:76
  128.3 119.6 %all-to-all-start.1 = ((bf16[16,5,256,128]{3,2,1,0:T(8,128)(2,1)}), bf16[16,5,256,128]{3,2,1,0:T(8,128)(2,1)}, u32[]{:S(2)}, u32[]{:S(2)}) async-start(bf16[16,5,256,128]{3,2,1,0:T(8,128)(2,1)} %select_select_fusion), calls=%async_computation.1 | async-start | bytes 10485760 | tf_op jit(solution)/shard_map/all_to_all | solution.py:80
  133.0 4.8 %copy-start.2 = (bf16[2,256,2048]{2,1,0:T(8,128)(2,1)S(1)}, bf16[2,256,2048]{2,1,0:T(8,128)(2,1)}, u32[]{:S(2)}) copy-start(bf16[2,256,2048]{2,1,0:T(8,128)(2,1)} %param.13) | copy-start | bytes 6291460
  133.0 261.0 %all-reduce.3.cloned.1.call-start = ((), (), s32[]{:S(2)}) async-start(), calls=%async_computation.2 | async-start | bytes 8388608 | tf_op jit(solution)/shard_map/psum | solution.py:129
  133.2 5.1 %copy-start.15 = (f32[2048]{0:T(1024)S(1)}, f32[2048]{0:T(1024)}, u32[]{:S(2)}) copy-start(f32[2048]{0:T(1024)} %param.14) | copy-start | bytes 24580
  138.3 5.2 %copy-start.13 = (s32[16]{0:T(128)S(1)}, s32[16]{0:T(128)}, u32[]{:S(2)}) copy-start(s32[16]{0:T(128)} %param.23) | copy-start | bytes 196
  141.7 1.1 copy-start.4
  144.9 2.8 copy-start.5
  144.9 2.8 copy-start.10
  144.9 2.8 copy-start.11
  147.3 1.0 copy-start.6
  252.0 4.1 %copy-start.1 = (bf16[2,5,2048,128]{3,2,1,0:T(8,128)(2,1)}, bf16[2,5,2048,128]{3,2,1,0:T(8,128)(2,1)S(1)}, u32[]{:S(2)}) copy-start(bf16[2,5,2048,128]{3,2,1,0:T(8,128)(2,1)S(1)} %bitcast_select_fusion) | copy-start | bytes 15728644
  299.6 6.4 %copy-start.7 = (bf16[5,64,256]{2,1,0:T(8,128)(2,1)S(1)}, bf16[5,64,256]{2,1,0:T(8,128)(2,1)}, u32[]{:S(2)}) copy-start(bf16[5,64,256]{2,1,0:T(8,128)(2,1)} %fusion.37) | copy-start | bytes 491524
  309.3 0.7 copy-start.14
  310.1 5.6 %copy-start.8 = (s32[4]{0:T(128)S(1)}, s32[4]{0:T(128)}, u32[]{:S(2)}) copy-start(s32[4]{0:T(128)} %constant.238) | copy-start | bytes 52
  340.5 53.4 %copy-start.3 = (bf16[2,256,2048]{2,1,0:T(8,128)(2,1)S(1)}, bf16[2,256,2048]{2,1,0:T(8,128)(2,1)}, u32[]{:S(2)}) copy-start(bf16[2,256,2048]{2,1,0:T(8,128)(2,1)} %param.13) | copy-start | bytes 6291460
  343.2 17.6 %collective-permute-start = (bf16[2,5,288,128]{3,2,1,0:T(8,128)(2,1)}, bf16[2,5,288,128]{3,2,1,0:T(8,128)(2,1)}, u32[]{:S(2)}, u32[]{:S(2)}) collective-permute-start(bf16[2,5,288,128]{3,2,1,0:T(8,128)(2,1)} %get-tuple-element.48), channel_id=1, source_target_pairs={{0,4},{4,0},{8,12},{12,8},{16,20},{20,16},{24,28},{28,24},{1,5},{5... | collective-permute-start | bytes 2211848 | tf_op jit(solution)/shard_map/ppermute | solution.py:12
Sparse Core Ops, SparseCore 0:
  309.4 84.5 all-reduce.2
where the time goes:
time: 407 us; the launch traced here: 405 us
  waiting for transfers between devices  236 us (58%)
  local copies, waits for them, and re-layouts  66.8 us (16%)
  other arithmetic  41.1 us (10%)
  matrix products  33 us (8%)
  between operations  14.3 us (4%)
  starting transfers between devices  13.9 us (3%)
    all_to_all x1, waiting for transfers between devices, on_device(): lax.all_to_all(jnp.where(live_all[:, None, None, None], select_chosen, jn...  96.6 us
    all_to_all x1, waiting for transfers between devices, on_device(): lax.all_to_all(stored, 'req', split_axis=2, concat_axis=0, tiled=True)  93.2 us
    psum x1, waiting for transfers between devices, on_device(): lax.psum(jnp.dot(mixed_all, w_out, preferred_element_type=jnp.float32), '...  30 us
    gather x4, local copies, waits for them, and re-layouts, on_device(): chosen = jnp.take(keys_all[number], head_select, axis=0)  20.1 us
    ppermute x1, waiting for transfers between devices, swapped(): return lax.ppermute(value, axis, pairs)  15.9 us
    dot_general x2, matrix products, attend(): jnp.einsum('hqk,hkd->qhd', probs, keys_one[..., head_dim:], preferred_ele...  13.3 us
    scatter x6, local copies, waits for them, and re-layouts  12.4 us
    scatter x4, other arithmetic  12.4 us
  transfers between devices with their start and end apart: 4, of which 4 were waited for; matrix products, arithmetic and copies ran while one was open for 13% of the time, Pallas kernels for 0%

commit v1 on v0

v1 whole, which is shorter than its diff:
```python
import functools
import math

import jax
import jax.numpy as jnp
import numpy as np
from jax import lax
from jax.experimental import pallas as pl
from jax.experimental.pallas import tpu as pltpu
from jax.sharding import PartitionSpec as P

BF16 = jnp.bfloat16
F32 = jnp.float32
LANES = 128
EPS = 1e-06
NEG = -1e30
SMEM = pl.BlockSpec(memory_space=pltpu.SMEM)


def cost(flops, moved):
    return pl.CostEstimate(flops=int(flops), bytes_accessed=int(moved), transcendentals=0)


def params(mib=48):
    return pltpu.CompilerParams(vmem_limit_bytes=mib << 20)


def lane_iota(rows):
    return lax.broadcasted_iota(jnp.int32, (rows, LANES), 1)


def angle_tables(head_dim, new_count, cache_span):
    half = head_dim // 2
    freq = np.exp(-math.log(10000.0) * np.arange(half, dtype=np.float64) * 2.0 / head_dim)
    freq = np.tile(freq.astype(np.float32).astype(np.float64), LANES // half)

    def pair(positions):
        angle = positions[:, None].astype(np.float64) * freq[None, :]
        return np.cos(angle).astype(np.float32), np.sin(angle).astype(np.float32)

    fine = pair(np.arange(new_count))
    coarse = pair(np.arange(cache_span // 16 + 8) * 16)
    small = pair(np.arange(16))
    return fine + coarse + small


def rotation(length, tables):
    cos_i, sin_i, cos_hi, sin_hi, cos_lo, sin_lo = tables
    high = length // 16
    low = length - high * 16
    ch, sh = cos_hi[pl.ds(high, 1), :], sin_hi[pl.ds(high, 1), :]
    cl, sl = cos_lo[pl.ds(low, 1), :], sin_lo[pl.ds(low, 1), :]
    cb, sb = ch * cl - sh * sl, sh * cl + ch * sl
    ci, si = cos_i[...], sin_i[...]
    cosine = ci * cb - si * sb
    sine = si * cb + ci * sb
    lanes = lane_iota(ci.shape[0])
    return cosine, jnp.where(lanes % 64 < 32, -sine, sine)


def norm_rope(tile, gain, cosine, sine, blocks):
    square = tile * tile
    high = square.astype(BF16)
    low = (square - high.astype(F32)).astype(BF16)
    mean = jnp.dot(high, blocks, preferred_element_type=F32) + jnp.dot(
        low, blocks, preferred_element_type=F32
    )
    unit = tile * lax.rsqrt(mean + EPS) * gain
    lanes = lane_iota(tile.shape[0])
    other = jnp.where(lanes % 64 < 32, pltpu.roll(unit, 96, 1), pltpu.roll(unit, 32, 1))
    return unit * cosine + other * sine


def half_blocks():
    rows = lax.broadcasted_iota(jnp.int32, (LANES, LANES), 0)
    cols = lax.broadcasted_iota(jnp.int32, (LANES, LANES), 1)
    return jnp.where(rows // 64 == cols // 64, 1.0 / 64.0, 0.0).astype(BF16)


def live_length(cont, clen, request):
    return jnp.where(cont[request] == 1, clen[request], 0)


def to_chunks(ref, lead, value, chunk):
    rows = value.shape[0]
    for start in range(0, rows, chunk):
        size = min(chunk, rows - start)
        ref[(start // chunk,) + lead + (pl.ds(0, size),)] = value[start : start + size]


def query_kernel(req_dev, chunk, cont, clen, tok, gain, w, qg, ci, si, ch, sh, cl, sl, normed, q):
    b = pl.program_id(0)
    length = live_length(cont, clen, lax.axis_index("req") * req_dev + b)
    x = tok[0].astype(F32)
    mean = jnp.mean(x * x, axis=-1, keepdims=True)
    h = (x * lax.rsqrt(mean + EPS) * gain[...]).astype(BF16)
    normed[0] = h
    cosine, sine = rotation(length, (ci, si, ch, sh, cl, sl))
    out = jnp.dot(h, w[...], preferred_element_type=F32)
    blocks = half_blocks()
    count = h.shape[0]
    half = count // 2
    pair01 = norm_rope(out[:, :128], qg[...], cosine, sine, blocks)
    pair23 = norm_rope(out[:, 128:256], qg[...], cosine, sine, blocks)
    last = out[:, 256:320]
    last = jnp.concatenate([last[:half], last[half:]], axis=1)
    lanes = lane_iota(half)
    pick = lambda v: jnp.where(lanes < 64, v[:half], v[half:])
    last = norm_rope(last, qg[...], pick(cosine), pick(sine), blocks)
    packed = (jnp.concatenate([pair01, pair23, last], axis=0) * 0.125).astype(BF16)
    to_chunks(q, (0,), packed, chunk)


def fresh_kernel(req_dev, cont, clen, normed, w, kg, ci, si, ch, sh, cl, sl, fresh):
    b = pl.program_id(0)
    length = live_length(cont, clen, lax.axis_index("req") * req_dev + b)
    cosine, sine = rotation(length, (ci, si, ch, sh, cl, sl))
    out = jnp.dot(normed[0], w[...], preferred_element_type=F32)
    blocks = half_blocks()
    lanes = lane_iota(out.shape[0])
    for head in range(fresh.shape[1]):
        tile = out[:, head * 128 : head * 128 + 128]
        keys = norm_rope(tile, kg[...], cosine, sine, blocks)
        fresh[0, head] = jnp.where(lanes < 64, keys, tile).astype(BF16)


def split_heads(packed, count):
    half = count // 2
    wide = packed.astype(F32)
    lanes = lane_iota(count)
    tiles = [wide[:count], pltpu.roll(wide[:count], 64, 1)]
    tiles += [wide[count : 2 * count], pltpu.roll(wide[count : 2 * count], 64, 1)]
    last = wide[2 * count : 2 * count + half]
    tiles.append(jnp.concatenate([last, pltpu.roll(last, 64, 1)], axis=0))
    extra = jnp.where(lanes == 64, 1.0, 0.0)
    return [jnp.where(lanes < 64, tile, extra).astype(BF16) for tile in tiles]


def soft(scores, values):
    top = jnp.max(scores, axis=-1, keepdims=True)
    weights = jnp.exp(scores - top).astype(BF16)
    out = jnp.dot(weights, values, preferred_element_type=F32)
    total = out[:, 0:1]
    return out / pltpu.roll(out, 64, 1), top + jnp.log(total)


def local_kernel(groups, q, fresh, out, lse):
    heads = 5
    count = fresh.shape[2]
    first = lax.axis_index("tp") * heads
    lanes = lane_iota(count)
    rows = lax.broadcasted_iota(jnp.int32, (count, count), 0)
    cols = lax.broadcasted_iota(jnp.int32, (count, count), 1)
    packed = q[...].reshape(-1, LANES)
    tiles = split_heads(packed, count)
    stats = jnp.zeros((count, LANES), F32)
    kept = []
    for head in range(heads):
        kv = fresh[0, (first + head) // groups].astype(F32)
        keys = jnp.where(lanes < 64, kv, 0.0).astype(BF16)
        values = jnp.where(lanes < 64, 1.0, kv).astype(BF16)
        scores = lax.dot_general(
            tiles[head], keys, (((1,), (1,)), ((), ())), preferred_element_type=F32
        )
        scores = jnp.where(cols <= rows, scores, NEG)
        mixed, level = soft(scores, values)
        stats = jnp.where(lanes == head, level, stats)
        kept.append(mixed)
    roll = lambda v: pltpu.roll(v, 64, 1)
    out[0, 0] = jnp.where(lanes < 64, roll(kept[0]), kept[1])
    out[0, 1] = jnp.where(lanes < 64, roll(kept[2]), kept[3])
    out[0, 2] = jnp.where(lanes < 64, roll(kept[4]), 0.0)
    lse[0] = stats


def route_kernel(by_row, requests, cont, crow, src, dst):
    def step(r, carry):
        if by_row:

            @pl.when(cont[r] == 1)
            def _():
                dst[crow[r]] = src[r]

        else:
            dst[r] = src[jnp.where(cont[r] == 1, crow[r], 0)]
        return carry

    lax.fori_loop(0, requests, step, 0)


def row_kernel(requests, chunk, cont, crow, clen, q, kv_ref, out, q_sc, o_sc, s_sc):
    head = pl.program_id(0)
    count = q_sc.shape[1]
    heads = q_sc.shape[0]
    row = lax.axis_index("req")

    def find(r, length):
        mine = jnp.logical_and(cont[r] == 1, crow[r] == row)
        return jnp.where(mine, clen[r], length)

    length = lax.fori_loop(0, requests, find, 0)

    @pl.when(head == 0)
    def _():
        packed = q[...].reshape(-1, LANES)
        for number, tile in enumerate(split_heads(packed, count)):
            q_sc[number] = tile
        s_sc[...] = jnp.zeros_like(s_sc)

    span = kv_ref.shape[2]
    kv = kv_ref[0, 0].astype(F32)
    lanes = lane_iota(span)
    position = lax.broadcasted_iota(jnp.int32, (span, LANES), 0)
    bias = jnp.where(jnp.logical_and(lanes == 64, position >= length), NEG, 0.0)
    keys = jnp.where(lanes < 64, kv, bias).astype(BF16)
    values = jnp.where(lanes < 64, 1.0, kv).astype(BF16)
    scores = lax.dot_general(
        q_sc[head], keys, (((1,), (1,)), ((), ())), preferred_element_type=F32
    )
    mixed, level = soft(scores, values)
    o_sc[head] = mixed
    s_sc[...] = jnp.where(lane_iota(count) == head, level, s_sc[...])

    @pl.when(head == heads - 1)
    def _():
        lanes = lane_iota(count)
        roll = lambda v, n: pltpu.roll(v, n, 1)
        level = s_sc[...]
        high = level.astype(BF16).astype(F32)
        mid = (level - high).astype(BF16).astype(F32)
        low = (level - high - mid).astype(BF16).astype(F32)
        stats = roll(high, 64) + roll(mid, 64 + heads) + roll(low, 64 + 2 * heads)
        tiles = [
            jnp.where(lanes < 64, roll(o_sc[0], 64), o_sc[1]),
            jnp.where(lanes < 64, roll(o_sc[2], 64), o_sc[3]),
            jnp.where(lanes < 64, roll(o_sc[4], 64), stats),
        ]
        to_chunks(out, (), jnp.concatenate(tiles, axis=0).astype(BF16), chunk)


def merge_kernel(req_dev, cont, far, near, lse, mixed):
    heads = 5
    count = near.shape[2]
    b = pl.program_id(0)
    request = lax.axis_index("req") * req_dev + b
    live = cont[request] == 1
    lanes = lane_iota(count)
    roll = lambda v, n: pltpu.roll(v, n, 1)
    packed = far[...].reshape(-1, LANES)
    tiles = [packed[p * count : (p + 1) * count].astype(F32) for p in range(3)]
    stats = roll(tiles[2], 64) + roll(tiles[2], 64 - heads) + roll(tiles[2], 64 - 2 * heads)
    far_level = jnp.where(jnp.logical_and(live, lanes < heads), stats, NEG)
    near_level = lse[0]
    top = jnp.maximum(far_level, near_level)
    far_part = jnp.exp(far_level - top)
    near_part = jnp.exp(near_level - top)
    share = far_part / (far_part + near_part)
    done = []
    for p in range(3):
        left = share[:, 2 * p : 2 * p + 1]
        right = share[:, 2 * p + 1 : 2 * p + 2] if 2 * p + 1 < heads else left
        weight = jnp.where(lanes < 64, left, right)
        done.append(weight * tiles[p] + (1.0 - weight) * near[0, p])
    half = count // 2
    last = jnp.where(lane_iota(half) < 64, done[2][:half], roll(done[2][half:], 64))
    mixed[0] = jnp.concatenate([done[0], done[1], last], axis=0).astype(BF16)


def project_kernel(m0, m1, m2, m3, w0, w1, w2, w3, tok, out, lhs):
    req_dev, count, block = out.shape
    half = count // 2

    @pl.when(pl.program_id(0) == 0)
    def _():
        lanes = lane_iota(half)
        sources = (m0, m1, m2, m3)
        for b in range(req_dev):
            base = b * count
            for number, m in enumerate(sources):
                for p in range(2):
                    col = number * 256 + p * 128
                    lhs[base : base + count, col : col + 128] = m[b, p * count : (p + 1) * count]
            for pair in range(2):
                left = sources[2 * pair][b, 2 * count :].astype(F32)
                right = sources[2 * pair + 1][b, 2 * count :].astype(F32)
                above = jnp.where(lanes < 64, left, pltpu.roll(right, 64, 1))
                below = jnp.where(lanes < 64, pltpu.roll(left, 64, 1), right)
                col = 1024 + pair * 128
                lhs[base : base + half, col : col + 128] = above.astype(BF16)
                lhs[base + half : base + count, col : col + 128] = below.astype(BF16)

    total = tok[...].reshape(req_dev * count, block).astype(F32)
    ws = (w0, w1, w2, w3)
    for number, w in enumerate(ws):
        total += jnp.dot(
            lhs[:, number * 256 : number * 256 + 256], w[:256], preferred_element_type=F32
        )
    rest = jnp.concatenate([w[256:] for w in ws], axis=0)
    total += jnp.dot(lhs[:, 1024:], rest, preferred_element_type=F32)
    out[...] = total.astype(BF16).reshape(req_dev, count, block)


def segment_kernel(segments, stored, own, other, sem):
    place, tp_place = lax.axis_index("req"), lax.axis_index("tp")
    per_side = segments // 2
    mine = (place % 2) * per_side + tp_place
    theirs = (1 - place % 2) * per_side + tp_place
    segment = own.shape[1]
    span = stored.shape[2]
    for which, dst in ((mine, own), (theirs, other)):
        for number in range(segments):
            size = min(segment, span - number * segment)
            if size <= 0:
                continue

            @pl.when(which == number)
            def _():
                copy = pltpu.make_async_copy(
                    stored.at[0, :, pl.ds(number * segment, size), :],
                    dst.at[:, pl.ds(0, size), :],
                    sem,
                )
                copy.start()
                copy.wait()


def cache_kernel(req_dev, cont, crow, clen, rows, mine, theirs, out, wide, cached, sem):
    l = pl.program_id(0)
    place, tp_place = lax.axis_index("req"), lax.axis_index("tp")
    side = place % 2
    kv_heads, segment = out.shape[1], out.shape[2]
    count = mine.shape[2]
    tp_count = lax.axis_size("tp")
    request = (place // 2) * 2 * req_dev + l
    length = live_length(cont, clen, request)
    row = jnp.where(cont[request] == 1, crow[request], 0)
    copy = pltpu.make_async_copy(rows.at[row // 2, (row % 2) ^ side], cached, sem)
    copy.start()
    start = (side * tp_count + tp_place) * segment
    shift = jnp.clip(start - length, -segment, count) + segment
    position = start + lax.broadcasted_iota(jnp.int32, (segment, LANES), 0)
    old = position < length
    new = jnp.logical_and(position >= length, position < length + count)
    local = l // req_dev == side
    copy.wait()
    for head in range(kv_heads):

        @pl.when(local)
        def _():
            wide[segment : segment + count] = mine[0, head].astype(F32)

        @pl.when(jnp.logical_not(local))
        def _():
            wide[segment : segment + count] = theirs[0, head].astype(F32)

        moved = wide[pl.ds(shift, segment), :]
        kept = cached[head].astype(F32)
        out[0, head] = jnp.where(old, kept, jnp.where(new, moved, 0.0)).astype(BF16)


def permuted(value, axis, mask):
    pairs = [(source, source ^ mask) for source in range(lax.axis_size(axis))]
    return lax.ppermute(value, axis, pairs)


def exchanged(value):
    return lax.all_to_all(value, "req", split_axis=0, concat_axis=0, tiled=True)


def full(shape):
    return pl.BlockSpec(shape, lambda *_: (0,) * len(shape))


def on_device(
    tokens,
    attn_gain,
    w_query,
    key_value_weight,
    w_out,
    q_gain,
    k_gain,
    stored,
    continuing,
    cache_row,
    cache_len,
):
    n_req = lax.axis_size("req")
    tp_count = lax.axis_size("tp")
    req_dev, count, width = tokens.shape
    head_dim = q_gain.shape[0]
    kv_heads = key_value_weight.shape[1] // (2 * head_dim)
    heads = w_query.shape[1] // head_dim
    groups = heads * tp_count // kv_heads
    span = stored.shape[2]
    requests = continuing.shape[0]
    segments = 2 * tp_count
    segment = (span + count) // segments
    q_rows = heads * head_dim * count // LANES
    o_rows = -(-heads * head_dim // LANES) * count
    q_chunk = -(-q_rows // (16 * n_req)) * 16
    o_chunk = -(-o_rows // (16 * n_req)) * 16

    tables = tuple(jnp.asarray(t) for t in angle_tables(head_dim, count, span))
    table_specs = [full(t.shape) for t in tables]
    gain_row = attn_gain.reshape(1, width)
    q_gain_row = jnp.tile(q_gain.reshape(1, head_dim), (1, LANES // head_dim))
    k_gain_row = jnp.tile(k_gain.reshape(1, head_dim), (1, LANES // head_dim))
    any_spec = pl.BlockSpec(memory_space=pl.ANY)

    own_part, other_part = pl.pallas_call(
        functools.partial(segment_kernel, segments),
        out_shape=(jax.ShapeDtypeStruct((kv_heads, segment, LANES), BF16),) * 2,
        in_specs=[any_spec],
        out_specs=(any_spec, any_spec),
        scratch_shapes=[pltpu.SemaphoreType.DMA],
        compiler_params=params(),
        cost_estimate=cost(0, 4 * kv_heads * segment * LANES * 2),
        name="segments",
    )(stored)
    partner_part = permuted(other_part, "req", 1)
    both = jnp.stack([own_part, partner_part])
    column = [list(range(side, n_req, 2)) for side in range(2)]
    rows = lax.all_gather(both, "req", axis_index_groups=column)

    w_x = permuted(w_out, "tp", tp_count // 2)
    w_c = permuted(w_out, "tp", 1)
    w_xc = permuted(w_x, "tp", 1)

    normed, q = pl.pallas_call(
        functools.partial(query_kernel, req_dev, q_chunk),
        grid=(req_dev,),
        out_shape=(
            jax.ShapeDtypeStruct(tokens.shape, BF16),
            jax.ShapeDtypeStruct((n_req, req_dev, q_chunk, LANES), BF16),
        ),
        in_specs=[
            SMEM,
            SMEM,
            pl.BlockSpec((1, count, width), lambda b: (b, 0, 0)),
            full((1, width)),
            full(w_query.shape),
            full((1, LANES)),
        ]
        + table_specs,
        out_specs=(
            pl.BlockSpec((1, count, width), lambda b: (b, 0, 0)),
            pl.BlockSpec((n_req, 1, q_chunk, LANES), lambda b: (0, b, 0, 0)),
        ),
        compiler_params=params(),
        cost_estimate=cost(2 * req_dev * count * width * 384, 6 << 20),
        name="query",
    )(continuing, cache_len, tokens, gain_row, w_query, q_gain_row, *tables)

    q_mid = exchanged(q).reshape(requests, q_chunk, LANES)

    fresh = pl.pallas_call(
        functools.partial(fresh_kernel, req_dev),
        grid=(req_dev,),
        out_shape=jax.ShapeDtypeStruct((req_dev, kv_heads, count, LANES), BF16),
        in_specs=[
            SMEM,
            SMEM,
            pl.BlockSpec((1, count, width), lambda b: (b, 0, 0)),
            full(key_value_weight.shape),
            full((1, LANES)),
        ]
        + table_specs,
        out_specs=pl.BlockSpec((1, kv_heads, count, LANES), lambda b: (b, 0, 0, 0)),
        compiler_params=params(),
        cost_estimate=cost(2 * req_dev * count * width * 640, 6 << 20),
        name="fresh",
    )(continuing, cache_len, normed, key_value_weight, k_gain_row, *tables)
    fresh_partner = permuted(fresh, "req", 1)

    near, near_lse = pl.pallas_call(
        functools.partial(local_kernel, groups),
        grid=(req_dev,),
        out_shape=(
            jax.ShapeDtypeStruct((req_dev, 3, count, LANES), F32),
            jax.ShapeDtypeStruct((req_dev, count, LANES), F32),
        ),
        in_specs=[
            pl.BlockSpec((n_req, 1, q_chunk, LANES), lambda b: (0, b, 0, 0)),
            pl.BlockSpec((1, kv_heads, count, LANES), lambda b: (b, 0, 0, 0)),
        ],
        out_specs=(
            pl.BlockSpec((1, 3, count, LANES), lambda b: (b, 0, 0, 0)),
            pl.BlockSpec((1, count, LANES), lambda b: (b, 0, 0)),
        ),
        compiler_params=params(),
        cost_estimate=cost(4 * req_dev * heads * count * count * 256, 4 << 20),
        name="attend_new",
    )(q, fresh)

    q_out = pl.pallas_call(
        functools.partial(route_kernel, True, requests),
        out_shape=jax.ShapeDtypeStruct((n_req, q_chunk, LANES), BF16),
        in_specs=[SMEM, SMEM, pl.BlockSpec(memory_space=pltpu.VMEM)],
        out_specs=pl.BlockSpec(memory_space=pltpu.VMEM),
        compiler_params=params(),
        cost_estimate=cost(0, 1 << 20),
        name="route_query",
    )(continuing, cache_row, q_mid)
    q_row = exchanged(q_out)

    def kv_index(h):
        return (0, (lax.axis_index("tp") * heads + h) // groups, 0, 0)

    far = pl.pallas_call(
        functools.partial(row_kernel, requests, o_chunk),
        grid=(heads,),
        out_shape=jax.ShapeDtypeStruct((n_req, o_chunk, LANES), BF16),
        in_specs=[
            SMEM,
            SMEM,
            SMEM,
            full((n_req, q_chunk, LANES)),
            pl.BlockSpec((1, 1, span, LANES), kv_index),
        ],
        out_specs=full((n_req, o_chunk, LANES)),
        scratch_shapes=[
            pltpu.VMEM((heads, count, LANES), BF16),
            pltpu.VMEM((heads, count, LANES), F32),
            pltpu.VMEM((count, LANES), F32),
        ],
        compiler_params=params(),
        cost_estimate=cost(4 * heads * count * span * 256, 2 << 20),
        name="attend_row",
    )(continuing, cache_row, cache_len, q_row, stored)

    far_mid = exchanged(far)
    far_out = pl.pallas_call(
        functools.partial(route_kernel, False, requests),
        out_shape=jax.ShapeDtypeStruct((requests, o_chunk, LANES), BF16),
        in_specs=[SMEM, SMEM, pl.BlockSpec(memory_space=pltpu.VMEM)],
        out_specs=pl.BlockSpec(memory_space=pltpu.VMEM),
        compiler_params=params(),
        cost_estimate=cost(0, 1 << 20),
        name="route_result",
    )(continuing, cache_row, far_mid)
    far_home = exchanged(far_out.reshape(n_req, req_dev, o_chunk, LANES))

    mixed = pl.pallas_call(
        functools.partial(merge_kernel, req_dev),
        grid=(req_dev,),
        out_shape=jax.ShapeDtypeStruct((req_dev, q_rows, LANES), BF16),
        in_specs=[
            SMEM,
            pl.BlockSpec((n_req, 1, o_chunk, LANES), lambda b: (0, b, 0, 0)),
            pl.BlockSpec((1, 3, count, LANES), lambda b: (b, 0, 0, 0)),
            pl.BlockSpec((1, count, LANES), lambda b: (b, 0, 0)),
        ],
        out_specs=pl.BlockSpec((1, q_rows, LANES), lambda b: (b, 0, 0)),
        compiler_params=params(),
        cost_estimate=cost(0, 3 << 20),
        name="merge",
    )(continuing, far_home, near, near_lse)

    m_x = permuted(mixed, "tp", tp_count // 2)
    m_c = permuted(mixed, "tp", 1)
    m_xc = permuted(m_x, "tp", 1)

    block = 512
    m_spec = full((req_dev, q_rows, LANES))
    w_spec = pl.BlockSpec((heads * head_dim, block), lambda n: (0, n))
    t_spec = pl.BlockSpec((req_dev, count, block), lambda n: (0, 0, n))
    layer = pl.pallas_call(
        project_kernel,
        grid=(width // block,),
        out_shape=jax.ShapeDtypeStruct(tokens.shape, BF16),
        in_specs=[m_spec] * 4 + [w_spec] * 4 + [t_spec],
        out_specs=t_spec,
        scratch_shapes=[pltpu.VMEM((req_dev * count, 1280), BF16)],
        compiler_params=params(),
        cost_estimate=cost(2 * req_dev * count * width * 1280, 10 << 20),
        name="project",
    )(mixed, m_x, m_c, m_xc, w_out, w_x, w_c, w_xc, tokens)

    new_spec = pl.BlockSpec((1, kv_heads, count, LANES), lambda l: (l % req_dev, 0, 0, 0))
    cache = pl.pallas_call(
        functools.partial(cache_kernel, req_dev),
        grid=(2 * req_dev,),
        out_shape=jax.ShapeDtypeStruct((2 * req_dev, kv_heads, segment, LANES), BF16),
        in_specs=[SMEM, SMEM, SMEM, any_spec, new_spec, new_spec],
        out_specs=pl.BlockSpec((1, kv_heads, segment, LANES), lambda l: (l, 0, 0, 0)),
        scratch_shapes=[
            pltpu.VMEM((2 * segment + count, LANES), F32),
            pltpu.VMEM((kv_heads, segment, LANES), BF16),
            pltpu.SemaphoreType.DMA,
        ],
        compiler_params=params(),
        cost_estimate=cost(0, 5 << 20),
        name="cache",
    )(continuing, cache_row, cache_len, rows, fresh, fresh_partner)
    return (layer, cache)


def solution(mesh):
    return jax.shard_map(
        on_device,
        mesh=mesh,
        in_specs=(
            P("req", None, None),
            P(),
            P(None, "tp"),
            P(),
            P("tp", None),
            P(),
            P(),
            P("req", None, None, None),
            P(),
            P(),
            P(),
        ),
        out_specs=(P("req", None, None), P("req", None, "tp", None)),
        check_vma=False,
    )
```

time: 407 us -> 148 us (0.36)
  waiting for transfers between devices: 236 us -> 35.9 us
  local copies, waits for them, and re-layouts: 66.8 us -> 15.5 us
  other arithmetic: 41.1 us -> 0.93 us
  Pallas kernels: 0 us -> 34.4 us
  matrix products: 33 us -> 0 us
  blocking collectives: 0 us -> 27.8 us
  starting transfers between devices: 13.9 us -> 18.5 us
    all_to_all x2, waiting for transfers between devices: 190 us -> 19.2 us  [exchanged(): return lax.all_to_all(value, 'req', split_axis=0, concat_axis=0, tiled=True)]
    pallas_call x0 -> x10, Pallas kernels: none -> 34.4 us  [the longest x1 6.88 us: on_device(): pl.pallas_call(project_kernel, grid=(width // block,), out_shape=jax.Shap...]
    psum x1 -> x0, waiting for transfers between devices: 30 us -> none  [on_device(): lax.psum(jnp.dot(mixed_all, w_out, preferred_element_type=jnp.float32), '...]
    all_to_all x0 -> x2, blocking collectives: none -> 27.8 us  [exchanged(): return lax.all_to_all(value, 'req', split_axis=0, concat_axis=0, tiled=True)]
    gather x5 -> x0, local copies, waits for them, and re-layouts: 25.4 us -> none  [the longest x4 20.1 us: on_device(): chosen = jnp.take(keys_all[number], head_select, axis=0)]
    dot_general x5 -> x0, matrix products: 22.3 us -> none  [the longest x2 13.3 us: attend(): jnp.einsum('hqk,hkd->qhd', probs, keys_one[..., head_dim:], preferred_ele...]
    select_n x6 -> x0, other arithmetic: 16.3 us -> none  [the longest x2 5.85 us: on_device(): chosen = jnp.take(keys_all[number], head_select, axis=0)]
    scatter x6 -> x0, local copies, waits for them, and re-layouts: 12.4 us -> none
  transfers between devices with their start and end apart: 4 -> 11, of which waited for: 4 -> 4; matrix products, arithmetic and copies ran while one was open for 13% -> 1% of each run, Pallas kernels for 0% -> 21%
where the time goes in v1:
time: 148 us; the launch traced here: 147 us
  waiting for transfers between devices  35.9 us (24%)
  Pallas kernels  34.4 us (23%)
  blocking collectives  27.8 us (19%)
  starting transfers between devices  18.5 us (12%)
  local copies, waits for them, and re-layouts  15.5 us (10%)
  between operations  14.4 us (10%)
    all_to_all x2, blocking collectives, exchanged(): return lax.all_to_all(value, 'req', split_axis=0, concat_axis=0, tiled=True)  27.8 us
    all_to_all x2, waiting for transfers between devices, exchanged(): return lax.all_to_all(value, 'req', split_axis=0, concat_axis=0, tiled=True)  19.2 us
    ppermute x8, waiting for transfers between devices, permuted(): return lax.ppermute(value, axis, pairs)  16.7 us
    unnamed x63, local copies, waits for them, and re-layouts  14.8 us
    all_to_all x2, starting transfers between devices, exchanged(): return lax.all_to_all(value, 'req', split_axis=0, concat_axis=0, tiled=True)  10.1 us
    ppermute x8, starting transfers between devices, permuted(): return lax.ppermute(value, axis, pairs)  8.32 us
    pallas_call x1, Pallas kernels, on_device(): pl.pallas_call(project_kernel, grid=(width // block,), out_shape=jax.Shap...  6.88 us
    pallas_call x1, Pallas kernels, on_device(): pl.pallas_call(functools.partial(row_kernel, requests, o_chunk), grid=(he...  6.8 us
  transfers between devices with their start and end apart: 11, of which 4 were waited for; matrix products, arithmetic and copies ran while one was open for 1% of the time, Pallas kernels for 21%

profile of v1, /device:TPU:0, one launch (start us, length us, event | category | flops | bytes accessed | tf_op | source)
XLA Modules:
  0.0 147.5 jit_solution(13882536901818874562)
XLA Ops:
  7.2 1.7 %copy-done.1 = bf16[1,5,2048,128]{3,2,1,0:T(8,128)(2,1)S(1)} copy-done((bf16[1,5,2048,128]{3,2,1,0:T(8,128)(2,1)S(1)}, bf16[1,5,2048,128]{3,2,1,0:T(8,128)(2,1)}, u32[]{:S(2)}) %copy-start.1) | copy-done | bytes 2621464
  9.1 3.0 %collective-permute-start.6 = (bf16[5,288,128]{2,1,0:T(8,128)(2,1)S(1)}, bf16[5,288,128]{2,1,0:T(8,128)(2,1)S(1)}, u32[]{:S(2)}, u32[]{:S(2)}) collective-permute-start(bf16[5,288,128]{2,1,0:T(8,128)(2,1)S(1)} %get-tuple-element.13), channel_id=1, source_target_pairs={{0,4},{4,0},{8,12},{12,8},{16,20},{20,16},{24,28},{28,24},{1,5},{5... | collective-permute-start | bytes 1105928 | tf_op jit(solution)/shard_map/ppermute | solution.py:363
  12.1 8.6 %collective-permute-done.6 = bf16[5,288,128]{2,1,0:T(8,128)(2,1)S(1)} collective-permute-done((bf16[5,288,128]{2,1,0:T(8,128)(2,1)S(1)}, bf16[5,288,128]{2,1,0:T(8,128)(2,1)S(1)}, u32[]{:S(2)}, u32[]{:S(2)}) %collective-permute-start.6) | collective-permute-done | bytes 368672 | tf_op jit(solution)/shard_map/ppermute | solution.py:363
  20.7 0.9 pad_maximum_fusion
  21.8 0.8 copy.20.w
  22.8 4.7 %query.1 = (bf16[2,256,2048]{2,1,0:T(8,128)(2,1)S(1)}, bf16[8,2,80,128]{3,2,1,0:T(8,128)(2,1)}) custom-call(s32[16]{0:T(128)S(1)} %copy-done.14, s32[16]{0:T(128)S(1)} %copy-done.19, bf16[2,256,2048]{2,1,0:T(8,128)(2,1)} %tok.3, f32[1,2048]{1,0:T(1,128)S(1)} %bitcast.9, bf16[2048,320]{1,0:T(8,128)(2,1)S(1)} %copy.20.w, f32[1,128]{1,0:T(1,128)S(1)} %tile.17.qg, ...), custom_call_target="tpu_custom_call" | custom-call | flops 805306368 | bytes 6291456 | tf_op jit(solution)/shard_map/query/pallas_call | solution.py:429
  27.5 1.3 copy-done.4
  28.8 6.1 %all-to-all-start = ((bf16[8,2,80,128]{3,2,1,0:T(8,128)(2,1)}), bf16[8,2,80,128]{3,2,1,0:T(8,128)(2,1)S(1)}, u32[]{:S(2)}, u32[]{:S(2)}) async-start(bf16[8,2,80,128]{3,2,1,0:T(8,128)(2,1)} %get-tuple-element.8.q), calls=%async_computation | async-start | bytes 655360 | tf_op jit(solution)/shard_map/all_to_all | solution.py:367
  34.9 1.5 collective-permute-start.3
  36.3 19.2 %all-to-all-done = bf16[8,2,80,128]{3,2,1,0:T(8,128)(2,1)S(1)} async-done(((bf16[8,2,80,128]{3,2,1,0:T(8,128)(2,1)}), bf16[8,2,80,128]{3,2,1,0:T(8,128)(2,1)S(1)}, u32[]{:S(2)}, u32[]{:S(2)}) %all-to-all-start) | async-done | bytes 327712 | tf_op jit(solution)/shard_map/all_to_all | solution.py:367
  55.5 0.8 route_query.1
  56.3 13.6 %all_to_all.20.q = bf16[8,80,128]{2,1,0:T(8,128)(2,1)S(1)} all-to-all(bf16[8,80,128]{2,1,0:T(8,128)(2,1)S(1)} %route_query.1), channel_id=1, replica_groups=mesh['req'=8,'tp'=4] {'req'}, dimensions={0} | all-to-all | bytes 327680 | tf_op jit(solution)/shard_map/all_to_all | solution.py:367
  69.9 1.8 %copy-done.2 = bf16[1,5,2048,128]{3,2,1,0:T(8,128)(2,1)S(1)} copy-done((bf16[1,5,2048,128]{3,2,1,0:T(8,128)(2,1)S(1)}, bf16[1,5,2048,128]{3,2,1,0:T(8,128)(2,1)}, u32[]{:S(2)}) %copy-start.2) | copy-done | bytes 2621464
  72.3 0.7 copy-done.20
  72.9 0.7 copy-done.24
  73.6 6.8 %attend_row.1 = bf16[8,96,128]{2,1,0:T(8,128)(2,1)S(1)} custom-call(s32[16]{0:T(128)S(1)} %copy-done.15, s32[16]{0:T(128)S(1)} %copy-done.24, s32[16]{0:T(128)S(1)} %copy-done.20, bf16[8,80,128]{2,1,0:T(8,128)(2,1)S(1)} %all_to_all.20.q, bf16[1,5,2048,128]{3,2,1,0:T(8,128)(2,1)S(1)} %copy-done.2), custom_call_target="tpu_custom_call" | custom-call | flops 2684354560 | bytes 2097152 | tf_op jit(solution)/shard_map/attend_row/pallas_call | solution.py:509
  80.4 14.3 %all_to_all.21.src = bf16[8,96,128]{2,1,0:T(8,128)(2,1)S(1)} all-to-all(bf16[8,96,128]{2,1,0:T(8,128)(2,1)S(1)} %attend_row.1), channel_id=1, replica_groups=mesh['req'=8,'tp'=4] {'req'}, dimensions={0} | all-to-all | bytes 393216 | tf_op jit(solution)/shard_map/all_to_all | solution.py:367
  94.7 1.5 %route_result.1 = bf16[16,96,128]{2,1,0:T(8,128)(2,1)} custom-call(s32[16]{0:T(128)S(1)} %copy-done.15, s32[16]{0:T(128)S(1)} %copy-done.25, bf16[8,96,128]{2,1,0:T(8,128)(2,1)S(1)} %all_to_all.21.src), custom_call_target="tpu_custom_call" | custom-call | bytes 1048576 | tf_op jit(solution)/shard_map/route_result/pallas_call | solution.py:532
  96.2 4.1 %all-to-all-start.3 = ((bf16[8,2,96,128]{3,2,1,0:T(8,128)(2,1)}), bf16[8,2,96,128]{3,2,1,0:T(8,128)(2,1)}, u32[]{:S(2)}, u32[]{:S(2)}) async-start(bf16[8,2,96,128]{3,2,1,0:T(8,128)(2,1)} %bitcast.2), calls=%async_computation.3 | async-start | bytes 786432 | tf_op jit(solution)/shard_map/all_to_all | solution.py:367
  101.4 1.6 %copy-done.5 = bf16[2,256,2048]{2,1,0:T(8,128)(2,1)S(1)} copy-done((bf16[2,256,2048]{2,1,0:T(8,128)(2,1)S(1)}, bf16[2,256,2048]{2,1,0:T(8,128)(2,1)}, u32[]{:S(2)}) %copy-start.5) | copy-done | bytes 2097176
  103.0 0.9 copy-done.9
  103.9 0.9 copy-done.11
  106.7 3.4 %fresh.1.mine = bf16[2,5,256,128]{3,2,1,0:T(8,128)(2,1)S(1)} custom-call(s32[16]{0:T(128)S(1)} %copy-done.16, s32[16]{0:T(128)S(1)} %copy-done.21, bf16[2,256,2048]{2,1,0:T(8,128)(2,1)S(1)} %copy-done.5, bf16[2048,640]{1,0:T(8,128)(2,1)S(1)} %copy-done.3, f32[1,128]{1,0:T(1,128)S(1)} %copy-done.27, f32[256,128]{1,0:T(8,128)S(1)} %copy-done.6, ...), custom_call_target="tpu_custom_call" | custom-call | flops 1342177280 | bytes 6291456 | tf_op jit(solution)/shard_map/fresh/pallas_call | solution.py:456
  110.1 5.0 %attend_new.1 = (f32[2,3,256,128]{3,2,1,0:T(8,128)S(1)}, f32[2,256,128]{2,1,0:T(8,128)S(1)}) custom-call(bf16[8,2,80,128]{3,2,1,0:T(8,128)(2,1)} %get-tuple-element.8.q, bf16[2,5,256,128]{3,2,1,0:T(8,128)(2,1)S(1)} %fresh.1.mine), custom_call_target="tpu_custom_call" | custom-call | flops 671088640 | bytes 4194304 | tf_op jit(solution)/shard_map/attend_new/pallas_call | solution.py:475
  115.2 1.9 %merge.1.m0 = bf16[2,640,128]{2,1,0:T(8,128)(2,1)S(1)} custom-call(s32[16]{0:T(128)S(1)} %copy-done.17, bf16[8,2,96,128]{3,2,1,0:T(8,128)(2,1)} %all-to-all-done.3.far, f32[2,3,256,128]{3,2,1,0:T(8,128)S(1)} %get-tuple-element.10.near, f32[2,256,128]{2,1,0:T(8,128)S(1)} %get-tuple-element.11.lse), custom_call_target="tpu_custom_call" | custom-call | bytes 3145728 | tf_op jit(solution)/shard_map/merge/pallas_call | solution.py:543
  117.1 1.5 collective-permute-start
  118.5 1.8 %collective-permute-start.7 = (bf16[2,5,256,128]{3,2,1,0:T(8,128)(2,1)S(1)}, bf16[2,5,256,128]{3,2,1,0:T(8,128)(2,1)S(1)}, u32[]{:S(2)}, u32[]{:S(2)}) collective-permute-start(bf16[2,5,256,128]{3,2,1,0:T(8,128)(2,1)S(1)} %fresh.1.mine), channel_id=1, source_target_pairs={{0,4},{4,0},{8,12},{12,8},{16,20},{20,16},{24,28},{28,24},{1,5},{5... | collective-permute-start | bytes 1966088 | tf_op jit(solution)/shard_map/ppermute | solution.py:363
  120.4 6.5 %collective-permute-done.m1 = bf16[2,640,128]{2,1,0:T(8,128)(2,1)S(1)} collective-permute-done((bf16[2,640,128]{2,1,0:T(8,128)(2,1)S(1)}, bf16[2,640,128]{2,1,0:T(8,128)(2,1)S(1)}, u32[]{:S(2)}, u32[]{:S(2)}) %collective-permute-start) | collective-permute-done | bytes 327712 | tf_op jit(solution)/shard_map/ppermute | solution.py:363
  126.9 1.6 %collective-permute-done.2.m3 = bf16[2,640,128]{2,1,0:T(8,128)(2,1)S(1)} collective-permute-done((bf16[2,640,128]{2,1,0:T(8,128)(2,1)S(1)}, bf16[2,640,128]{2,1,0:T(8,128)(2,1)S(1)}, u32[]{:S(2)}, u32[]{:S(2)}) %collective-permute-start.2) | collective-permute-done | bytes 327712 | tf_op jit(solution)/shard_map/ppermute | solution.py:363
  128.5 6.9 %project.1 = bf16[2,256,2048]{2,1,0:T(8,128)(2,1)} custom-call(bf16[2,640,128]{2,1,0:T(8,128)(2,1)S(1)} %merge.1.m0, bf16[2,640,128]{2,1,0:T(8,128)(2,1)S(1)} %collective-permute-done.m1, bf16[2,640,128]{2,1,0:T(8,128)(2,1)S(1)} %collective-permute-done.1.m2, bf16[2,640,128]{2,1,0:T(8,128)(2,1)S(1)} %collective-permute-done.2.m3, bf16[320,2048]{1,0:T(8,128)(2,1)} %w0.1, ...), custom_call_target="tpu_custom_call" | custom-call | flops 2684354560 | bytes 10485760 | tf_op jit(solution)/shard_map/project/pallas_call | solution.py:567
  135.4 1.8 %copy-done = bf16[8,5,288,128]{3,2,1,0:T(8,128)(2,1)S(1)} copy-done((bf16[8,5,288,128]{3,2,1,0:T(8,128)(2,1)S(1)}, bf16[8,5,288,128]{3,2,1,0:T(8,128)(2,1)}, u32[]{:S(2)}) %copy-start) | copy-done | bytes 2949144
  137.2 3.4 %cache.1 = bf16[4,5,288,128]{3,2,1,0:T(8,128)(2,1)} custom-call(s32[16]{0:T(128)S(1)} %copy-done.17, s32[16]{0:T(128)S(1)} %copy-done.26, s32[16]{0:T(128)S(1)} %copy-done.22, bf16[4,2,5,288,128]{4,3,2,1,0:T(8,128)(2,1)S(1)} %bitcast.6, bf16[2,5,256,128]{3,2,1,0:T(8,128)(2,1)S(1)} %fresh.1.mine, bf16[2,5,256,128]{3,2,1,0:T(8,128)(2,1)S(1)} %collective-permute-done.7.theirs), custom_call_target="tpu_custom_call" | custom-call | bytes 5242880 | tf_op jit(solution)/shard_map/cache/pallas_call | solution.py:580
  (71 shorter events, 4.2 us)
Async XLA Ops:
  7.2 128.2 %all-gather.3.cloned.1.call-start = ((), (), s32[]{:S(2)}) async-start(), calls=%async_computation.4 | async-start | bytes 3686400 | tf_op jit(solution)/shard_map/all_gather | solution.py:423
  7.2 1.7 %copy-start.1 = (bf16[1,5,2048,128]{3,2,1,0:T(8,128)(2,1)S(1)}, bf16[1,5,2048,128]{3,2,1,0:T(8,128)(2,1)}, u32[]{:S(2)}) copy-start(bf16[1,5,2048,128]{3,2,1,0:T(8,128)(2,1)} %stored.1) | copy-start | bytes 7864324
  9.1 12.6 %copy-start.28 = (bf16[2048,320]{0,1:T(8,128)(2,1)S(1)}, bf16[2048,320]{0,1:T(8,128)(2,1)}, u32[]{:S(2)}) copy-start(bf16[2048,320]{0,1:T(8,128)(2,1)} %param.19) | copy-start | bytes 3932164
  9.1 11.6 %collective-permute-start.6 = (bf16[5,288,128]{2,1,0:T(8,128)(2,1)S(1)}, bf16[5,288,128]{2,1,0:T(8,128)(2,1)S(1)}, u32[]{:S(2)}, u32[]{:S(2)}) collective-permute-start(bf16[5,288,128]{2,1,0:T(8,128)(2,1)S(1)} %get-tuple-element.13), channel_id=1, source_target_pairs={{0,4},{4,0},{8,12},{12,8},{16,20},{20,16},{24,28},{28,24},{1,5},{5... | collective-permute-start | bytes 1105928 | tf_op jit(solution)/shard_map/ppermute | solution.py:363
  21.7 1.1 copy-start.6
  21.7 1.1 copy-start.7
  21.7 1.1 copy-start.8
  21.7 1.0 copy-start.10
  21.7 1.0 copy-start.12
  21.8 1.0 copy-start.13
  21.8 1.0 copy-start.14
  21.8 1.0 copy-start.18
  22.8 32.7 %copy-start.23 = (s32[16]{0:T(128)S(1)}, s32[16]{0:T(128)}, u32[]{:S(2)}) copy-start(s32[16]{0:T(128)} %crow.7) | copy-start | bytes 196
  27.5 1.3 copy-start.4
  28.8 26.7 %all-to-all-start = ((bf16[8,2,80,128]{3,2,1,0:T(8,128)(2,1)}), bf16[8,2,80,128]{3,2,1,0:T(8,128)(2,1)S(1)}, u32[]{:S(2)}, u32[]{:S(2)}) async-start(bf16[8,2,80,128]{3,2,1,0:T(8,128)(2,1)} %get-tuple-element.8.q), calls=%async_computation | async-start | bytes 655360 | tf_op jit(solution)/shard_map/all_to_all | solution.py:367
  34.9 65.5 %collective-permute-start.3 = (bf16[320,2048]{1,0:T(8,128)(2,1)}, bf16[320,2048]{1,0:T(8,128)(2,1)}, u32[]{:S(2)}, u32[]{:S(2)}) collective-permute-start(bf16[320,2048]{1,0:T(8,128)(2,1)} %w0.1), channel_id=1, source_target_pairs={{0,2},{1,3},{2,0},{3,1},{4,6},{5,7},{6,4},{7,5},{8,10},{9,11},{10,... | collective-permute-start | bytes 3932168 | tf_op jit(solution)/shard_map/ppermute | solution.py:363
  69.9 1.8 %copy-start.2 = (bf16[1,5,2048,128]{3,2,1,0:T(8,128)(2,1)S(1)}, bf16[1,5,2048,128]{3,2,1,0:T(8,128)(2,1)}, u32[]{:S(2)}) copy-start(bf16[1,5,2048,128]{3,2,1,0:T(8,128)(2,1)} %stored.1) | copy-start | bytes 7864324
  73.6 21.1 %copy-start.25 = (s32[16]{0:T(128)S(1)}, s32[16]{0:T(128)}, u32[]{:S(2)}) copy-start(s32[16]{0:T(128)} %crow.7) | copy-start | bytes 196
  73.6 27.8 %copy-start.3 = (bf16[2048,640]{1,0:T(8,128)(2,1)S(1)}, bf16[2048,640]{1,0:T(8,128)(2,1)}, u32[]{:S(2)}) copy-start(bf16[2048,640]{1,0:T(8,128)(2,1)} %w.2) | copy-start | bytes 7864324
  80.4 20.4 %copy-start.30 = (f32[64]{0:T(128)S(1)}, f32[64]{0:T(128)}, u32[]{:S(2)}) copy-start(f32[64]{0:T(128)} %param.23) | copy-start | bytes 772
  96.2 19.0 %all-to-all-start.3 = ((bf16[8,2,96,128]{3,2,1,0:T(8,128)(2,1)}), bf16[8,2,96,128]{3,2,1,0:T(8,128)(2,1)}, u32[]{:S(2)}, u32[]{:S(2)}) async-start(bf16[8,2,96,128]{3,2,1,0:T(8,128)(2,1)} %bitcast.2), calls=%async_computation.3 | async-start | bytes 786432 | tf_op jit(solution)/shard_map/all_to_all | solution.py:367
  100.3 26.6 %collective-permute-start.4 = (bf16[320,2048]{1,0:T(8,128)(2,1)}, bf16[320,2048]{1,0:T(8,128)(2,1)}, u32[]{:S(2)}, u32[]{:S(2)}) collective-permute-start(bf16[320,2048]{1,0:T(8,128)(2,1)} %w0.1), channel_id=1, source_target_pairs={{0,1},{1,0},{2,3},{3,2},{4,5},{5,4},{6,7},{7,6},{8,9},{9,8},{10,11... | collective-permute-start | bytes 3932168 | tf_op jit(solution)/shard_map/ppermute | solution.py:363
  100.4 28.1 %collective-permute-start.5 = (bf16[320,2048]{1,0:T(8,128)(2,1)}, bf16[320,2048]{1,0:T(8,128)(2,1)}, u32[]{:S(2)}, u32[]{:S(2)}) collective-permute-start(bf16[320,2048]{1,0:T(8,128)(2,1)} %collective-permute-done.3.w1), channel_id=1, source_target_pairs={{0,1},{1,0},{2,3},{3,2},{4,5},{5,4},{6,7},{7,6},{8,9},{9,8},{10,11... | collective-permute-start | bytes 3932168 | tf_op jit(solution)/shard_map/ppermute | solution.py:363
  101.4 1.6 %copy-start.5 = (bf16[2,256,2048]{2,1,0:T(8,128)(2,1)S(1)}, bf16[2,256,2048]{2,1,0:T(8,128)(2,1)}, u32[]{:S(2)}) copy-start(bf16[2,256,2048]{2,1,0:T(8,128)(2,1)} %copy-done.4) | copy-start | bytes 6291460
  110.1 5.0 %copy-start.17 = (s32[16]{0:T(128)S(1)}, s32[16]{0:T(128)}, u32[]{:S(2)}) copy-start(s32[16]{0:T(128)} %cont.13) | copy-start | bytes 196
  117.1 18.3 %copy-start.22 = (s32[16]{0:T(128)S(1)}, s32[16]{0:T(128)}, u32[]{:S(2)}) copy-start(s32[16]{0:T(128)} %clen.7) | copy-start | bytes 196
  117.1 18.3 %copy-start.26 = (s32[16]{0:T(128)S(1)}, s32[16]{0:T(128)}, u32[]{:S(2)}) copy-start(s32[16]{0:T(128)} %crow.7) | copy-start | bytes 196
  117.1 9.8 %collective-permute-start = (bf16[2,640,128]{2,1,0:T(8,128)(2,1)S(1)}, bf16[2,640,128]{2,1,0:T(8,128)(2,1)S(1)}, u32[]{:S(2)}, u32[]{:S(2)}) collective-permute-start(bf16[2,640,128]{2,1,0:T(8,128)(2,1)S(1)} %merge.1.m0), channel_id=1, source_target_pairs={{0,2},{1,3},{2,0},{3,1},{4,6},{5,7},{6,4},{7,5},{8,10},{9,11},{10,... | collective-permute-start | bytes 983048 | tf_op jit(solution)/shard_map/ppermute | solution.py:363
  118.5 16.8 %collective-permute-start.7 = (bf16[2,5,256,128]{3,2,1,0:T(8,128)(2,1)S(1)}, bf16[2,5,256,128]{3,2,1,0:T(8,128)(2,1)S(1)}, u32[]{:S(2)}, u32[]{:S(2)}) collective-permute-start(bf16[2,5,256,128]{3,2,1,0:T(8,128)(2,1)S(1)} %fresh.1.mine), channel_id=1, source_target_pairs={{0,4},{4,0},{8,12},{12,8},{16,20},{20,16},{24,28},{28,24},{1,5},{5... | collective-permute-start | bytes 1966088 | tf_op jit(solution)/shard_map/ppermute | solution.py:363
  120.4 6.5 %collective-permute-start.1 = (bf16[2,640,128]{2,1,0:T(8,128)(2,1)S(1)}, bf16[2,640,128]{2,1,0:T(8,128)(2,1)S(1)}, u32[]{:S(2)}, u32[]{:S(2)}) collective-permute-start(bf16[2,640,128]{2,1,0:T(8,128)(2,1)S(1)} %merge.1.m0), channel_id=1, source_target_pairs={{0,1},{1,0},{2,3},{3,2},{4,5},{5,4},{6,7},{7,6},{8,9},{9,8},{10,11... | collective-permute-start | bytes 983048 | tf_op jit(solution)/shard_map/ppermute | solution.py:363
  126.9 1.6 %collective-permute-start.2 = (bf16[2,640,128]{2,1,0:T(8,128)(2,1)S(1)}, bf16[2,640,128]{2,1,0:T(8,128)(2,1)S(1)}, u32[]{:S(2)}, u32[]{:S(2)}) collective-permute-start(bf16[2,640,128]{2,1,0:T(8,128)(2,1)S(1)} %collective-permute-done.m1), channel_id=1, source_target_pairs={{0,1},{1,0},{2,3},{3,2},{4,5},{5,4},{6,7},{7,6},{8,9},{9,8},{10,11... | collective-permute-start | bytes 983048 | tf_op jit(solution)/shard_map/ppermute | solution.py:363
  135.4 1.8 %copy-start = (bf16[8,5,288,128]{3,2,1,0:T(8,128)(2,1)S(1)}, bf16[8,5,288,128]{3,2,1,0:T(8,128)(2,1)}, u32[]{:S(2)}) copy-start(bf16[8,5,288,128]{3,2,1,0:T(8,128)(2,1)} %all-gather.3.cloned.1.call-done) | copy-start | bytes 8847364
  (10 other events, 7.6 us)
Sparse Core Ops, SparseCore 0:
  21.8 76.1 all-gather.2

commit v2 on v1

v2 whole, which is shorter than its diff:
```python
import functools
import math

import jax
import jax.numpy as jnp
import numpy as np
from jax import lax
from jax.experimental import pallas as pl
from jax.experimental.pallas import tpu as pltpu
from jax.sharding import PartitionSpec as P

BF16 = jnp.bfloat16
F32 = jnp.float32
LANES = 128
EPS = 1e-06
NEG = -1e30
SMEM = pl.BlockSpec(memory_space=pltpu.SMEM)


HINT = pl.CostEstimate(flops=0, bytes_accessed=1024, transcendentals=0)


def cost(flops, moved):
    return pl.CostEstimate(flops=int(flops), bytes_accessed=int(moved), transcendentals=0)


def params(mib=20):
    return pltpu.CompilerParams(vmem_limit_bytes=mib << 20)


def lane_iota(rows):
    return lax.broadcasted_iota(jnp.int32, (rows, LANES), 1)


def angle_tables(head_dim, new_count, cache_span):
    half = head_dim // 2
    freq = np.exp(-math.log(10000.0) * np.arange(half, dtype=np.float64) * 2.0 / head_dim)
    freq = np.tile(freq.astype(np.float32).astype(np.float64), LANES // half)

    def pair(positions):
        angle = positions[:, None].astype(np.float64) * freq[None, :]
        return np.cos(angle).astype(np.float32), np.sin(angle).astype(np.float32)

    fine = pair(np.arange(new_count))
    coarse = pair(np.arange(cache_span // 16 + 8) * 16)
    small = pair(np.arange(16))
    return np.stack([np.concatenate(part) for part in zip(fine, small, coarse)])


def rotation(length, count, table):
    high = length // 16
    low = length - high * 16
    row = lambda which, place: table[which, pl.ds(place, 1), :]
    ch, sh = row(0, count + 16 + high), row(1, count + 16 + high)
    cl, sl = row(0, count + low), row(1, count + low)
    cb, sb = ch * cl - sh * sl, sh * cl + ch * sl
    ci, si = table[0, :count], table[1, :count]
    cosine = ci * cb - si * sb
    sine = si * cb + ci * sb
    lanes = lane_iota(ci.shape[0])
    return cosine, jnp.where(lanes % 64 < 32, -sine, sine)


def norm_rope(tile, gain, cosine, sine, blocks):
    square = tile * tile
    high = square.astype(BF16)
    low = (square - high.astype(F32)).astype(BF16)
    mean = jnp.dot(high, blocks, preferred_element_type=F32) + jnp.dot(
        low, blocks, preferred_element_type=F32
    )
    unit = tile * lax.rsqrt(mean + EPS) * gain
    lanes = lane_iota(tile.shape[0])
    other = jnp.where(lanes % 64 < 32, pltpu.roll(unit, 96, 1), pltpu.roll(unit, 32, 1))
    return unit * cosine + other * sine


def half_blocks():
    rows = lax.broadcasted_iota(jnp.int32, (LANES, LANES), 0)
    cols = lax.broadcasted_iota(jnp.int32, (LANES, LANES), 1)
    return jnp.where(rows // 64 == cols // 64, 1.0 / 64.0, 0.0).astype(BF16)


def live(meta, request):
    return meta[0, request] == 1


def live_length(meta, request):
    return jnp.where(live(meta, request), meta[2, request], 0)


def to_chunks(ref, lead, value, chunk):
    rows = value.shape[0]
    for start in range(0, rows, chunk):
        size = min(chunk, rows - start)
        ref[(start // chunk,) + lead + (pl.ds(0, size),)] = value[start : start + size]


def normalized(tok, gain):
    x = tok[0].astype(F32)
    mean = jnp.mean(x * x, axis=-1, keepdims=True)
    return (x * lax.rsqrt(mean + EPS) * gain[...]).astype(BF16)


def query_kernel(req_dev, chunk, cont, clen, tok, gain, w, qg, table, q):
    b = pl.program_id(0)
    count = tok.shape[1]
    half = count // 2
    request = lax.axis_index("req") * req_dev + b
    length = jnp.where(cont[request] == 1, clen[request], 0)
    out = lax.dot_general(
        normalized(tok, gain), w[...], (((1,), (1,)), ((), ())), preferred_element_type=F32
    )
    cosine, sine = rotation(length, count, table)
    blocks = half_blocks()
    gains = jnp.concatenate([qg[...]] * 2, axis=1)
    pair01 = norm_rope(out[:, :128], gains, cosine, sine, blocks)
    pair23 = norm_rope(out[:, 128:256], gains, cosine, sine, blocks)
    last = out[:, 256:320]
    last = jnp.concatenate([last[:half], last[half:]], axis=1)
    lanes = lane_iota(half)
    pick = lambda v: jnp.where(lanes < 64, v[:half], v[half:])
    last = norm_rope(last, gains, pick(cosine), pick(sine), blocks)
    packed = (jnp.concatenate([pair01, pair23, last], axis=0) * 0.125).astype(BF16)
    to_chunks(q, (0,), packed, chunk)


def fresh_kernel(req_dev, meta, tok, gain, w, kg, table, after, fresh):
    del after
    b = pl.program_id(0)
    count = tok.shape[1]
    length = live_length(meta, lax.axis_index("req") * req_dev + b)
    out = jnp.dot(normalized(tok, gain), w[...], preferred_element_type=F32)
    cosine, sine = rotation(length, count, table)
    blocks = half_blocks()
    lanes = lane_iota(count)
    gains = jnp.concatenate([kg[...]] * 2, axis=1)
    for head in range(fresh.shape[1]):
        tile = out[:, head * 128 : head * 128 + 128]
        keys = norm_rope(tile, gains, cosine, sine, blocks)
        fresh[0, head] = jnp.where(lanes < 64, keys, tile).astype(BF16)


def split_heads(packed, count):
    half = count // 2
    wide = packed.astype(F32)
    lanes = lane_iota(count)
    tiles = [wide[:count], pltpu.roll(wide[:count], 64, 1)]
    tiles += [wide[count : 2 * count], pltpu.roll(wide[count : 2 * count], 64, 1)]
    last = wide[2 * count : 2 * count + half]
    tiles.append(jnp.concatenate([last, pltpu.roll(last, 64, 1)], axis=0))
    return [jnp.where(lanes < 64, tile, 0.0).astype(BF16) for tile in tiles]


def soft(scores, values):
    top = jnp.max(scores, axis=-1, keepdims=True)
    weights = jnp.exp(scores - top)
    total = jnp.sum(weights, axis=-1, keepdims=True)
    out = jnp.dot(weights.astype(BF16), values, preferred_element_type=F32)
    return out / total, top + jnp.log(total)


def local_kernel(groups, q, fresh, out):
    heads = 5
    count = fresh.shape[2]
    first = lax.axis_index("tp") * heads
    lanes = lane_iota(count)
    rows = lax.broadcasted_iota(jnp.int32, (count, count), 0)
    cols = lax.broadcasted_iota(jnp.int32, (count, count), 1)
    packed = q[...].reshape(-1, LANES)
    tiles = split_heads(packed, count)
    stats = jnp.zeros((count, LANES), F32)
    kept = []
    for head in range(heads):
        kv = fresh[0, (first + head) // groups]
        scores = lax.dot_general(
            tiles[head], kv, (((1,), (1,)), ((), ())), preferred_element_type=F32
        )
        scores = jnp.where(cols <= rows, scores, NEG)
        mixed, level = soft(scores, kv)
        stats = jnp.where(lanes == head, level, stats)
        kept.append(mixed)
    roll = lambda v: pltpu.roll(v, 64, 1)
    out[0, 0] = jnp.where(lanes < 64, roll(kept[0]), kept[1])
    out[0, 1] = jnp.where(lanes < 64, roll(kept[2]), kept[3])
    out[0, 2] = jnp.where(lanes < 64, roll(kept[4]), roll(stats))


def each(requests, step):
    if requests <= 32:
        for r in range(requests):
            step(r)
    else:
        pl.loop(0, requests)(step)


def route_query_kernel(requests, meta, src, dst):
    def step(r):
        @pl.when(live(meta, r))
        def _():
            dst[meta[1, r]] = src[r]

    each(requests, step)


def route_result_kernel(requests, meta, src, dst):
    def step(r):
        dst[r] = src[jnp.where(live(meta, r), meta[1, r], 0)]

    each(requests, step)


def row_kernel(requests, groups, chunk, meta, q, stored, out, q_sc, o_sc, s_sc, kv_sc, b_sc, sem):
    head = pl.program_id(0)
    heads, count = q_sc.shape[:2]
    span, kv_heads = kv_sc.shape[1], stored.shape[1]
    first = lax.axis_index("tp") * heads // groups
    which = (lax.axis_index("tp") * heads + head) // groups - first

    def fetch(number):
        source = stored.at[0, jnp.minimum(first + number, kv_heads - 1)]
        return pltpu.make_async_copy(source, kv_sc.at[number], sem.at[number])

    @pl.when(head == 0)
    def _():
        fetch(0).start()
        fetch(1).start()
        row = lax.axis_index("req")

        def find(r, length):
            mine = jnp.logical_and(live(meta, r), meta[1, r] == row)
            return jnp.where(mine, meta[2, r], length)

        length = lax.fori_loop(0, requests, find, 0)
        position = lax.broadcasted_iota(jnp.int32, (8, span), 1)
        b_sc[...] = jnp.where(position < length, 0.0, NEG)
        packed = q[...].reshape(-1, LANES)
        for number, tile in enumerate(split_heads(packed, count)):
            q_sc[number] = tile
        s_sc[...] = jnp.zeros_like(s_sc)
        fetch(0).wait()
        fetch(1).wait()

    kv = kv_sc[which]
    scores = lax.dot_general(
        q_sc[head], kv, (((1,), (1,)), ((), ())), preferred_element_type=F32
    )
    mixed, level = soft(scores + b_sc[0:1, :], kv)
    o_sc[head] = mixed
    s_sc[...] = jnp.where(lane_iota(count) == head, level, s_sc[...])

    @pl.when(head == heads - 1)
    def _():
        lanes = lane_iota(count)
        roll = lambda v, n: pltpu.roll(v, n, 1)
        level = s_sc[...]
        high = level.astype(BF16).astype(F32)
        mid = (level - high).astype(BF16).astype(F32)
        low = (level - high - mid).astype(BF16).astype(F32)
        stats = roll(high, 64) + roll(mid, 64 + heads) + roll(low, 64 + 2 * heads)
        tiles = [
            jnp.where(lanes < 64, roll(o_sc[0], 64), o_sc[1]),
            jnp.where(lanes < 64, roll(o_sc[2], 64), o_sc[3]),
            jnp.where(lanes < 64, roll(o_sc[4], 64), stats),
        ]
        to_chunks(out, (), jnp.concatenate(tiles, axis=0).astype(BF16), chunk)


def merge_kernel(req_dev, meta, far, near, mixed):
    heads = 5
    count = near.shape[2]
    b = pl.program_id(0)
    request = lax.axis_index("req") * req_dev + b
    lanes = lane_iota(count)
    roll = lambda v, n: pltpu.roll(v, n, 1)
    packed = far[...].reshape(-1, LANES)
    tiles = [packed[p * count : (p + 1) * count].astype(F32) for p in range(3)]
    stats = roll(tiles[2], 64) + roll(tiles[2], 64 - heads) + roll(tiles[2], 64 - 2 * heads)
    far_level = jnp.where(jnp.logical_and(live(meta, request), lanes < heads), stats, NEG)
    near_level = jnp.where(lanes < heads, roll(near[0, 2], 64), 0.0)
    top = jnp.maximum(far_level, near_level)
    far_part = jnp.exp(far_level - top)
    near_part = jnp.exp(near_level - top)
    share = far_part / (far_part + near_part)
    done = []
    for p in range(3):
        left = share[:, 2 * p : 2 * p + 1]
        right = share[:, 2 * p + 1 : 2 * p + 2] if 2 * p + 1 < heads else left
        weight = jnp.where(lanes < 64, left, right)
        done.append(weight * tiles[p] + (1.0 - weight) * near[0, p])
    half = count // 2
    last = jnp.where(lane_iota(half) < 64, done[2][:half], roll(done[2][half:], 64))
    mixed[0] = jnp.concatenate([done[0], done[1], last], axis=0).astype(BF16)


def project_kernel(m_a, m_b, w_a, w_b, base, out, lhs):
    req_dev, count, block = out.shape
    half = count // 2
    sources = (m_a, m_b)

    @pl.when(pl.program_id(0) == 0)
    def _():
        lanes = lane_iota(half)
        for b in range(req_dev):
            start = b * count
            for number, m in enumerate(sources):
                for p in range(2):
                    col = number * 256 + p * 128
                    lhs[start : start + count, col : col + 128] = m[b, p * count : (p + 1) * count]
            left = m_a[b, 2 * count :].astype(F32)
            right = m_b[b, 2 * count :].astype(F32)
            above = jnp.where(lanes < 64, left, pltpu.roll(right, 64, 1))
            below = jnp.where(lanes < 64, pltpu.roll(left, 64, 1), right)
            lhs[start : start + half, 512:640] = above.astype(BF16)
            lhs[start + half : start + count, 512:640] = below.astype(BF16)

    total = base[...].reshape(req_dev * count, block).astype(F32)
    weights = jnp.concatenate([w_a[:256], w_b[:256], w_a[256:], w_b[256:]], axis=0)
    total += jnp.dot(lhs[...], weights, preferred_element_type=F32)
    out[...] = total.astype(out.dtype).reshape(req_dev, count, block)


def held(plane, here):
    apart = plane ^ here
    mid = jnp.logical_or(here == 1, here == 2)
    return jnp.where(apart < 2, apart, jnp.where(mid, 5 - apart, 2 + apart))


def cache_kernel(req_dev, span, meta, *refs):
    blocks, (mine, theirs, _, out, wide, kept_sc, sem) = refs[:-7], refs[-7:]
    l = pl.program_id(0)
    place, tp_place = lax.axis_index("req"), lax.axis_index("tp")
    side = place % 2
    kv_heads, segment = out.shape[1], out.shape[2]
    count = mine.shape[2]

    def fetch(number, action):
        request = (place // 2) * 2 * req_dev + number
        row = jnp.where(live(meta, request), meta[1, request], 0)
        plane, which = row // 2, (row % 2) ^ side
        dst = kept_sc.at[number, :, pl.ds(0, segment), :]
        if len(blocks) == 1:
            action(pltpu.make_async_copy(blocks[0].at[plane, which], dst, sem.at[number]))
            return
        for step, block in enumerate(blocks):

            @pl.when(held(plane, place // 2) == step)
            def _():
                action(pltpu.make_async_copy(block.at[which], dst, sem.at[number]))

    @pl.when(l == 0)
    def _():
        for number in range(2 * req_dev):
            fetch(number, lambda copy: copy.start())

    length = live_length(meta, (place // 2) * 2 * req_dev + l)
    start = (side * lax.axis_size("tp") + tp_place) * segment
    skip = pl.multiple_of(start - jnp.minimum(start, span - segment), 16)
    shift = jnp.clip(start - length, -segment, count) + segment
    position = start + lax.broadcasted_iota(jnp.int32, (segment, LANES), 0)
    old = position < length
    new = jnp.logical_and(position >= length, position < length + count)
    local = l // req_dev == side
    for head in range(kv_heads):

        @pl.when(local)
        def _():
            wide[head, segment : segment + count] = mine[0, head].astype(F32)

        @pl.when(jnp.logical_not(local))
        def _():
            wide[head, segment : segment + count] = theirs[0, head].astype(F32)

    fetch(l, lambda copy: copy.wait())
    for head in range(kv_heads):
        moved = wide[head, pl.ds(shift, segment), :]
        kept = kept_sc[l, head, pl.ds(skip, segment), :].astype(F32)
        out[0, head] = jnp.where(old, kept, jnp.where(new, moved, 0.0)).astype(BF16)


def permuted(value, axis, mask):
    pairs = [(source, source ^ mask) for source in range(lax.axis_size(axis))]
    return lax.ppermute(value, axis, pairs)


def exchanged(value):
    return lax.all_to_all(value, "req", split_axis=0, concat_axis=0, tiled=True)


def full(shape):
    return pl.BlockSpec(shape, lambda *_: (0,) * len(shape))


def on_device(
    tokens,
    attn_gain,
    w_query,
    key_value_weight,
    w_out,
    q_gain,
    k_gain,
    stored,
    continuing,
    cache_row,
    cache_len,
):
    n_req = lax.axis_size("req")
    tp_count = lax.axis_size("tp")
    req_dev, count, width = tokens.shape
    head_dim = q_gain.shape[0]
    kv_heads = key_value_weight.shape[1] // (2 * head_dim)
    heads = w_query.shape[1] // head_dim
    groups = heads * tp_count // kv_heads
    span = stored.shape[2]
    requests = continuing.shape[0]
    segments = 2 * tp_count
    segment = (span + count) // segments
    q_rows = heads * head_dim * count // LANES
    o_rows = -(-heads * head_dim // LANES) * count
    q_chunk = -(-q_rows // (16 * n_req)) * 16
    o_chunk = -(-o_rows // (16 * n_req)) * 16

    table = jnp.asarray(angle_tables(head_dim, count, span))
    table_spec = full(table.shape)
    meta = jnp.stack([continuing, cache_row, cache_len])
    gain_row = attn_gain.reshape(1, width)
    q_gain_row = q_gain.reshape(1, head_dim)
    k_gain_row = k_gain.reshape(1, head_dim)
    w_query_rows = w_query.T
    any_spec = pl.BlockSpec(memory_space=pl.ANY)
    hbm_spec = pl.BlockSpec(memory_space=pltpu.HBM)
    vmem_spec = pl.BlockSpec(memory_space=pltpu.VMEM)
    token_spec = pl.BlockSpec((1, count, width), lambda b: (b, 0, 0))

    side = lax.axis_index("req") % 2
    tp_place = lax.axis_index("tp")

    def part(which):
        start = (which * tp_count + tp_place) * segment
        return lax.dynamic_slice_in_dim(stored[0], start, segment, 1)

    own_part, other_part = part(side), part(1 - side)
    partner_part = permuted(other_part, "req", 1)
    q = pl.pallas_call(
        functools.partial(query_kernel, req_dev, q_chunk),
        grid=(req_dev,),
        out_shape=jax.ShapeDtypeStruct((n_req, req_dev, q_chunk, LANES), BF16),
        in_specs=[
            SMEM,
            SMEM,
            token_spec,
            full((1, width)),
            full(w_query_rows.shape),
            full((1, head_dim)),
            table_spec,
        ],
        out_specs=pl.BlockSpec((n_req, 1, q_chunk, LANES), lambda b: (0, b, 0, 0)),
        compiler_params=params(60),
        cost_estimate=cost(2 * req_dev * count * width * 384, 6 << 20),
        name="query",
    )(continuing, cache_len, tokens, gain_row, w_query_rows, q_gain_row, table)
    q_mid = exchanged(q).reshape(requests, q_chunk, LANES)

    partner_part = lax.optimization_barrier((partner_part, q))[0]
    both = jnp.stack([own_part, partner_part])
    planes = n_req // 2
    hops = planes == 4

    def crossed(value, pairs):
        pairs = [(2 * a + parity, 2 * b + parity) for a, b in pairs for parity in range(2)]
        return lax.ppermute(value, "req", pairs)

    if hops:
        outer = [(z, z ^ 1) for z in range(planes)]
        beside = crossed(both, outer)
        middle = crossed(both, [(1, 2), (2, 1)])
        far_middle = crossed(beside, [(1, 2), (2, 1)])
        outward = crossed(middle, [(1, 0), (2, 3)])
        far_outward = crossed(far_middle, [(1, 0), (2, 3)])
        blocks = [both, beside, middle, far_middle, outward, far_outward]
    else:
        column = [list(range(parity, n_req, 2)) for parity in range(2)]
        blocks = [lax.all_gather(both, "req", axis_index_groups=column)]
        beside = middle = far_middle = outward = both

    w_x = permuted(w_out, "tp", tp_count // 2)
    w_c = permuted(w_out, "tp", 1)
    w_xc = permuted(w_x, "tp", 1)

    fresh = pl.pallas_call(
        functools.partial(fresh_kernel, req_dev),
        grid=(req_dev,),
        out_shape=jax.ShapeDtypeStruct((req_dev, kv_heads, count, LANES), BF16),
        in_specs=[
            SMEM,
            token_spec,
            full((1, width)),
            full(key_value_weight.shape),
            full((1, head_dim)),
            table_spec,
            any_spec,
        ],
        out_specs=pl.BlockSpec((1, kv_heads, count, LANES), lambda b: (b, 0, 0, 0)),
        compiler_params=params(),
        cost_estimate=HINT,
        name="fresh",
    )(meta, tokens, gain_row, key_value_weight, k_gain_row, table, q)

    q_out = pl.pallas_call(
        functools.partial(route_query_kernel, requests),
        out_shape=jax.ShapeDtypeStruct((n_req, q_chunk, LANES), BF16),
        in_specs=[SMEM, vmem_spec],
        out_specs=vmem_spec,
        compiler_params=params(),
        cost_estimate=cost(0, 1 << 20),
        name="route_query",
    )(meta, q_mid)
    q_row = lax.optimization_barrier((exchanged(q_out), beside, middle, fresh))[0]
    fresh_partner = permuted(fresh, "req", 1)

    near = pl.pallas_call(
        functools.partial(local_kernel, groups),
        grid=(req_dev,),
        out_shape=jax.ShapeDtypeStruct((req_dev, 3, count, LANES), F32),
        in_specs=[
            pl.BlockSpec((n_req, 1, q_chunk, LANES), lambda b: (0, b, 0, 0)),
            pl.BlockSpec((1, kv_heads, count, LANES), lambda b: (b, 0, 0, 0)),
        ],
        out_specs=pl.BlockSpec((1, 3, count, LANES), lambda b: (b, 0, 0, 0)),
        compiler_params=params(),
        cost_estimate=HINT,
        name="attend_new",
    )(q, fresh)

    far = pl.pallas_call(
        functools.partial(row_kernel, requests, groups, o_chunk),
        grid=(heads,),
        out_shape=jax.ShapeDtypeStruct((n_req, o_chunk, LANES), BF16),
        in_specs=[SMEM, full((n_req, q_chunk, LANES)), any_spec],
        out_specs=full((n_req, o_chunk, LANES)),
        scratch_shapes=[
            pltpu.VMEM((heads, count, LANES), BF16),
            pltpu.VMEM((heads, count, LANES), F32),
            pltpu.VMEM((count, LANES), F32),
            pltpu.VMEM((2, span, LANES), BF16),
            pltpu.VMEM((8, span), F32),
            pltpu.SemaphoreType.DMA((2,)),
        ],
        compiler_params=params(60),
        cost_estimate=cost(4 * heads * count * span * 256, 32 << 20),
        name="attend_row",
    )(meta, q_row, stored)

    far_mid = exchanged(far)
    far_out = pl.pallas_call(
        functools.partial(route_result_kernel, requests),
        out_shape=jax.ShapeDtypeStruct((requests, o_chunk, LANES), BF16),
        in_specs=[SMEM, vmem_spec],
        out_specs=vmem_spec,
        compiler_params=params(),
        cost_estimate=cost(0, 1 << 20),
        name="route_result",
    )(meta, far_mid)
    far_home = exchanged(far_out.reshape(n_req, req_dev, o_chunk, LANES))
    far_home = lax.optimization_barrier((far_home, far_middle, outward))[0]

    mixed = pl.pallas_call(
        functools.partial(merge_kernel, req_dev),
        grid=(req_dev,),
        out_shape=jax.ShapeDtypeStruct((req_dev, q_rows, LANES), BF16),
        in_specs=[
            SMEM,
            pl.BlockSpec((n_req, 1, o_chunk, LANES), lambda b: (0, b, 0, 0)),
            pl.BlockSpec((1, 3, count, LANES), lambda b: (b, 0, 0, 0)),
        ],
        out_specs=pl.BlockSpec((1, q_rows, LANES), lambda b: (b, 0, 0)),
        compiler_params=params(),
        cost_estimate=HINT,
        name="merge",
    )(meta, far_home, near)

    m_x = permuted(mixed, "tp", tp_count // 2)
    m_c = permuted(mixed, "tp", 1)

    block = 512
    t_spec = pl.BlockSpec((req_dev, count, block), lambda n: (0, 0, n))

    def project(m_a, m_b, w_a, w_b, base, dtype, name):
        m_spec = full((req_dev, q_rows, LANES))
        w_spec = pl.BlockSpec((heads * head_dim, block), lambda n: (0, n))
        return pl.pallas_call(
            project_kernel,
            grid=(width // block,),
            out_shape=jax.ShapeDtypeStruct(tokens.shape, dtype),
            in_specs=[m_spec] * 2 + [w_spec] * 2 + [t_spec],
            out_specs=t_spec,
            scratch_shapes=[pltpu.VMEM((req_dev * count, 640), BF16)],
            compiler_params=params(),
            cost_estimate=cost(2 * req_dev * count * width * 640, 6 << 20),
            name=name,
        )(m_a, m_b, w_a, w_b, base)

    partial = project(mixed, m_c, w_out, w_c, tokens, F32, "project_chip")
    new_spec = pl.BlockSpec((1, kv_heads, count, LANES), lambda l: (l % req_dev, 0, 0, 0))
    cache = pl.pallas_call(
        functools.partial(cache_kernel, req_dev, span),
        grid=(2 * req_dev,),
        in_specs=[SMEM] + [any_spec] * len(blocks) + [new_spec, new_spec, any_spec],
        out_specs=pl.BlockSpec((1, kv_heads, segment, LANES), lambda l: (l, 0, 0, 0)),
        scratch_shapes=[
            pltpu.VMEM((kv_heads, 2 * segment + count, LANES), F32),
            pltpu.VMEM((2 * req_dev, kv_heads, 2 * segment, LANES), BF16),
            pltpu.SemaphoreType.DMA((2 * req_dev,)),
        ],
        out_shape=jax.ShapeDtypeStruct((2 * req_dev, kv_heads, segment, LANES), BF16),
        compiler_params=params(),
        cost_estimate=HINT,
        name="cache",
    )(meta, *blocks, fresh, fresh_partner, partial)
    m_x = lax.optimization_barrier((m_x, partial, cache))[0]
    m_xc = permuted(m_x, "tp", 1)
    layer = project(m_x, m_xc, w_x, w_xc, partial, BF16, "project_rest")

    return (layer, cache)


def solution(mesh):
    return jax.shard_map(
        on_device,
        mesh=mesh,
        in_specs=(
            P("req", None, None),
            P(),
            P(None, "tp"),
            P(),
            P("tp", None),
            P(),
            P(),
            P("req", None, None, None),
            P(),
            P(),
            P(),
        ),
        out_specs=(P("req", None, None), P("req", None, "tp", None)),
        check_vma=False,
    )
```

time: 148 us -> 117 us (0.79)
  blocking collectives: 27.8 us -> 0 us
  between operations: 14.4 us -> 0.94 us
  starting transfers between devices: 18.5 us -> 31.9 us
  local copies, waits for them, and re-layouts: 15.5 us -> 5.81 us
  Pallas kernels: 34.4 us -> 39.2 us
    all_to_all x2 -> x0, blocking collectives: 27.8 us -> none  [exchanged(): return lax.all_to_all(value, 'req', split_axis=0, concat_axis=0, tiled=True)]
    ppermute x8, waiting for transfers between devices: 16.7 us -> 1.67 us  [permuted(): return lax.ppermute(value, axis, pairs)]
    ppermute x0 -> x5, waiting for transfers between devices: none -> 12.6 us  [crossed(): return lax.ppermute(value, 'req', pairs)]
    unnamed x63 -> x28, local copies, waits for them, and re-layouts: 14.8 us -> 3.79 us
    ppermute x0 -> x5, starting transfers between devices: none -> 7.69 us  [crossed(): return lax.ppermute(value, 'req', pairs)]
    pallas_call x6, Pallas kernels: 19.4 us -> 25.8 us  [the longest x2 9.31 us: project(): pl.pallas_call(project_kernel, grid=(width // block,), out_shape=jax.Shap...]
    all_to_all x2 -> x4, starting transfers between devices: 10.1 us -> 16 us  [exchanged(): return lax.all_to_all(value, 'req', split_axis=0, concat_axis=0, tiled=True)]
    all_to_all x2 -> x4, waiting for transfers between devices: 19.2 us -> 22.3 us  [exchanged(): return lax.all_to_all(value, 'req', split_axis=0, concat_axis=0, tiled=True)]
  transfers between devices with their start and end apart: 11 -> 17, of which waited for: 4 -> 8; matrix products, arithmetic and copies ran while one was open for 1% -> 2% of each run, Pallas kernels for 21% -> 29%
where the time goes in v2:
time: 117 us; the launch traced here: 116 us
  Pallas kernels  39.2 us (34%)
  waiting for transfers between devices  36.5 us (31%)
  starting transfers between devices  31.9 us (27%)
  local copies, waits for them, and re-layouts  5.81 us (5%)
  other arithmetic  2.04 us (2%)
    all_to_all x4, waiting for transfers between devices, exchanged(): return lax.all_to_all(value, 'req', split_axis=0, concat_axis=0, tiled=True)  22.3 us
    all_to_all x4, starting transfers between devices, exchanged(): return lax.all_to_all(value, 'req', split_axis=0, concat_axis=0, tiled=True)  16 us
    ppermute x5, waiting for transfers between devices, crossed(): return lax.ppermute(value, 'req', pairs)  12.6 us
    pallas_call x2, Pallas kernels, project(): pl.pallas_call(project_kernel, grid=(width // block,), out_shape=jax.Shap...  9.31 us
    pallas_call x1, Pallas kernels, on_device(): pl.pallas_call(functools.partial(row_kernel, requests, groups, o_chunk),...  8.7 us
    ppermute x8, starting transfers between devices, permuted(): return lax.ppermute(value, axis, pairs)  8.21 us
    ppermute x5, starting transfers between devices, crossed(): return lax.ppermute(value, 'req', pairs)  7.69 us
    pallas_call x1, Pallas kernels, on_device(): pl.pallas_call(functools.partial(query_kernel, req_dev, q_chunk), grid=(r...  5.12 us
  transfers between devices with their start and end apart: 17, of which 8 were waited for; matrix products, arithmetic and copies ran while one was open for 2% of the time, Pallas kernels for 29%

profile of v2, /device:TPU:0, one launch (start us, length us, event | category | flops | bytes accessed | tf_op | source)
XLA Modules:
  0.0 116.4 jit_solution(2419534950807648856)
XLA Ops:
  0.7 2.0 %constant_dynamic-slice_fusion = (bf16[1,5,288,128]{3,2,1,0:T(8,128)(2,1)}, bf16[5,288,128]{2,1,0:T(8,128)(2,1)}) fusion(bf16[1,5,2048,128]{3,2,1,0:T(8,128)(2,1)} %stored.1, s32[]{:T(128)S(6)} %select_n.14, s32[]{:T(128)S(6)} %select_n.15), kind=kLoop, calls=%fused_computation.3 | loop fusion | bytes 1474568 | tf_op jit(solution)/shard_map/dynamic_slice | solution.py:439
  2.7 3.0 %collective-permute-start = (bf16[5,288,128]{2,1,0:T(8,128)(2,1)}, bf16[5,288,128]{2,1,0:T(8,128)(2,1)}, u32[]{:S(2)}, u32[]{:S(2)}) collective-permute-start(bf16[5,288,128]{2,1,0:T(8,128)(2,1)} %get-tuple-element.11), channel_id=1, source_target_pairs={{0,4},{4,0},{8,12},{12,8},{16,20},{20,16},{24,28},{28,24},{1,5},{5... | collective-permute-start | bytes 1105928 | tf_op jit(solution)/shard_map/ppermute | solution.py:382
  5.6 5.1 %query.1.after.q = bf16[8,2,80,128]{3,2,1,0:T(8,128)(2,1)} custom-call(s32[16]{0:T(128)} %cont.1, s32[16]{0:T(128)} %clen.1, bf16[2,256,2048]{2,1,0:T(8,128)(2,1)} %base.1, f32[1,2048]{1,0:T(1,128)} %bitcast.13, bf16[320,2048]{1,0:T(8,128)(2,1)} %bitcast.16, f32[1,64]{1,0:T(1,128)} %bitcast.19, f32[2,408,128]{2,1,0:T(8,128)} %constant.34.clone.table), custom_call_target="tpu_custom_call" | custom-call | flops 805306368 | bytes 6291456 | tf_op jit(solution)/shard_map/query/pallas_call | solution.py:443
  10.8 5.2 %all-to-all-start = ((bf16[8,2,80,128]{3,2,1,0:T(8,128)(2,1)}), bf16[8,2,80,128]{3,2,1,0:T(8,128)(2,1)S(1)}, u32[]{:S(2)}, u32[]{:S(2)}) async-start(bf16[8,2,80,128]{3,2,1,0:T(8,128)(2,1)} %query.1.after.q), calls=%async_computation | async-start | bytes 655360 | tf_op jit(solution)/shard_map/all_to_all | solution.py:386
  16.0 2.0 %pad_maximum_fusion.refs_0_ = bf16[2,5,288,128]{3,2,1,0:T(8,128)(2,1)} fusion(bf16[1,5,288,128]{3,2,1,0:T(8,128)(2,1)} %bitcast.8, bf16[1,5,288,128]{3,2,1,0:T(8,128)(2,1)} %get-tuple-element.10), kind=kLoop, calls=%fused_computation | loop fusion | flops 368640 | bytes 1474560 | tf_op jit(solution)/shard_map/stack | solution.py:464
  18.0 2.0 %collective-permute-start.1 = (bf16[2,5,288,128]{3,2,1,0:T(8,128)(2,1)}, bf16[2,5,288,128]{3,2,1,0:T(8,128)(2,1)}, u32[]{:S(2)}, u32[]{:S(2)}) collective-permute-start(bf16[2,5,288,128]{3,2,1,0:T(8,128)(2,1)} %pad_maximum_fusion.refs_0_), channel_id=1, source_target_pairs={{0,8},{4,12},{8,0},{12,4},{16,24},{20,28},{24,16},{28,20},{1,9},{5... | collective-permute-start | bytes 2211848 | tf_op jit(solution)/shard_map/ppermute | solution.py:470
  20.0 1.6 %collective-permute-start.2 = (bf16[2,5,288,128]{3,2,1,0:T(8,128)(2,1)}, bf16[2,5,288,128]{3,2,1,0:T(8,128)(2,1)}, u32[]{:S(2)}, u32[]{:S(2)}) collective-permute-start(bf16[2,5,288,128]{3,2,1,0:T(8,128)(2,1)} %pad_maximum_fusion.refs_0_), channel_id=1, source_target_pairs={{8,16},{12,20},{16,8},{20,12},{9,17},{13,21},{17,9},{21,13},{10,18... | collective-permute-start | bytes 2211848 | tf_op jit(solution)/shard_map/ppermute | solution.py:470
  21.6 1.5 %collective-permute-start.11 = (bf16[320,2048]{1,0:T(8,128)(2,1)}, bf16[320,2048]{1,0:T(8,128)(2,1)}, u32[]{:S(2)}, u32[]{:S(2)}) collective-permute-start(bf16[320,2048]{1,0:T(8,128)(2,1)} %w_a.1), channel_id=1, source_target_pairs={{0,2},{1,3},{2,0},{3,1},{4,6},{5,7},{6,4},{7,5},{8,10},{9,11},{10,... | collective-permute-start | bytes 3932168 | tf_op jit(solution)/shard_map/ppermute | solution.py:382
  23.1 3.8 %all-to-all-done = bf16[8,2,80,128]{3,2,1,0:T(8,128)(2,1)S(1)} async-done(((bf16[8,2,80,128]{3,2,1,0:T(8,128)(2,1)}), bf16[8,2,80,128]{3,2,1,0:T(8,128)(2,1)S(1)}, u32[]{:S(2)}, u32[]{:S(2)}) %all-to-all-start) | async-done | bytes 327712 | tf_op jit(solution)/shard_map/all_to_all | solution.py:386
  26.9 1.4 %route_query.1 = bf16[8,80,128]{2,1,0:T(8,128)(2,1)} custom-call(s32[3,16]{1,0:T(4,128)S(1)} %pad_add_fusion.meta, bf16[16,80,128]{2,1,0:T(8,128)(2,1)S(1)} %bitcast.12), custom_call_target="tpu_custom_call" | custom-call | bytes 1048576 | tf_op jit(solution)/shard_map/route_query/pallas_call | solution.py:508
  28.3 4.0 %all-to-all-start.1 = ((bf16[8,80,128]{2,1,0:T(8,128)(2,1)}), bf16[8,80,128]{2,1,0:T(8,128)(2,1)}, u32[]{:S(2)}, u32[]{:S(2)}) async-start(bf16[8,80,128]{2,1,0:T(8,128)(2,1)} %route_query.1), calls=%async_computation.1 | async-start | bytes 327680 | tf_op jit(solution)/shard_map/all_to_all | solution.py:386
  32.4 1.7 %copy-done.4 = bf16[2048,640]{1,0:T(8,128)(2,1)S(1)} copy-done((bf16[2048,640]{1,0:T(8,128)(2,1)S(1)}, bf16[2048,640]{1,0:T(8,128)(2,1)}, u32[]{:S(2)}) %copy-start.4) | copy-done | bytes 2621464
  34.2 3.9 %fresh.1.refs_6_ = bf16[2,5,256,128]{3,2,1,0:T(8,128)(2,1)S(1)} custom-call(s32[3,16]{1,0:T(4,128)S(1)} %pad_add_fusion.meta, bf16[2,256,2048]{2,1,0:T(8,128)(2,1)S(1)} %copy-done, f32[1,2048]{1,0:T(1,128)S(1)} %bitcast.14, bf16[2048,640]{1,0:T(8,128)(2,1)S(1)} %copy-done.4, f32[1,64]{1,0:T(1,128)S(1)} %bitcast.15, f32[2,408,128]{2,1,0:T(8,128)S(1)} %copy-done.5, ...), custom_call_target="tpu_custom_call" | custom-call | bytes 1024 | tf_op jit(solution)/shard_map/fresh/pallas_call | solution.py:489
  38.1 7.5 %all-to-all-done.1.q = bf16[8,80,128]{2,1,0:T(8,128)(2,1)} async-done(((bf16[8,80,128]{2,1,0:T(8,128)(2,1)}), bf16[8,80,128]{2,1,0:T(8,128)(2,1)}, u32[]{:S(2)}, u32[]{:S(2)}) %all-to-all-start.1) | async-done | bytes 163872 | tf_op jit(solution)/shard_map/all_to_all | solution.py:386
  45.6 8.7 %attend_row.1 = bf16[8,96,128]{2,1,0:T(8,128)(2,1)} custom-call(s32[3,16]{1,0:T(4,128)} %copy-done.7, bf16[8,80,128]{2,1,0:T(8,128)(2,1)} %all-to-all-done.1.q, bf16[1,5,2048,128]{3,2,1,0:T(8,128)(2,1)} %stored.1), custom_call_target="tpu_custom_call" | custom-call | flops 2684354560 | bytes 33554432 | tf_op jit(solution)/shard_map/attend_row/pallas_call | solution.py:534
  54.3 3.4 %all-to-all-start.2 = ((bf16[8,96,128]{2,1,0:T(8,128)(2,1)}), bf16[8,96,128]{2,1,0:T(8,128)(2,1)S(1)}, u32[]{:S(2)}, u32[]{:S(2)}) async-start(bf16[8,96,128]{2,1,0:T(8,128)(2,1)} %attend_row.1), calls=%async_computation.2 | async-start | bytes 393216 | tf_op jit(solution)/shard_map/all_to_all | solution.py:386
  57.8 1.5 %collective-permute-start.3 = (bf16[2,5,288,128]{3,2,1,0:T(8,128)(2,1)}, bf16[2,5,288,128]{3,2,1,0:T(8,128)(2,1)}, u32[]{:S(2)}, u32[]{:S(2)}) collective-permute-start(bf16[2,5,288,128]{3,2,1,0:T(8,128)(2,1)} %collective-permute-done.1.refs_1_), channel_id=1, source_target_pairs={{8,16},{12,20},{16,8},{20,12},{9,17},{13,21},{17,9},{21,13},{10,18... | collective-permute-start | bytes 2211848 | tf_op jit(solution)/shard_map/ppermute | solution.py:470
  60.6 5.5 %all-to-all-done.2.src = bf16[8,96,128]{2,1,0:T(8,128)(2,1)S(1)} async-done(((bf16[8,96,128]{2,1,0:T(8,128)(2,1)}), bf16[8,96,128]{2,1,0:T(8,128)(2,1)S(1)}, u32[]{:S(2)}, u32[]{:S(2)}) %all-to-all-start.2) | async-done | bytes 196640 | tf_op jit(solution)/shard_map/all_to_all | solution.py:386
  66.1 1.4 %route_result.1 = bf16[16,96,128]{2,1,0:T(8,128)(2,1)} custom-call(s32[3,16]{1,0:T(4,128)S(1)} %copy-done.8, bf16[8,96,128]{2,1,0:T(8,128)(2,1)S(1)} %all-to-all-done.2.src), custom_call_target="tpu_custom_call" | custom-call | bytes 1048576 | tf_op jit(solution)/shard_map/route_result/pallas_call | solution.py:554
  67.5 3.5 %all-to-all-start.3 = ((bf16[8,2,96,128]{3,2,1,0:T(8,128)(2,1)}), bf16[8,2,96,128]{3,2,1,0:T(8,128)(2,1)S(1)}, u32[]{:S(2)}, u32[]{:S(2)}) async-start(bf16[8,2,96,128]{3,2,1,0:T(8,128)(2,1)} %bitcast.10), calls=%async_computation.3 | async-start | bytes 786432 | tf_op jit(solution)/shard_map/all_to_all | solution.py:386
  71.0 1.3 %collective-permute-start.8 = (bf16[2,5,288,128]{3,2,1,0:T(8,128)(2,1)}, bf16[2,5,288,128]{3,2,1,0:T(8,128)(2,1)}, u32[]{:S(2)}, u32[]{:S(2)}) collective-permute-start(bf16[2,5,288,128]{3,2,1,0:T(8,128)(2,1)} %collective-permute-done.3.refs_3_), channel_id=1, source_target_pairs={{8,0},{12,4},{16,24},{20,28},{9,1},{13,5},{17,25},{21,29},{10,2},{... | collective-permute-start | bytes 2211848 | tf_op jit(solution)/shard_map/ppermute | solution.py:470
  72.3 1.9 %collective-permute-start.9 = (bf16[2,5,256,128]{3,2,1,0:T(8,128)(2,1)S(1)}, bf16[2,5,256,128]{3,2,1,0:T(8,128)(2,1)}, u32[]{:S(2)}, u32[]{:S(2)}) collective-permute-start(bf16[2,5,256,128]{3,2,1,0:T(8,128)(2,1)S(1)} %fresh.1.refs_6_), channel_id=1, source_target_pairs={{0,4},{4,0},{8,12},{12,8},{16,20},{20,16},{24,28},{28,24},{1,5},{5... | collective-permute-start | bytes 1966088 | tf_op jit(solution)/shard_map/ppermute | solution.py:382
  74.2 2.8 %attend_new.1.near = f32[2,3,256,128]{3,2,1,0:T(8,128)S(1)} custom-call(bf16[8,2,80,128]{3,2,1,0:T(8,128)(2,1)S(1)} %copy-done.1, bf16[2,5,256,128]{3,2,1,0:T(8,128)(2,1)S(1)} %fresh.1.refs_6_), custom_call_target="tpu_custom_call" | custom-call | bytes 1024 | tf_op jit(solution)/shard_map/attend_new/pallas_call | solution.py:520
  78.0 5.9 %collective-permute-done.4.refs_4_ = bf16[2,5,288,128]{3,2,1,0:T(8,128)(2,1)} collective-permute-done((bf16[2,5,288,128]{3,2,1,0:T(8,128)(2,1)}, bf16[2,5,288,128]{3,2,1,0:T(8,128)(2,1)}, u32[]{:S(2)}, u32[]{:S(2)}) %collective-permute-start.4) | collective-permute-done | bytes 737312 | tf_op jit(solution)/shard_map/ppermute | solution.py:470
  83.8 5.5 %all-to-all-done.3.far = bf16[8,2,96,128]{3,2,1,0:T(8,128)(2,1)S(1)} async-done(((bf16[8,2,96,128]{3,2,1,0:T(8,128)(2,1)}), bf16[8,2,96,128]{3,2,1,0:T(8,128)(2,1)S(1)}, u32[]{:S(2)}, u32[]{:S(2)}) %all-to-all-start.3) | async-done | bytes 393248 | tf_op jit(solution)/shard_map/all_to_all | solution.py:386
  90.5 1.5 %merge.1.m_a = bf16[2,640,128]{2,1,0:T(8,128)(2,1)S(1)} custom-call(s32[3,16]{1,0:T(4,128)S(1)} %copy-done.8, bf16[8,2,96,128]{3,2,1,0:T(8,128)(2,1)S(1)} %all-to-all-done.3.far, f32[2,3,256,128]{3,2,1,0:T(8,128)S(1)} %copy-done.3), custom_call_target="tpu_custom_call" | custom-call | bytes 1024 | tf_op jit(solution)/shard_map/merge/pallas_call | solution.py:566
  92.1 1.6 %collective-permute-start.5 = (bf16[2,640,128]{2,1,0:T(8,128)(2,1)S(1)}, bf16[2,640,128]{2,1,0:T(8,128)(2,1)S(1)}, u32[]{:S(2)}, u32[]{:S(2)}) collective-permute-start(bf16[2,640,128]{2,1,0:T(8,128)(2,1)S(1)} %merge.1.m_a), channel_id=1, source_target_pairs={{0,2},{1,3},{2,0},{3,1},{4,6},{5,7},{6,4},{7,5},{8,10},{9,11},{10,... | collective-permute-start | bytes 983048 | tf_op jit(solution)/shard_map/ppermute | solution.py:382
  93.7 4.2 %project_chip.1.refs_8_.base = f32[2,256,2048]{2,1,0:T(8,128)S(1)} custom-call(bf16[2,640,128]{2,1,0:T(8,128)(2,1)S(1)} %merge.1.m_a, bf16[2,640,128]{2,1,0:T(8,128)(2,1)S(1)} %collective-permute-done.6.m_b, bf16[320,2048]{1,0:T(8,128)(2,1)S(1)} %copy-done.6, bf16[320,2048]{1,0:T(8,128)(2,1)} %collective-permute-done.7.w_b, bf16[2,256,2048]{2,1,0:T(8,128)(2,1)S(1)} %copy-done), custom_call_target="tpu_custom_call" | custom-call | flops 1342177280 | bytes 6291456 | tf_op jit(solution)/shard_map/project_chip/pallas_call | solution.py:590
  97.9 6.7 %collective-permute-done.8.refs_5_ = bf16[2,5,288,128]{3,2,1,0:T(8,128)(2,1)} collective-permute-done((bf16[2,5,288,128]{3,2,1,0:T(8,128)(2,1)}, bf16[2,5,288,128]{3,2,1,0:T(8,128)(2,1)}, u32[]{:S(2)}, u32[]{:S(2)}) %collective-permute-start.8) | collective-permute-done | bytes 737312 | tf_op jit(solution)/shard_map/ppermute | solution.py:470
  104.6 5.0 %cache.1 = bf16[4,5,288,128]{3,2,1,0:T(8,128)(2,1)} custom-call(s32[3,16]{1,0:T(4,128)S(1)} %copy-done.8, bf16[2,5,288,128]{3,2,1,0:T(8,128)(2,1)} %pad_maximum_fusion.refs_0_, bf16[2,5,288,128]{3,2,1,0:T(8,128)(2,1)} %collective-permute-done.1.refs_1_, bf16[2,5,288,128]{3,2,1,0:T(8,128)(2,1)} %collective-permute-done.2.refs_2_, ...), custom_call_target="tpu_custom_call" | custom-call | bytes 1024 | tf_op jit(solution)/shard_map/cache/pallas_call | solution.py:604
  109.7 1.6 %collective-permute-done.10.m_b = bf16[2,640,128]{2,1,0:T(8,128)(2,1)S(1)} collective-permute-done((bf16[2,640,128]{2,1,0:T(8,128)(2,1)S(1)}, bf16[2,640,128]{2,1,0:T(8,128)(2,1)S(1)}, u32[]{:S(2)}, u32[]{:S(2)}) %collective-permute-start.10) | collective-permute-done | bytes 327712 | tf_op jit(solution)/shard_map/ppermute | solution.py:382
  111.3 5.2 %project_rest.1 = bf16[2,256,2048]{2,1,0:T(8,128)(2,1)} custom-call(bf16[2,640,128]{2,1,0:T(8,128)(2,1)S(1)} %collective-permute-done.5.m_a, bf16[2,640,128]{2,1,0:T(8,128)(2,1)S(1)} %collective-permute-done.10.m_b, bf16[320,2048]{1,0:T(8,128)(2,1)} %collective-permute-done.11.w_a, bf16[320,2048]{1,0:T(8,128)(2,1)} %collective-permute-done.12.w_b, ...), custom_call_target="tpu_custom_call" | custom-call | flops 1342177280 | bytes 6291456 | tf_op jit(solution)/shard_map/project_rest/pallas_call | solution.py:590
  (43 shorter events, 3.7 us)
Async XLA Ops:
  2.7 13.3 %collective-permute-start = (bf16[5,288,128]{2,1,0:T(8,128)(2,1)}, bf16[5,288,128]{2,1,0:T(8,128)(2,1)}, u32[]{:S(2)}, u32[]{:S(2)}) collective-permute-start(bf16[5,288,128]{2,1,0:T(8,128)(2,1)} %get-tuple-element.11), channel_id=1, source_target_pairs={{0,4},{4,0},{8,12},{12,8},{16,20},{20,16},{24,28},{28,24},{1,5},{5... | collective-permute-start | bytes 1105928 | tf_op jit(solution)/shard_map/ppermute | solution.py:382
  5.6 17.4 %copy-start.11 = (s32[16]{0:T(128)S(1)}, s32[16]{0:T(128)}, u32[]{:S(2)}) copy-start(s32[16]{0:T(128)} %clen.1) | copy-start | bytes 196
  5.6 17.4 %copy-start.12 = (s32[16]{0:T(128)S(1)}, s32[16]{0:T(128)}, u32[]{:S(2)}) copy-start(s32[16]{0:T(128)} %cont.1) | copy-start | bytes 196
  5.6 17.4 %copy-start.13 = (s32[16]{0:T(128)S(1)}, s32[16]{0:T(128)}, u32[]{:S(2)}) copy-start(s32[16]{0:T(128)} %param.21) | copy-start | bytes 196
  10.8 21.6 %copy-start = (bf16[2,256,2048]{2,1,0:T(8,128)(2,1)S(1)}, bf16[2,256,2048]{2,1,0:T(8,128)(2,1)}, u32[]{:S(2)}) copy-start(bf16[2,256,2048]{2,1,0:T(8,128)(2,1)} %base.1) | copy-start | bytes 6291460
  10.8 21.6 %copy-start.1 = (bf16[8,2,80,128]{3,2,1,0:T(8,128)(2,1)S(1)}, bf16[8,2,80,128]{3,2,1,0:T(8,128)(2,1)}, u32[]{:S(2)}) copy-start(bf16[8,2,80,128]{3,2,1,0:T(8,128)(2,1)} %query.1.after.q) | copy-start | bytes 983044
  10.8 21.6 %copy-start.5 = (f32[2,408,128]{2,1,0:T(8,128)S(1)}, f32[2,408,128]{2,1,0:T(8,128)}, u32[]{:S(2)}) copy-start(f32[2,408,128]{2,1,0:T(8,128)} %constant.34.clone.table) | copy-start | bytes 1253380
  10.8 21.6 %copy-start.9 = (f32[2048]{0:T(1024)S(1)}, f32[2048]{0:T(1024)}, u32[]{:S(2)}) copy-start(f32[2048]{0:T(1024)} %param.13) | copy-start | bytes 24580
  10.8 21.6 %copy-start.10 = (f32[64]{0:T(128)S(1)}, f32[64]{0:T(128)}, u32[]{:S(2)}) copy-start(f32[64]{0:T(128)} %param.18) | copy-start | bytes 772
  10.8 16.1 %all-to-all-start = ((bf16[8,2,80,128]{3,2,1,0:T(8,128)(2,1)}), bf16[8,2,80,128]{3,2,1,0:T(8,128)(2,1)S(1)}, u32[]{:S(2)}, u32[]{:S(2)}) async-start(bf16[8,2,80,128]{3,2,1,0:T(8,128)(2,1)} %query.1.after.q), calls=%async_computation | async-start | bytes 655360 | tf_op jit(solution)/shard_map/all_to_all | solution.py:386
  18.0 27.6 %collective-permute-start.1 = (bf16[2,5,288,128]{3,2,1,0:T(8,128)(2,1)}, bf16[2,5,288,128]{3,2,1,0:T(8,128)(2,1)}, u32[]{:S(2)}, u32[]{:S(2)}) collective-permute-start(bf16[2,5,288,128]{3,2,1,0:T(8,128)(2,1)} %pad_maximum_fusion.refs_0_), channel_id=1, source_target_pairs={{0,8},{4,12},{8,0},{12,4},{16,24},{20,28},{24,16},{28,20},{1,9},{5... | collective-permute-start | bytes 2211848 | tf_op jit(solution)/shard_map/ppermute | solution.py:470
  20.0 25.6 %collective-permute-start.2 = (bf16[2,5,288,128]{3,2,1,0:T(8,128)(2,1)}, bf16[2,5,288,128]{3,2,1,0:T(8,128)(2,1)}, u32[]{:S(2)}, u32[]{:S(2)}) collective-permute-start(bf16[2,5,288,128]{3,2,1,0:T(8,128)(2,1)} %pad_maximum_fusion.refs_0_), channel_id=1, source_target_pairs={{8,16},{12,20},{16,8},{20,12},{9,17},{13,21},{17,9},{21,13},{10,18... | collective-permute-start | bytes 2211848 | tf_op jit(solution)/shard_map/ppermute | solution.py:470
  21.6 49.4 %collective-permute-start.11 = (bf16[320,2048]{1,0:T(8,128)(2,1)}, bf16[320,2048]{1,0:T(8,128)(2,1)}, u32[]{:S(2)}, u32[]{:S(2)}) collective-permute-start(bf16[320,2048]{1,0:T(8,128)(2,1)} %w_a.1), channel_id=1, source_target_pairs={{0,2},{1,3},{2,0},{3,1},{4,6},{5,7},{6,4},{7,5},{8,10},{9,11},{10,... | collective-permute-start | bytes 3932168 | tf_op jit(solution)/shard_map/ppermute | solution.py:382
  23.1 15.0 %copy-start.7 = (s32[3,16]{1,0:T(4,128)}, s32[3,16]{1,0:T(4,128)S(1)}, u32[]{:S(2)}) copy-start(s32[3,16]{1,0:T(4,128)S(1)} %pad_add_fusion.meta) | copy-start | bytes 580
  28.3 17.3 %all-to-all-start.1 = ((bf16[8,80,128]{2,1,0:T(8,128)(2,1)}), bf16[8,80,128]{2,1,0:T(8,128)(2,1)}, u32[]{:S(2)}, u32[]{:S(2)}) async-start(bf16[8,80,128]{2,1,0:T(8,128)(2,1)} %route_query.1), calls=%async_computation.1 | async-start | bytes 327680 | tf_op jit(solution)/shard_map/all_to_all | solution.py:386
  32.3 59.8 %collective-permute-start.7 = (bf16[320,2048]{1,0:T(8,128)(2,1)}, bf16[320,2048]{1,0:T(8,128)(2,1)}, u32[]{:S(2)}, u32[]{:S(2)}) collective-permute-start(bf16[320,2048]{1,0:T(8,128)(2,1)} %w_a.1), channel_id=1, source_target_pairs={{0,1},{1,0},{2,3},{3,2},{4,5},{5,4},{6,7},{7,6},{8,9},{9,8},{10,11... | collective-permute-start | bytes 3932168 | tf_op jit(solution)/shard_map/ppermute | solution.py:382
  32.4 1.7 %copy-start.4 = (bf16[2048,640]{1,0:T(8,128)(2,1)S(1)}, bf16[2048,640]{1,0:T(8,128)(2,1)}, u32[]{:S(2)}) copy-start(bf16[2048,640]{1,0:T(8,128)(2,1)} %w.1) | copy-start | bytes 7864324
  45.6 20.4 %copy-start.8 = (s32[3,16]{1,0:T(4,128)S(1)}, s32[3,16]{1,0:T(4,128)}, u32[]{:S(2)}) copy-start(s32[3,16]{1,0:T(4,128)} %copy-done.7) | copy-start | bytes 580
  54.3 11.7 %all-to-all-start.2 = ((bf16[8,96,128]{2,1,0:T(8,128)(2,1)}), bf16[8,96,128]{2,1,0:T(8,128)(2,1)S(1)}, u32[]{:S(2)}, u32[]{:S(2)}) async-start(bf16[8,96,128]{2,1,0:T(8,128)(2,1)} %attend_row.1), calls=%async_computation.2 | async-start | bytes 393216 | tf_op jit(solution)/shard_map/all_to_all | solution.py:386
  57.8 13.3 %collective-permute-start.3 = (bf16[2,5,288,128]{3,2,1,0:T(8,128)(2,1)}, bf16[2,5,288,128]{3,2,1,0:T(8,128)(2,1)}, u32[]{:S(2)}, u32[]{:S(2)}) collective-permute-start(bf16[2,5,288,128]{3,2,1,0:T(8,128)(2,1)} %collective-permute-done.1.refs_1_), channel_id=1, source_target_pairs={{8,16},{12,20},{16,8},{20,12},{9,17},{13,21},{17,9},{21,13},{10,18... | collective-permute-start | bytes 2211848 | tf_op jit(solution)/shard_map/ppermute | solution.py:470
  59.3 24.5 %collective-permute-start.4 = (bf16[2,5,288,128]{3,2,1,0:T(8,128)(2,1)}, bf16[2,5,288,128]{3,2,1,0:T(8,128)(2,1)}, u32[]{:S(2)}, u32[]{:S(2)}) collective-permute-start(bf16[2,5,288,128]{3,2,1,0:T(8,128)(2,1)} %collective-permute-done.2.refs_2_), channel_id=1, source_target_pairs={{8,0},{12,4},{16,24},{20,28},{9,1},{13,5},{17,25},{21,29},{10,2},{... | collective-permute-start | bytes 2211848 | tf_op jit(solution)/shard_map/ppermute | solution.py:470
  67.5 21.9 %all-to-all-start.3 = ((bf16[8,2,96,128]{3,2,1,0:T(8,128)(2,1)}), bf16[8,2,96,128]{3,2,1,0:T(8,128)(2,1)S(1)}, u32[]{:S(2)}, u32[]{:S(2)}) async-start(bf16[8,2,96,128]{3,2,1,0:T(8,128)(2,1)} %bitcast.10), calls=%async_computation.3 | async-start | bytes 786432 | tf_op jit(solution)/shard_map/all_to_all | solution.py:386
  70.9 38.7 %collective-permute-start.12 = (bf16[320,2048]{1,0:T(8,128)(2,1)}, bf16[320,2048]{1,0:T(8,128)(2,1)}, u32[]{:S(2)}, u32[]{:S(2)}) collective-permute-start(bf16[320,2048]{1,0:T(8,128)(2,1)} %collective-permute-done.11.w_a), channel_id=1, source_target_pairs={{0,1},{1,0},{2,3},{3,2},{4,5},{5,4},{6,7},{7,6},{8,9},{9,8},{10,11... | collective-permute-start | bytes 3932168 | tf_op jit(solution)/shard_map/ppermute | solution.py:382
  71.0 33.6 %collective-permute-start.8 = (bf16[2,5,288,128]{3,2,1,0:T(8,128)(2,1)}, bf16[2,5,288,128]{3,2,1,0:T(8,128)(2,1)}, u32[]{:S(2)}, u32[]{:S(2)}) collective-permute-start(bf16[2,5,288,128]{3,2,1,0:T(8,128)(2,1)} %collective-permute-done.3.refs_3_), channel_id=1, source_target_pairs={{8,0},{12,4},{16,24},{20,28},{9,1},{13,5},{17,25},{21,29},{10,2},{... | collective-permute-start | bytes 2211848 | tf_op jit(solution)/shard_map/ppermute | solution.py:470
  72.3 25.6 %collective-permute-start.9 = (bf16[2,5,256,128]{3,2,1,0:T(8,128)(2,1)S(1)}, bf16[2,5,256,128]{3,2,1,0:T(8,128)(2,1)}, u32[]{:S(2)}, u32[]{:S(2)}) collective-permute-start(bf16[2,5,256,128]{3,2,1,0:T(8,128)(2,1)S(1)} %fresh.1.refs_6_), channel_id=1, source_target_pairs={{0,4},{4,0},{8,12},{12,8},{16,20},{20,16},{24,28},{28,24},{1,5},{5... | collective-permute-start | bytes 1966088 | tf_op jit(solution)/shard_map/ppermute | solution.py:382
  77.1 0.9 copy-start.2
  89.3 1.1 copy-start.3
  90.5 3.3 %copy-start.6 = (bf16[320,2048]{1,0:T(8,128)(2,1)S(1)}, bf16[320,2048]{1,0:T(8,128)(2,1)}, u32[]{:S(2)}) copy-start(bf16[320,2048]{1,0:T(8,128)(2,1)} %w_a.1) | copy-start | bytes 3932164
  92.0 1.7 %collective-permute-start.6 = (bf16[2,640,128]{2,1,0:T(8,128)(2,1)S(1)}, bf16[2,640,128]{2,1,0:T(8,128)(2,1)S(1)}, u32[]{:S(2)}, u32[]{:S(2)}) collective-permute-start(bf16[2,640,128]{2,1,0:T(8,128)(2,1)S(1)} %merge.1.m_a), channel_id=1, source_target_pairs={{0,1},{1,0},{2,3},{3,2},{4,5},{5,4},{6,7},{7,6},{8,9},{9,8},{10,11... | collective-permute-start | bytes 983048 | tf_op jit(solution)/shard_map/ppermute | solution.py:382
  92.1 17.4 %collective-permute-start.5 = (bf16[2,640,128]{2,1,0:T(8,128)(2,1)S(1)}, bf16[2,640,128]{2,1,0:T(8,128)(2,1)S(1)}, u32[]{:S(2)}, u32[]{:S(2)}) collective-permute-start(bf16[2,640,128]{2,1,0:T(8,128)(2,1)S(1)} %merge.1.m_a), channel_id=1, source_target_pairs={{0,2},{1,3},{2,0},{3,1},{4,6},{5,7},{6,4},{7,5},{8,10},{9,11},{10,... | collective-permute-start | bytes 983048 | tf_op jit(solution)/shard_map/ppermute | solution.py:382
  109.6 1.7 %collective-permute-start.10 = (bf16[2,640,128]{2,1,0:T(8,128)(2,1)S(1)}, bf16[2,640,128]{2,1,0:T(8,128)(2,1)S(1)}, u32[]{:S(2)}, u32[]{:S(2)}) collective-permute-start(bf16[2,640,128]{2,1,0:T(8,128)(2,1)S(1)} %collective-permute-done.5.m_a), channel_id=1, source_target_pairs={{0,1},{1,0},{2,3},{3,2},{4,5},{5,4},{6,7},{7,6},{8,9},{9,8},{10,11... | collective-permute-start | bytes 983048 | tf_op jit(solution)/shard_map/ppermute | solution.py:382

commit v3 on v2

--- a/solution.py
+++ b/solution.py
@@ -209,60 +209,51 @@
     each(requests, step)
 
 
-def row_kernel(requests, groups, chunk, meta, q, stored, out, q_sc, o_sc, s_sc, kv_sc, b_sc, sem):
-    head = pl.program_id(0)
-    heads, count = q_sc.shape[:2]
+def row_kernel(requests, count, heads, groups, chunk, meta, q, stored, out, kv_sc, sem):
     span, kv_heads = kv_sc.shape[1], stored.shape[1]
-    first = lax.axis_index("tp") * heads // groups
-    which = (lax.axis_index("tp") * heads + head) // groups - first
+    offset = lax.axis_index("tp") * heads
+    first = offset // groups
 
     def fetch(number):
         source = stored.at[0, jnp.minimum(first + number, kv_heads - 1)]
         return pltpu.make_async_copy(source, kv_sc.at[number], sem.at[number])
 
-    @pl.when(head == 0)
-    def _():
-        fetch(0).start()
-        fetch(1).start()
-        row = lax.axis_index("req")
-
-        def find(r, length):
-            mine = jnp.logical_and(live(meta, r), meta[1, r] == row)
-            return jnp.where(mine, meta[2, r], length)
-
-        length = lax.fori_loop(0, requests, find, 0)
-        position = lax.broadcasted_iota(jnp.int32, (8, span), 1)
-        b_sc[...] = jnp.where(position < length, 0.0, NEG)
-        packed = q[...].reshape(-1, LANES)
-        for number, tile in enumerate(split_heads(packed, count)):
-            q_sc[number] = tile
-        s_sc[...] = jnp.zeros_like(s_sc)
-        fetch(0).wait()
-        fetch(1).wait()
-
-    kv = kv_sc[which]
-    scores = lax.dot_general(
-        q_sc[head], kv, (((1,), (1,)), ((), ())), preferred_element_type=F32
-    )
-    mixed, level = soft(scores + b_sc[0:1, :], kv)
-    o_sc[head] = mixed
-    s_sc[...] = jnp.where(lane_iota(count) == head, level, s_sc[...])
-
-    @pl.when(head == heads - 1)
-    def _():
-        lanes = lane_iota(count)
-        roll = lambda v, n: pltpu.roll(v, n, 1)
-        level = s_sc[...]
-        high = level.astype(BF16).astype(F32)
-        mid = (level - high).astype(BF16).astype(F32)
-        low = (level - high - mid).astype(BF16).astype(F32)
-        stats = roll(high, 64) + roll(mid, 64 + heads) + roll(low, 64 + 2 * heads)
-        tiles = [
-            jnp.where(lanes < 64, roll(o_sc[0], 64), o_sc[1]),
-            jnp.where(lanes < 64, roll(o_sc[2], 64), o_sc[3]),
-            jnp.where(lanes < 64, roll(o_sc[4], 64), stats),
-        ]
-        to_chunks(out, (), jnp.concatenate(tiles, axis=0).astype(BF16), chunk)
+    fetch(0).start()
+    fetch(1).start()
+    row = lax.axis_index("req")
+
+    def find(r, length):
+        mine = jnp.logical_and(live(meta, r), meta[1, r] == row)
+        return jnp.where(mine, meta[2, r], length)
+
+    length = lax.fori_loop(0, requests, find, 0)
+    position = lax.broadcasted_iota(jnp.int32, (8, span), 1)
+    bias = jnp.where(position < length, 0.0, NEG)[0:1]
+    tiles = split_heads(q[...].reshape(-1, LANES), count)
+    lanes = lane_iota(count)
+    level = jnp.zeros((count, LANES), F32)
+    kept = []
+    for head in range(heads):
+        if head < 2:
+            fetch(head).wait()
+        kv = kv_sc[(offset + head) // groups - first]
+        scores = lax.dot_general(
+            tiles[head], kv, (((1,), (1,)), ((), ())), preferred_element_type=F32
+        )
+        mixed, one = soft(scores + bias, kv)
+        level = jnp.where(lanes == head, one, level)
+        kept.append(mixed)
+    roll = lambda v, n: pltpu.roll(v, n, 1)
+    high = level.astype(BF16).astype(F32)
+    mid = (level - high).astype(BF16).astype(F32)
+    low = (level - high - mid).astype(BF16).astype(F32)
+    stats = roll(high, 64) + roll(mid, 64 + heads) + roll(low, 64 + 2 * heads)
+    tiles = [
+        jnp.where(lanes < 64, roll(kept[0], 64), kept[1]),
+        jnp.where(lanes < 64, roll(kept[2], 64), kept[3]),
+        jnp.where(lanes < 64, roll(kept[4], 64), stats),
+    ]
+    to_chunks(out, (), jnp.concatenate(tiles, axis=0).astype(BF16), chunk)
 
 
 def merge_kernel(req_dev, meta, far, near, mixed):
@@ -292,31 +283,26 @@
     mixed[0] = jnp.concatenate([done[0], done[1], last], axis=0).astype(BF16)
 
 
-def project_kernel(m_a, m_b, w_a, w_b, base, out, lhs):
-    req_dev, count, block = out.shape
+def project_kernel(block, m_a, m_b, w_a, w_b, base, out, lhs):
+    count, width = out.shape[1:]
     half = count // 2
-    sources = (m_a, m_b)
-
-    @pl.when(pl.program_id(0) == 0)
-    def _():
-        lanes = lane_iota(half)
-        for b in range(req_dev):
-            start = b * count
-            for number, m in enumerate(sources):
-                for p in range(2):
-                    col = number * 256 + p * 128
-                    lhs[start : start + count, col : col + 128] = m[b, p * count : (p + 1) * count]
-            left = m_a[b, 2 * count :].astype(F32)
-            right = m_b[b, 2 * count :].astype(F32)
-            above = jnp.where(lanes < 64, left, pltpu.roll(right, 64, 1))
-            below = jnp.where(lanes < 64, pltpu.roll(left, 64, 1), right)
-            lhs[start : start + half, 512:640] = above.astype(BF16)
-            lhs[start + half : start + count, 512:640] = below.astype(BF16)
-
-    total = base[...].reshape(req_dev * count, block).astype(F32)
-    weights = jnp.concatenate([w_a[:256], w_b[:256], w_a[256:], w_b[256:]], axis=0)
-    total += jnp.dot(lhs[...], weights, preferred_element_type=F32)
-    out[...] = total.astype(out.dtype).reshape(req_dev, count, block)
+    lanes = lane_iota(half)
+    for number, m in enumerate((m_a, m_b)):
+        for p in range(2):
+            col = number * 256 + p * 128
+            lhs[:, col : col + 128] = m[0, p * count : (p + 1) * count]
+    left = m_a[0, 2 * count :].astype(F32)
+    right = m_b[0, 2 * count :].astype(F32)
+    lhs[:half, 512:] = jnp.where(lanes < 64, left, pltpu.roll(right, 64, 1)).astype(BF16)
+    lhs[half:, 512:] = jnp.where(lanes < 64, pltpu.roll(left, 64, 1), right).astype(BF16)
+    for start in range(0, width, block):
+        part = pl.ds(start, block)
+        weights = jnp.concatenate(
+            [w_a[:256, part], w_b[:256, part], w_a[256:, part], w_b[256:, part]], axis=0
+        )
+        total = base[0, :, part].astype(F32)
+        total += jnp.dot(lhs[...], weights, preferred_element_type=F32)
+        out[0, :, part] = total.astype(out.dtype)
 
 
 def held(plane, here):
@@ -326,16 +312,17 @@
 
 
 def cache_kernel(req_dev, span, meta, *refs):
-    blocks, (mine, theirs, _, out, wide, kept_sc, sem) = refs[:-7], refs[-7:]
-    l = pl.program_id(0)
+    blocks, (mine, theirs, _, out, kept_sc, out_sc, sem, out_sem) = refs[:-8], refs[-8:]
     place, tp_place = lax.axis_index("req"), lax.axis_index("tp")
     side = place % 2
     kv_heads, segment = out.shape[1], out.shape[2]
     count = mine.shape[2]
+    start = (side * lax.axis_size("tp") + tp_place) * segment
+    skip = pl.multiple_of(start - jnp.minimum(start, span - segment), 16)
+    first = (place // 2) * 2 * req_dev
 
     def fetch(number, action):
-        request = (place // 2) * 2 * req_dev + number
-        row = jnp.where(live(meta, request), meta[1, request], 0)
+        row = jnp.where(live(meta, first + number), meta[1, first + number], 0)
         plane, which = row // 2, (row % 2) ^ side
         dst = kept_sc.at[number, :, pl.ds(0, segment), :]
         if len(blocks) == 1:
@@ -347,34 +334,32 @@
             def _():
                 action(pltpu.make_async_copy(block.at[which], dst, sem.at[number]))
 
-    @pl.when(l == 0)
-    def _():
-        for number in range(2 * req_dev):
-            fetch(number, lambda copy: copy.start())
-
-    length = live_length(meta, (place // 2) * 2 * req_dev + l)
-    start = (side * lax.axis_size("tp") + tp_place) * segment
-    skip = pl.multiple_of(start - jnp.minimum(start, span - segment), 16)
-    shift = jnp.clip(start - length, -segment, count) + segment
-    position = start + lax.broadcasted_iota(jnp.int32, (segment, LANES), 0)
-    old = position < length
-    new = jnp.logical_and(position >= length, position < length + count)
-    local = l // req_dev == side
-    for head in range(kv_heads):
-
-        @pl.when(local)
-        def _():
-            wide[head, segment : segment + count] = mine[0, head].astype(F32)
-
-        @pl.when(jnp.logical_not(local))
-        def _():
-            wide[head, segment : segment + count] = theirs[0, head].astype(F32)
-
-    fetch(l, lambda copy: copy.wait())
-    for head in range(kv_heads):
-        moved = wide[head, pl.ds(shift, segment), :]
-        kept = kept_sc[l, head, pl.ds(skip, segment), :].astype(F32)
-        out[0, head] = jnp.where(old, kept, jnp.where(new, moved, 0.0)).astype(BF16)
+    def write(number):
+        return pltpu.make_async_copy(out_sc.at[number], out.at[number], out_sem.at[number])
+
+    for number in range(2 * req_dev):
+        fetch(number, lambda copy: copy.start())
+    rows = lax.broadcasted_iota(jnp.int32, (segment, count), 0)
+    cols = lax.broadcasted_iota(jnp.int32, (segment, count), 1)
+    for number in range(2 * req_dev):
+        ahead = live_length(meta, first + number) - start
+        shift = jnp.where(rows - cols == ahead, 1.0, 0.0).astype(BF16)
+        local = number // req_dev == side
+        place_of = number % req_dev
+        new = jnp.concatenate(
+            [jnp.where(local, mine[place_of, h], theirs[place_of, h]) for h in range(kv_heads)],
+            axis=1,
+        )
+        moved = jnp.dot(shift, new, preferred_element_type=F32)
+        old = lax.broadcasted_iota(jnp.int32, (segment, LANES), 0) < ahead
+        fetch(number, lambda copy: copy.wait())
+        for head in range(kv_heads):
+            kept = kept_sc[number, head, pl.ds(skip, segment), :].astype(F32)
+            part = moved[:, head * LANES : head * LANES + LANES]
+            out_sc[number, head] = jnp.where(old, kept, part).astype(BF16)
+        write(number).start()
+    for number in range(2 * req_dev):
+        write(number).wait()
 
 
 def permuted(value, axis, mask):
@@ -473,14 +458,10 @@
         outer = [(z, z ^ 1) for z in range(planes)]
         beside = crossed(both, outer)
         middle = crossed(both, [(1, 2), (2, 1)])
-        far_middle = crossed(beside, [(1, 2), (2, 1)])
-        outward = crossed(middle, [(1, 0), (2, 3)])
-        far_outward = crossed(far_middle, [(1, 0), (2, 3)])
-        blocks = [both, beside, middle, far_middle, outward, far_outward]
     else:
         column = [list(range(parity, n_req, 2)) for parity in range(2)]
         blocks = [lax.all_gather(both, "req", axis_index_groups=column)]
-        beside = middle = far_middle = outward = both
+        beside = middle = both
 
     w_x = permuted(w_out, "tp", tp_count // 2)
     w_c = permuted(w_out, "tp", 1)
@@ -514,7 +495,10 @@
         cost_estimate=cost(0, 1 << 20),
         name="route_query",
     )(meta, q_mid)
-    q_row = lax.optimization_barrier((exchanged(q_out), beside, middle, fresh))[0]
+    q_row, beside, middle, _ = lax.optimization_barrier((exchanged(q_out), beside, middle, fresh))
+    if hops:
+        far_middle = crossed(beside, [(1, 2), (2, 1)])
+        outward = crossed(middle, [(1, 0), (2, 3)])
     fresh_partner = permuted(fresh, "req", 1)
 
     near = pl.pallas_call(
@@ -532,17 +516,12 @@
     )(q, fresh)
 
     far = pl.pallas_call(
-        functools.partial(row_kernel, requests, groups, o_chunk),
-        grid=(heads,),
+        functools.partial(row_kernel, requests, count, heads, groups, o_chunk),
         out_shape=jax.ShapeDtypeStruct((n_req, o_chunk, LANES), BF16),
-        in_specs=[SMEM, full((n_req, q_chunk, LANES)), any_spec],
-        out_specs=full((n_req, o_chunk, LANES)),
+        in_specs=[SMEM, vmem_spec, any_spec],
+        out_specs=vmem_spec,
         scratch_shapes=[
-            pltpu.VMEM((heads, count, LANES), BF16),
-            pltpu.VMEM((heads, count, LANES), F32),
-            pltpu.VMEM((count, LANES), F32),
             pltpu.VMEM((2, span, LANES), BF16),
-            pltpu.VMEM((8, span), F32),
             pltpu.SemaphoreType.DMA((2,)),
         ],
         compiler_params=params(60),
@@ -551,6 +530,10 @@
     )(meta, q_row, stored)
 
     far_mid = exchanged(far)
+    if hops:
+        far_mid = lax.optimization_barrier((far_mid, far_middle, outward, fresh_partner, near))[0]
+        far_outward = crossed(far_middle, [(1, 0), (2, 3)])
+        blocks = [both, beside, middle, far_middle, outward, far_outward]
     far_out = pl.pallas_call(
         functools.partial(route_result_kernel, requests),
         out_shape=jax.ShapeDtypeStruct((requests, o_chunk, LANES), BF16),
@@ -561,7 +544,6 @@
         name="route_result",
     )(meta, far_mid)
     far_home = exchanged(far_out.reshape(n_req, req_dev, o_chunk, LANES))
-    far_home = lax.optimization_barrier((far_home, far_middle, outward))[0]
 
     mixed = pl.pallas_call(
         functools.partial(merge_kernel, req_dev),
@@ -581,45 +563,40 @@
     m_x = permuted(mixed, "tp", tp_count // 2)
     m_c = permuted(mixed, "tp", 1)
 
-    block = 512
-    t_spec = pl.BlockSpec((req_dev, count, block), lambda n: (0, 0, n))
-
     def project(m_a, m_b, w_a, w_b, base, dtype, name):
-        m_spec = full((req_dev, q_rows, LANES))
-        w_spec = pl.BlockSpec((heads * head_dim, block), lambda n: (0, n))
+        m_spec = pl.BlockSpec((1, q_rows, LANES), lambda b: (b, 0, 0))
         return pl.pallas_call(
-            project_kernel,
-            grid=(width // block,),
+            functools.partial(project_kernel, 512),
+            grid=(req_dev,),
             out_shape=jax.ShapeDtypeStruct(tokens.shape, dtype),
-            in_specs=[m_spec] * 2 + [w_spec] * 2 + [t_spec],
-            out_specs=t_spec,
-            scratch_shapes=[pltpu.VMEM((req_dev * count, 640), BF16)],
+            in_specs=[m_spec] * 2 + [full(w_out.shape)] * 2 + [token_spec],
+            out_specs=token_spec,
+            scratch_shapes=[pltpu.VMEM((count, 640), BF16)],
             compiler_params=params(),
-            cost_estimate=cost(2 * req_dev * count * width * 640, 6 << 20),
+            cost_estimate=HINT,
             name=name,
         )(m_a, m_b, w_a, w_b, base)
 
     partial = project(mixed, m_c, w_out, w_c, tokens, F32, "project_chip")
-    new_spec = pl.BlockSpec((1, kv_heads, count, LANES), lambda l: (l % req_dev, 0, 0, 0))
+    m_x = lax.optimization_barrier((m_x, partial))[0]
+    m_xc = permuted(m_x, "tp", 1)
+    layer = project(m_x, m_xc, w_x, w_xc, partial, BF16, "project_rest")
+
     cache = pl.pallas_call(
         functools.partial(cache_kernel, req_dev, span),
-        grid=(2 * req_dev,),
-        in_specs=[SMEM] + [any_spec] * len(blocks) + [new_spec, new_spec, any_spec],
-        out_specs=pl.BlockSpec((1, kv_heads, segment, LANES), lambda l: (l, 0, 0, 0)),
+        in_specs=[SMEM] + [any_spec] * len(blocks) + [vmem_spec, vmem_spec, any_spec],
+        out_specs=any_spec,
         scratch_shapes=[
-            pltpu.VMEM((kv_heads, 2 * segment + count, LANES), F32),
             pltpu.VMEM((2 * req_dev, kv_heads, 2 * segment, LANES), BF16),
+            pltpu.VMEM((2 * req_dev, kv_heads, segment, LANES), BF16),
+            pltpu.SemaphoreType.DMA((2 * req_dev,)),
             pltpu.SemaphoreType.DMA((2 * req_dev,)),
         ],
         out_shape=jax.ShapeDtypeStruct((2 * req_dev, kv_heads, segment, LANES), BF16),
-        compiler_params=params(),
+        compiler_params=params(60),
         cost_estimate=HINT,
         name="cache",
-    )(meta, *blocks, fresh, fresh_partner, partial)
-    m_x = lax.optimization_barrier((m_x, partial, cache))[0]
-    m_xc = permuted(m_x, "tp", 1)
-    layer = project(m_x, m_xc, w_x, w_xc, partial, BF16, "project_rest")
-
+    )(meta, *blocks, fresh, fresh_partner, layer)
     return (layer, cache)
 
 

time: 117 us -> 110 us (0.940)
  waiting for transfers between devices: 36.5 us -> 31.2 us
  Pallas kernels: 39.2 us -> 35.9 us
  starting transfers between devices: 31.9 us -> 33.1 us
    ppermute x5, waiting for transfers between devices: 12.6 us -> 0.01 us  [crossed(): return lax.ppermute(value, 'req', pairs)]
    ppermute x8, waiting for transfers between devices: 1.67 us -> 6.9 us  [permuted(): return lax.ppermute(value, axis, pairs)]
    pallas_call x4, Pallas kernels: 23 us -> 19.8 us  [the longest x2 7.97 us: project(): pl.pallas_call(functools.partial(project_kernel, 512), grid=(req_dev,), o...]
    all_to_all x4, waiting for transfers between devices: 22.3 us -> 24.3 us  [exchanged(): return lax.all_to_all(value, 'req', split_axis=0, concat_axis=0, tiled=True)]
    all_to_all x4, starting transfers between devices: 16 us -> 17.8 us  [exchanged(): return lax.all_to_all(value, 'req', split_axis=0, concat_axis=0, tiled=True)]
    unnamed x28 -> x26, local copies, waits for them, and re-layouts: 3.79 us -> 3.79 us
  transfers between devices with their start and end apart: 17 -> 17, of which waited for: 8 -> 7; matrix products, arithmetic and copies ran while one was open for 2% -> 2% of each run, Pallas kernels for 29% -> 29%
where the time goes in v3:
time: 110 us; the launch traced here: 109 us
  Pallas kernels  35.9 us (33%)
  starting transfers between devices  33.1 us (30%)
  waiting for transfers between devices  31.2 us (28%)
  local copies, waits for them, and re-layouts  5.68 us (5%)
  other arithmetic  2.62 us (2%)
    all_to_all x4, waiting for transfers between devices, exchanged(): return lax.all_to_all(value, 'req', split_axis=0, concat_axis=0, tiled=True)  24.3 us
    all_to_all x4, starting transfers between devices, exchanged(): return lax.all_to_all(value, 'req', split_axis=0, concat_axis=0, tiled=True)  17.8 us
    pallas_call x2, Pallas kernels, project(): pl.pallas_call(functools.partial(project_kernel, 512), grid=(req_dev,), o...  7.97 us
    ppermute x5, starting transfers between devices, crossed(): return lax.ppermute(value, 'req', pairs)  7.84 us
    pallas_call x1, Pallas kernels, on_device(): pl.pallas_call(functools.partial(row_kernel, requests, count, heads, grou...  7.43 us
    ppermute x8, starting transfers between devices, permuted(): return lax.ppermute(value, axis, pairs)  7.43 us
    ppermute x8, waiting for transfers between devices, permuted(): return lax.ppermute(value, axis, pairs)  6.9 us
    pallas_call x1, Pallas kernels, on_device(): pl.pallas_call(functools.partial(query_kernel, req_dev, q_chunk), grid=(r...  5.1 us
  transfers between devices with their start and end apart: 17, of which 7 were waited for; matrix products, arithmetic and copies ran while one was open for 2% of the time, Pallas kernels for 29%

profile of v3, /device:TPU:0, one launch (start us, length us, event | category | flops | bytes accessed | tf_op | source)
XLA Modules:
  0.0 109.5 jit_solution(14546040013988130551)
XLA Ops:
  0.7 1.9 %constant_dynamic-slice_fusion = (bf16[1,5,288,128]{3,2,1,0:T(8,128)(2,1)S(1)}, bf16[5,288,128]{2,1,0:T(8,128)(2,1)}) fusion(bf16[1,5,2048,128]{3,2,1,0:T(8,128)(2,1)} %stored.1, s32[]{:T(128)S(6)} %select_n.14, s32[]{:T(128)S(6)} %select_n.15), kind=kLoop, calls=%fused_computation.3 | loop fusion | bytes 1474568 | tf_op jit(solution)/shard_map/dynamic_slice | solution.py:424
  2.5 3.0 %collective-permute-start = (bf16[5,288,128]{2,1,0:T(8,128)(2,1)}, bf16[5,288,128]{2,1,0:T(8,128)(2,1)}, u32[]{:S(2)}, u32[]{:S(2)}) collective-permute-start(bf16[5,288,128]{2,1,0:T(8,128)(2,1)} %get-tuple-element.15), channel_id=1, source_target_pairs={{0,4},{4,0},{8,12},{12,8},{16,20},{20,16},{24,28},{28,24},{1,5},{5... | collective-permute-start | bytes 1105928 | tf_op jit(solution)/shard_map/ppermute | solution.py:367
  5.5 5.1 %query.1.after.q = bf16[8,2,80,128]{3,2,1,0:T(8,128)(2,1)} custom-call(s32[16]{0:T(128)} %cont.1, s32[16]{0:T(128)} %clen.1, bf16[2,256,2048]{2,1,0:T(8,128)(2,1)} %base.1, f32[1,2048]{1,0:T(1,128)} %bitcast.13, bf16[320,2048]{1,0:T(8,128)(2,1)} %bitcast.16, f32[1,64]{1,0:T(1,128)} %bitcast.19, f32[2,408,128]{2,1,0:T(8,128)} %constant.34.clone.table), custom_call_target="tpu_custom_call" | custom-call | flops 805306368 | bytes 6291456 | tf_op jit(solution)/shard_map/query/pallas_call | solution.py:428
  10.7 5.2 %all-to-all-start = ((bf16[8,2,80,128]{3,2,1,0:T(8,128)(2,1)}), bf16[8,2,80,128]{3,2,1,0:T(8,128)(2,1)S(1)}, u32[]{:S(2)}, u32[]{:S(2)}) async-start(bf16[8,2,80,128]{3,2,1,0:T(8,128)(2,1)} %query.1.after.q), calls=%async_computation | async-start | bytes 655360 | tf_op jit(solution)/shard_map/all_to_all | solution.py:371
  15.8 1.9 %pad_maximum_fusion.refs_0_ = bf16[2,5,288,128]{3,2,1,0:T(8,128)(2,1)} fusion(bf16[1,5,288,128]{3,2,1,0:T(8,128)(2,1)} %bitcast.8, bf16[1,5,288,128]{3,2,1,0:T(8,128)(2,1)S(1)} %get-tuple-element.14), kind=kLoop, calls=%fused_computation | loop fusion | flops 368640 | bytes 1474560 | tf_op jit(solution)/shard_map/stack | solution.py:449
  17.8 2.0 %collective-permute-start.1 = (bf16[2,5,288,128]{3,2,1,0:T(8,128)(2,1)}, bf16[2,5,288,128]{3,2,1,0:T(8,128)(2,1)}, u32[]{:S(2)}, u32[]{:S(2)}) collective-permute-start(bf16[2,5,288,128]{3,2,1,0:T(8,128)(2,1)} %pad_maximum_fusion.refs_0_), channel_id=1, source_target_pairs={{0,8},{4,12},{8,0},{12,4},{16,24},{20,28},{24,16},{28,20},{1,9},{5... | collective-permute-start | bytes 2211848 | tf_op jit(solution)/shard_map/ppermute | solution.py:455
  19.8 1.5 %collective-permute-start.2 = (bf16[2,5,288,128]{3,2,1,0:T(8,128)(2,1)}, bf16[2,5,288,128]{3,2,1,0:T(8,128)(2,1)}, u32[]{:S(2)}, u32[]{:S(2)}) collective-permute-start(bf16[2,5,288,128]{3,2,1,0:T(8,128)(2,1)} %pad_maximum_fusion.refs_0_), channel_id=1, source_target_pairs={{8,16},{12,20},{16,8},{20,12},{9,17},{13,21},{17,9},{21,13},{10,18... | collective-permute-start | bytes 2211848 | tf_op jit(solution)/shard_map/ppermute | solution.py:455
  21.3 1.5 %collective-permute-start.10 = (bf16[320,2048]{1,0:T(8,128)(2,1)}, bf16[320,2048]{1,0:T(8,128)(2,1)}, u32[]{:S(2)}, u32[]{:S(2)}) collective-permute-start(bf16[320,2048]{1,0:T(8,128)(2,1)} %w_a.1), channel_id=1, source_target_pairs={{0,2},{1,3},{2,0},{3,1},{4,6},{5,7},{6,4},{7,5},{8,10},{9,11},{10,... | collective-permute-start | bytes 3932168 | tf_op jit(solution)/shard_map/ppermute | solution.py:367
  23.5 3.3 %all-to-all-done = bf16[8,2,80,128]{3,2,1,0:T(8,128)(2,1)S(1)} async-done(((bf16[8,2,80,128]{3,2,1,0:T(8,128)(2,1)}), bf16[8,2,80,128]{3,2,1,0:T(8,128)(2,1)S(1)}, u32[]{:S(2)}, u32[]{:S(2)}) %all-to-all-start) | async-done | bytes 327712 | tf_op jit(solution)/shard_map/all_to_all | solution.py:371
  26.8 1.4 %route_query.1 = bf16[8,80,128]{2,1,0:T(8,128)(2,1)} custom-call(s32[3,16]{1,0:T(4,128)S(1)} %pad_add_fusion.meta, bf16[16,80,128]{2,1,0:T(8,128)(2,1)S(1)} %bitcast.12), custom_call_target="tpu_custom_call" | custom-call | bytes 1048576 | tf_op jit(solution)/shard_map/route_query/pallas_call | solution.py:489
  28.1 4.0 %all-to-all-start.1 = ((bf16[8,80,128]{2,1,0:T(8,128)(2,1)}), bf16[8,80,128]{2,1,0:T(8,128)(2,1)}, u32[]{:S(2)}, u32[]{:S(2)}) async-start(bf16[8,80,128]{2,1,0:T(8,128)(2,1)} %route_query.1), calls=%async_computation.1 | async-start | bytes 327680 | tf_op jit(solution)/shard_map/all_to_all | solution.py:371
  32.2 1.7 %copy-done.5 = bf16[2048,640]{1,0:T(8,128)(2,1)S(1)} copy-done((bf16[2048,640]{1,0:T(8,128)(2,1)S(1)}, bf16[2048,640]{1,0:T(8,128)(2,1)}, u32[]{:S(2)}) %copy-start.5) | copy-done | bytes 2621464
  33.9 3.9 %fresh.1.refs_6_ = bf16[2,5,256,128]{3,2,1,0:T(8,128)(2,1)S(1)} custom-call(s32[3,16]{1,0:T(4,128)S(1)} %pad_add_fusion.meta, bf16[2,256,2048]{2,1,0:T(8,128)(2,1)S(1)} %copy-done, f32[1,2048]{1,0:T(1,128)S(1)} %bitcast.14, bf16[2048,640]{1,0:T(8,128)(2,1)S(1)} %copy-done.5, f32[1,64]{1,0:T(1,128)S(1)} %bitcast.15, f32[2,408,128]{2,1,0:T(8,128)S(1)} %copy-done.6, ...), custom_call_target="tpu_custom_call" | custom-call | bytes 1024 | tf_op jit(solution)/shard_map/fresh/pallas_call | solution.py:470
  37.9 7.6 %all-to-all-done.1.q = bf16[8,80,128]{2,1,0:T(8,128)(2,1)} async-done(((bf16[8,80,128]{2,1,0:T(8,128)(2,1)}), bf16[8,80,128]{2,1,0:T(8,128)(2,1)}, u32[]{:S(2)}, u32[]{:S(2)}) %all-to-all-start.1) | async-done | bytes 163872 | tf_op jit(solution)/shard_map/all_to_all | solution.py:371
  45.5 1.5 %collective-permute-start.3 = (bf16[2,5,288,128]{3,2,1,0:T(8,128)(2,1)}, bf16[2,5,288,128]{3,2,1,0:T(8,128)(2,1)}, u32[]{:S(2)}, u32[]{:S(2)}) collective-permute-start(bf16[2,5,288,128]{3,2,1,0:T(8,128)(2,1)} %collective-permute-done.1.refs_1_), channel_id=1, source_target_pairs={{8,16},{12,20},{16,8},{20,12},{9,17},{13,21},{17,9},{21,13},{10,18... | collective-permute-start | bytes 2211848 | tf_op jit(solution)/shard_map/ppermute | solution.py:455
  47.0 1.3 %collective-permute-start.4 = (bf16[2,5,288,128]{3,2,1,0:T(8,128)(2,1)}, bf16[2,5,288,128]{3,2,1,0:T(8,128)(2,1)}, u32[]{:S(2)}, u32[]{:S(2)}) collective-permute-start(bf16[2,5,288,128]{3,2,1,0:T(8,128)(2,1)} %collective-permute-done.2.refs_2_), channel_id=1, source_target_pairs={{8,0},{12,4},{16,24},{20,28},{9,1},{13,5},{17,25},{21,29},{10,2},{... | collective-permute-start | bytes 2211848 | tf_op jit(solution)/shard_map/ppermute | solution.py:455
  48.3 1.3 %collective-permute-start.5 = (bf16[2,5,256,128]{3,2,1,0:T(8,128)(2,1)S(1)}, bf16[2,5,256,128]{3,2,1,0:T(8,128)(2,1)}, u32[]{:S(2)}, u32[]{:S(2)}) collective-permute-start(bf16[2,5,256,128]{3,2,1,0:T(8,128)(2,1)S(1)} %fresh.1.refs_6_), channel_id=1, source_target_pairs={{0,4},{4,0},{8,12},{12,8},{16,20},{20,16},{24,28},{28,24},{1,5},{5... | collective-permute-start | bytes 1966088 | tf_op jit(solution)/shard_map/ppermute | solution.py:367
  49.6 7.4 %attend_row.1 = bf16[8,96,128]{2,1,0:T(8,128)(2,1)} custom-call(s32[3,16]{1,0:T(4,128)} %copy-done.8, bf16[8,80,128]{2,1,0:T(8,128)(2,1)} %all-to-all-done.1.q, bf16[1,5,2048,128]{3,2,1,0:T(8,128)(2,1)} %stored.1), custom_call_target="tpu_custom_call" | custom-call | flops 2684354560 | bytes 33554432 | tf_op jit(solution)/shard_map/attend_row/pallas_call | solution.py:518
  57.0 5.2 %all-to-all-start.2 = ((bf16[8,96,128]{2,1,0:T(8,128)(2,1)}), bf16[8,96,128]{2,1,0:T(8,128)(2,1)S(1)}, u32[]{:S(2)}, u32[]{:S(2)}) async-start(bf16[8,96,128]{2,1,0:T(8,128)(2,1)} %attend_row.1), calls=%async_computation.2 | async-start | bytes 393216 | tf_op jit(solution)/shard_map/all_to_all | solution.py:371
  62.2 2.8 %attend_new.1.near = f32[2,3,256,128]{3,2,1,0:T(8,128)S(1)} custom-call(bf16[8,2,80,128]{3,2,1,0:T(8,128)(2,1)S(1)} %copy-done.2, bf16[2,5,256,128]{3,2,1,0:T(8,128)(2,1)S(1)} %fresh.1.refs_6_), custom_call_target="tpu_custom_call" | custom-call | bytes 1024 | tf_op jit(solution)/shard_map/attend_new/pallas_call | solution.py:504
  66.0 4.3 %all-to-all-done.2.src = bf16[8,96,128]{2,1,0:T(8,128)(2,1)S(1)} async-done(((bf16[8,96,128]{2,1,0:T(8,128)(2,1)}), bf16[8,96,128]{2,1,0:T(8,128)(2,1)S(1)}, u32[]{:S(2)}, u32[]{:S(2)}) %all-to-all-start.2) | async-done | bytes 196640 | tf_op jit(solution)/shard_map/all_to_all | solution.py:371
  70.2 1.3 %route_result.1 = bf16[16,96,128]{2,1,0:T(8,128)(2,1)} custom-call(s32[3,16]{1,0:T(4,128)S(1)} %copy-done.9, bf16[8,96,128]{2,1,0:T(8,128)(2,1)S(1)} %all-to-all-done.2.src), custom_call_target="tpu_custom_call" | custom-call | bytes 1048576 | tf_op jit(solution)/shard_map/route_result/pallas_call | solution.py:537
  71.6 3.5 %all-to-all-start.3 = ((bf16[8,2,96,128]{3,2,1,0:T(8,128)(2,1)}), bf16[8,2,96,128]{3,2,1,0:T(8,128)(2,1)S(1)}, u32[]{:S(2)}, u32[]{:S(2)}) async-start(bf16[8,2,96,128]{3,2,1,0:T(8,128)(2,1)} %bitcast.10), calls=%async_computation.3 | async-start | bytes 786432 | tf_op jit(solution)/shard_map/all_to_all | solution.py:371
  75.1 1.5 %collective-permute-start.12 = (bf16[2,5,288,128]{3,2,1,0:T(8,128)(2,1)}, bf16[2,5,288,128]{3,2,1,0:T(8,128)(2,1)}, u32[]{:S(2)}, u32[]{:S(2)}) collective-permute-start(bf16[2,5,288,128]{3,2,1,0:T(8,128)(2,1)} %collective-permute-done.3.refs_3_), channel_id=1, source_target_pairs={{8,0},{12,4},{16,24},{20,28},{9,1},{13,5},{17,25},{21,29},{10,2},{... | collective-permute-start | bytes 2211848 | tf_op jit(solution)/shard_map/ppermute | solution.py:455
  76.6 9.2 %all-to-all-done.3.far = bf16[8,2,96,128]{3,2,1,0:T(8,128)(2,1)S(1)} async-done(((bf16[8,2,96,128]{3,2,1,0:T(8,128)(2,1)}), bf16[8,2,96,128]{3,2,1,0:T(8,128)(2,1)S(1)}, u32[]{:S(2)}, u32[]{:S(2)}) %all-to-all-start.3) | async-done | bytes 393248 | tf_op jit(solution)/shard_map/all_to_all | solution.py:371
  86.9 1.5 %merge.1.m_a = bf16[2,640,128]{2,1,0:T(8,128)(2,1)S(1)} custom-call(s32[3,16]{1,0:T(4,128)S(1)} %copy-done.9, bf16[8,2,96,128]{3,2,1,0:T(8,128)(2,1)S(1)} %all-to-all-done.3.far, f32[2,3,256,128]{3,2,1,0:T(8,128)S(1)} %copy-done.4), custom_call_target="tpu_custom_call" | custom-call | bytes 1024 | tf_op jit(solution)/shard_map/merge/pallas_call | solution.py:548
  88.5 1.5 %collective-permute-start.6 = (bf16[2,640,128]{2,1,0:T(8,128)(2,1)S(1)}, bf16[2,640,128]{2,1,0:T(8,128)(2,1)S(1)}, u32[]{:S(2)}, u32[]{:S(2)}) collective-permute-start(bf16[2,640,128]{2,1,0:T(8,128)(2,1)S(1)} %merge.1.m_a), channel_id=1, source_target_pairs={{0,2},{1,3},{2,0},{3,1},{4,6},{5,7},{6,4},{7,5},{8,10},{9,11},{10,... | collective-permute-start | bytes 983048 | tf_op jit(solution)/shard_map/ppermute | solution.py:367
  90.2 3.3 %project_chip.1.base = f32[2,256,2048]{2,1,0:T(8,128)S(1)} custom-call(bf16[2,640,128]{2,1,0:T(8,128)(2,1)S(1)} %merge.1.m_a, bf16[2,640,128]{2,1,0:T(8,128)(2,1)S(1)} %collective-permute-done.7.m_b, bf16[320,2048]{1,0:T(8,128)(2,1)S(1)} %copy-done.7, bf16[320,2048]{1,0:T(8,128)(2,1)} %collective-permute-done.8.w_b, bf16[2,256,2048]{2,1,0:T(8,128)(2,1)S(1)} %copy-done), custom_call_target="tpu_custom_call" | custom-call | bytes 1024 | tf_op jit(solution)/shard_map/project_chip/pallas_call | solution.py:568
  93.5 5.2 %collective-permute-done.6.m_a = bf16[2,640,128]{2,1,0:T(8,128)(2,1)S(1)} collective-permute-done((bf16[2,640,128]{2,1,0:T(8,128)(2,1)S(1)}, bf16[2,640,128]{2,1,0:T(8,128)(2,1)S(1)}, u32[]{:S(2)}, u32[]{:S(2)}) %collective-permute-start.6) | collective-permute-done | bytes 327712 | tf_op jit(solution)/shard_map/ppermute | solution.py:367
  98.7 1.6 %collective-permute-done.9.m_b = bf16[2,640,128]{2,1,0:T(8,128)(2,1)S(1)} collective-permute-done((bf16[2,640,128]{2,1,0:T(8,128)(2,1)S(1)}, bf16[2,640,128]{2,1,0:T(8,128)(2,1)S(1)}, u32[]{:S(2)}, u32[]{:S(2)}) %collective-permute-start.9) | collective-permute-done | bytes 327712 | tf_op jit(solution)/shard_map/ppermute | solution.py:367
  100.3 4.7 %project_rest.1.refs_8_ = bf16[2,256,2048]{2,1,0:T(8,128)(2,1)} custom-call(bf16[2,640,128]{2,1,0:T(8,128)(2,1)S(1)} %collective-permute-done.6.m_a, bf16[2,640,128]{2,1,0:T(8,128)(2,1)S(1)} %collective-permute-done.9.m_b, bf16[320,2048]{1,0:T(8,128)(2,1)} %collective-permute-done.10.w_a, bf16[320,2048]{1,0:T(8,128)(2,1)} %collective-permute-done.11.w_b, ...), custom_call_target="tpu_custom_call" | custom-call | bytes 1024 | tf_op jit(solution)/shard_map/project_rest/pallas_call | solution.py:568
  105.0 4.4 %cache.1 = bf16[4,5,288,128]{3,2,1,0:T(8,128)(2,1)} custom-call(s32[3,16]{1,0:T(4,128)} %copy-done.8, bf16[2,5,288,128]{3,2,1,0:T(8,128)(2,1)} %pad_maximum_fusion.refs_0_, bf16[2,5,288,128]{3,2,1,0:T(8,128)(2,1)} %collective-permute-done.1.refs_1_, bf16[2,5,288,128]{3,2,1,0:T(8,128)(2,1)} %collective-permute-done.2.refs_2_, ...), custom_call_target="tpu_custom_call" | custom-call | bytes 1024 | tf_op jit(solution)/shard_map/cache/pallas_call | solution.py:585
  (41 shorter events, 3.0 us)
Async XLA Ops:
  2.5 13.3 %collective-permute-start = (bf16[5,288,128]{2,1,0:T(8,128)(2,1)}, bf16[5,288,128]{2,1,0:T(8,128)(2,1)}, u32[]{:S(2)}, u32[]{:S(2)}) collective-permute-start(bf16[5,288,128]{2,1,0:T(8,128)(2,1)} %get-tuple-element.15), channel_id=1, source_target_pairs={{0,4},{4,0},{8,12},{12,8},{16,20},{20,16},{24,28},{28,24},{1,5},{5... | collective-permute-start | bytes 1105928 | tf_op jit(solution)/shard_map/ppermute | solution.py:367
  5.5 17.3 %copy-start.12 = (s32[16]{0:T(128)S(1)}, s32[16]{0:T(128)}, u32[]{:S(2)}) copy-start(s32[16]{0:T(128)} %clen.1) | copy-start | bytes 196
  10.6 21.5 %copy-start = (bf16[2,256,2048]{2,1,0:T(8,128)(2,1)S(1)}, bf16[2,256,2048]{2,1,0:T(8,128)(2,1)}, u32[]{:S(2)}) copy-start(bf16[2,256,2048]{2,1,0:T(8,128)(2,1)} %base.1) | copy-start | bytes 6291460
  10.6 21.5 %copy-start.2 = (bf16[8,2,80,128]{3,2,1,0:T(8,128)(2,1)S(1)}, bf16[8,2,80,128]{3,2,1,0:T(8,128)(2,1)}, u32[]{:S(2)}) copy-start(bf16[8,2,80,128]{3,2,1,0:T(8,128)(2,1)} %query.1.after.q) | copy-start | bytes 983044
  10.6 21.6 %copy-start.6 = (f32[2,408,128]{2,1,0:T(8,128)S(1)}, f32[2,408,128]{2,1,0:T(8,128)}, u32[]{:S(2)}) copy-start(f32[2,408,128]{2,1,0:T(8,128)} %constant.34.clone.table) | copy-start | bytes 1253380
  10.6 21.5 %copy-start.10 = (f32[2048]{0:T(1024)S(1)}, f32[2048]{0:T(1024)}, u32[]{:S(2)}) copy-start(f32[2048]{0:T(1024)} %param.13) | copy-start | bytes 24580
  10.6 21.5 %copy-start.11 = (f32[64]{0:T(128)S(1)}, f32[64]{0:T(128)}, u32[]{:S(2)}) copy-start(f32[64]{0:T(128)} %param.18) | copy-start | bytes 772
  10.7 16.1 %all-to-all-start = ((bf16[8,2,80,128]{3,2,1,0:T(8,128)(2,1)}), bf16[8,2,80,128]{3,2,1,0:T(8,128)(2,1)S(1)}, u32[]{:S(2)}, u32[]{:S(2)}) async-start(bf16[8,2,80,128]{3,2,1,0:T(8,128)(2,1)} %query.1.after.q), calls=%async_computation | async-start | bytes 655360 | tf_op jit(solution)/shard_map/all_to_all | solution.py:371
  17.8 27.7 %collective-permute-start.1 = (bf16[2,5,288,128]{3,2,1,0:T(8,128)(2,1)}, bf16[2,5,288,128]{3,2,1,0:T(8,128)(2,1)}, u32[]{:S(2)}, u32[]{:S(2)}) collective-permute-start(bf16[2,5,288,128]{3,2,1,0:T(8,128)(2,1)} %pad_maximum_fusion.refs_0_), channel_id=1, source_target_pairs={{0,8},{4,12},{8,0},{12,4},{16,24},{20,28},{24,16},{28,20},{1,9},{5... | collective-permute-start | bytes 2211848 | tf_op jit(solution)/shard_map/ppermute | solution.py:455
  19.8 25.7 %collective-permute-start.2 = (bf16[2,5,288,128]{3,2,1,0:T(8,128)(2,1)}, bf16[2,5,288,128]{3,2,1,0:T(8,128)(2,1)}, u32[]{:S(2)}, u32[]{:S(2)}) collective-permute-start(bf16[2,5,288,128]{3,2,1,0:T(8,128)(2,1)} %pad_maximum_fusion.refs_0_), channel_id=1, source_target_pairs={{8,16},{12,20},{16,8},{20,12},{9,17},{13,21},{17,9},{21,13},{10,18... | collective-permute-start | bytes 2211848 | tf_op jit(solution)/shard_map/ppermute | solution.py:455
  21.3 53.7 %collective-permute-start.10 = (bf16[320,2048]{1,0:T(8,128)(2,1)}, bf16[320,2048]{1,0:T(8,128)(2,1)}, u32[]{:S(2)}, u32[]{:S(2)}) collective-permute-start(bf16[320,2048]{1,0:T(8,128)(2,1)} %w_a.1), channel_id=1, source_target_pairs={{0,2},{1,3},{2,0},{3,1},{4,6},{5,7},{6,4},{7,5},{8,10},{9,11},{10,... | collective-permute-start | bytes 3932168 | tf_op jit(solution)/shard_map/ppermute | solution.py:367
  23.5 14.4 %copy-start.8 = (s32[3,16]{1,0:T(4,128)}, s32[3,16]{1,0:T(4,128)S(1)}, u32[]{:S(2)}) copy-start(s32[3,16]{1,0:T(4,128)S(1)} %pad_add_fusion.meta) | copy-start | bytes 580
  28.1 17.3 %all-to-all-start.1 = ((bf16[8,80,128]{2,1,0:T(8,128)(2,1)}), bf16[8,80,128]{2,1,0:T(8,128)(2,1)}, u32[]{:S(2)}, u32[]{:S(2)}) async-start(bf16[8,80,128]{2,1,0:T(8,128)(2,1)} %route_query.1), calls=%async_computation.1 | async-start | bytes 327680 | tf_op jit(solution)/shard_map/all_to_all | solution.py:371
  32.2 1.7 %copy-start.5 = (bf16[2048,640]{1,0:T(8,128)(2,1)S(1)}, bf16[2048,640]{1,0:T(8,128)(2,1)}, u32[]{:S(2)}) copy-start(bf16[2048,640]{1,0:T(8,128)(2,1)} %w.1) | copy-start | bytes 7864324
  37.9 24.3 %copy-start.1 = (bf16[2,5,256,128]{3,2,1,0:T(8,128)(2,1)}, bf16[2,5,256,128]{3,2,1,0:T(8,128)(2,1)S(1)}, u32[]{:S(2)}) copy-start(bf16[2,5,256,128]{3,2,1,0:T(8,128)(2,1)S(1)} %fresh.1.refs_6_) | copy-start | bytes 1966084
  45.5 24.8 %collective-permute-start.3 = (bf16[2,5,288,128]{3,2,1,0:T(8,128)(2,1)}, bf16[2,5,288,128]{3,2,1,0:T(8,128)(2,1)}, u32[]{:S(2)}, u32[]{:S(2)}) collective-permute-start(bf16[2,5,288,128]{3,2,1,0:T(8,128)(2,1)} %collective-permute-done.1.refs_1_), channel_id=1, source_target_pairs={{8,16},{12,20},{16,8},{20,12},{9,17},{13,21},{17,9},{21,13},{10,18... | collective-permute-start | bytes 2211848 | tf_op jit(solution)/shard_map/ppermute | solution.py:455
  47.0 23.2 %collective-permute-start.4 = (bf16[2,5,288,128]{3,2,1,0:T(8,128)(2,1)}, bf16[2,5,288,128]{3,2,1,0:T(8,128)(2,1)}, u32[]{:S(2)}, u32[]{:S(2)}) collective-permute-start(bf16[2,5,288,128]{3,2,1,0:T(8,128)(2,1)} %collective-permute-done.2.refs_2_), channel_id=1, source_target_pairs={{8,0},{12,4},{16,24},{20,28},{9,1},{13,5},{17,25},{21,29},{10,2},{... | collective-permute-start | bytes 2211848 | tf_op jit(solution)/shard_map/ppermute | solution.py:455
  48.3 17.7 %collective-permute-start.5 = (bf16[2,5,256,128]{3,2,1,0:T(8,128)(2,1)S(1)}, bf16[2,5,256,128]{3,2,1,0:T(8,128)(2,1)}, u32[]{:S(2)}, u32[]{:S(2)}) collective-permute-start(bf16[2,5,256,128]{3,2,1,0:T(8,128)(2,1)S(1)} %fresh.1.refs_6_), channel_id=1, source_target_pairs={{0,4},{4,0},{8,12},{12,8},{16,20},{20,16},{24,28},{28,24},{1,5},{5... | collective-permute-start | bytes 1966088 | tf_op jit(solution)/shard_map/ppermute | solution.py:367
  57.0 13.2 %copy-start.9 = (s32[3,16]{1,0:T(4,128)S(1)}, s32[3,16]{1,0:T(4,128)}, u32[]{:S(2)}) copy-start(s32[3,16]{1,0:T(4,128)} %copy-done.8) | copy-start | bytes 580
  57.0 13.2 %all-to-all-start.2 = ((bf16[8,96,128]{2,1,0:T(8,128)(2,1)}), bf16[8,96,128]{2,1,0:T(8,128)(2,1)S(1)}, u32[]{:S(2)}, u32[]{:S(2)}) async-start(bf16[8,96,128]{2,1,0:T(8,128)(2,1)} %attend_row.1), calls=%async_computation.2 | async-start | bytes 393216 | tf_op jit(solution)/shard_map/all_to_all | solution.py:371
  62.2 27.9 %collective-permute-start.8 = (bf16[320,2048]{1,0:T(8,128)(2,1)}, bf16[320,2048]{1,0:T(8,128)(2,1)}, u32[]{:S(2)}, u32[]{:S(2)}) collective-permute-start(bf16[320,2048]{1,0:T(8,128)(2,1)} %w_a.1), channel_id=1, source_target_pairs={{0,1},{1,0},{2,3},{3,2},{4,5},{5,4},{6,7},{7,6},{8,9},{9,8},{10,11... | collective-permute-start | bytes 3932168 | tf_op jit(solution)/shard_map/ppermute | solution.py:367
  65.1 0.9 copy-start.3
  71.6 14.2 %all-to-all-start.3 = ((bf16[8,2,96,128]{3,2,1,0:T(8,128)(2,1)}), bf16[8,2,96,128]{3,2,1,0:T(8,128)(2,1)S(1)}, u32[]{:S(2)}, u32[]{:S(2)}) async-start(bf16[8,2,96,128]{3,2,1,0:T(8,128)(2,1)} %bitcast.10), calls=%async_computation.3 | async-start | bytes 786432 | tf_op jit(solution)/shard_map/all_to_all | solution.py:371
  75.1 23.6 %collective-permute-start.11 = (bf16[320,2048]{1,0:T(8,128)(2,1)}, bf16[320,2048]{1,0:T(8,128)(2,1)}, u32[]{:S(2)}, u32[]{:S(2)}) collective-permute-start(bf16[320,2048]{1,0:T(8,128)(2,1)} %collective-permute-done.10.w_a), channel_id=1, source_target_pairs={{0,1},{1,0},{2,3},{3,2},{4,5},{5,4},{6,7},{7,6},{8,9},{9,8},{10,11... | collective-permute-start | bytes 3932168 | tf_op jit(solution)/shard_map/ppermute | solution.py:367
  75.1 29.8 %collective-permute-start.12 = (bf16[2,5,288,128]{3,2,1,0:T(8,128)(2,1)}, bf16[2,5,288,128]{3,2,1,0:T(8,128)(2,1)}, u32[]{:S(2)}, u32[]{:S(2)}) collective-permute-start(bf16[2,5,288,128]{3,2,1,0:T(8,128)(2,1)} %collective-permute-done.3.refs_3_), channel_id=1, source_target_pairs={{8,0},{12,4},{16,24},{20,28},{9,1},{13,5},{17,25},{21,29},{10,2},{... | collective-permute-start | bytes 2211848 | tf_op jit(solution)/shard_map/ppermute | solution.py:455
  85.8 1.1 %copy-start.4 = (f32[2,3,256,128]{3,2,1,0:T(8,128)S(1)}, f32[2,3,256,128]{3,2,1,0:T(8,128)}, u32[]{:S(2)}) copy-start(f32[2,3,256,128]{3,2,1,0:T(8,128)} %copy-done.3) | copy-start | bytes 2359300
  86.9 3.3 %copy-start.7 = (bf16[320,2048]{1,0:T(8,128)(2,1)S(1)}, bf16[320,2048]{1,0:T(8,128)(2,1)}, u32[]{:S(2)}) copy-start(bf16[320,2048]{1,0:T(8,128)(2,1)} %w_a.1) | copy-start | bytes 3932164
  88.5 1.7 %collective-permute-start.7 = (bf16[2,640,128]{2,1,0:T(8,128)(2,1)S(1)}, bf16[2,640,128]{2,1,0:T(8,128)(2,1)S(1)}, u32[]{:S(2)}, u32[]{:S(2)}) collective-permute-start(bf16[2,640,128]{2,1,0:T(8,128)(2,1)S(1)} %merge.1.m_a), channel_id=1, source_target_pairs={{0,1},{1,0},{2,3},{3,2},{4,5},{5,4},{6,7},{7,6},{8,9},{9,8},{10,11... | collective-permute-start | bytes 983048 | tf_op jit(solution)/shard_map/ppermute | solution.py:367
  88.5 10.1 %collective-permute-start.6 = (bf16[2,640,128]{2,1,0:T(8,128)(2,1)S(1)}, bf16[2,640,128]{2,1,0:T(8,128)(2,1)S(1)}, u32[]{:S(2)}, u32[]{:S(2)}) collective-permute-start(bf16[2,640,128]{2,1,0:T(8,128)(2,1)S(1)} %merge.1.m_a), channel_id=1, source_target_pairs={{0,2},{1,3},{2,0},{3,1},{4,6},{5,7},{6,4},{7,5},{8,10},{9,11},{10,... | collective-permute-start | bytes 983048 | tf_op jit(solution)/shard_map/ppermute | solution.py:367
  98.7 1.6 %collective-permute-start.9 = (bf16[2,640,128]{2,1,0:T(8,128)(2,1)S(1)}, bf16[2,640,128]{2,1,0:T(8,128)(2,1)S(1)}, u32[]{:S(2)}, u32[]{:S(2)}) collective-permute-start(bf16[2,640,128]{2,1,0:T(8,128)(2,1)S(1)} %collective-permute-done.6.m_a), channel_id=1, source_target_pairs={{0,1},{1,0},{2,3},{3,2},{4,5},{5,4},{6,7},{7,6},{8,9},{9,8},{10,11... | collective-permute-start | bytes 983048 | tf_op jit(solution)/shard_map/ppermute | solution.py:367

commit v4 on v3

--- a/solution.py
+++ b/solution.py
@@ -209,17 +209,11 @@
     each(requests, step)
 
 
-def row_kernel(requests, count, heads, groups, chunk, meta, q, stored, out, kv_sc, sem):
-    span, kv_heads = kv_sc.shape[1], stored.shape[1]
+def row_kernel(requests, count, heads, groups, chunk, meta, q, pair, out):
+    span = pair.shape[1]
     offset = lax.axis_index("tp") * heads
     first = offset // groups
 
-    def fetch(number):
-        source = stored.at[0, jnp.minimum(first + number, kv_heads - 1)]
-        return pltpu.make_async_copy(source, kv_sc.at[number], sem.at[number])
-
-    fetch(0).start()
-    fetch(1).start()
     row = lax.axis_index("req")
 
     def find(r, length):
@@ -234,9 +228,7 @@
     level = jnp.zeros((count, LANES), F32)
     kept = []
     for head in range(heads):
-        if head < 2:
-            fetch(head).wait()
-        kv = kv_sc[(offset + head) // groups - first]
+        kv = pair[(offset + head) // groups - first]
         scores = lax.dot_general(
             tiles[head], kv, (((1,), (1,)), ((), ())), preferred_element_type=F32
         )
@@ -311,7 +303,7 @@
     return jnp.where(apart < 2, apart, jnp.where(mid, 5 - apart, 2 + apart))
 
 
-def cache_kernel(req_dev, span, meta, *refs):
+def cache_kernel(req_dev, span, steps, meta, *refs):
     blocks, (mine, theirs, _, out, kept_sc, out_sc, sem, out_sem) = refs[:-8], refs[-8:]
     place, tp_place = lax.axis_index("req"), lax.axis_index("tp")
     side = place % 2
@@ -320,29 +312,36 @@
     start = (side * lax.axis_size("tp") + tp_place) * segment
     skip = pl.multiple_of(start - jnp.minimum(start, span - segment), 16)
     first = (place // 2) * 2 * req_dev
-
-    def fetch(number, action):
-        row = jnp.where(live(meta, first + number), meta[1, first + number], 0)
-        plane, which = row // 2, (row % 2) ^ side
+    numbers = range(2 * req_dev)
+    found = []
+    for number in numbers:
+        row = jnp.where(live(meta, first + number), meta[1, first + number], place)
+        step = 0 if len(blocks[0].shape) == 5 else held(row // 2, place // 2)
+        found.append((row // 2, (row % 2) ^ side, step))
+
+    def here(number, action):
+        wanted = functools.reduce(jnp.logical_or, [found[number][2] == step for step in steps])
+        pl.when(wanted)(action)
+
+    def fetch(number):
+        plane, which, step = found[number]
         dst = kept_sc.at[number, :, pl.ds(0, segment), :]
-        if len(blocks) == 1:
-            action(pltpu.make_async_copy(blocks[0].at[plane, which], dst, sem.at[number]))
+        if len(blocks[0].shape) == 5:
+            pltpu.make_async_copy(blocks[0].at[plane, which], dst, sem.at[number]).start()
             return
-        for step, block in enumerate(blocks):
-
-            @pl.when(held(plane, place // 2) == step)
+        for step_of, block in zip(steps, blocks):
+
+            @pl.when(step == step_of)
             def _():
-                action(pltpu.make_async_copy(block.at[which], dst, sem.at[number]))
+                pltpu.make_async_copy(block.at[which], dst, sem.at[number]).start()
 
     def write(number):
         return pltpu.make_async_copy(out_sc.at[number], out.at[number], out_sem.at[number])
 
-    for number in range(2 * req_dev):
-        fetch(number, lambda copy: copy.start())
-    rows = lax.broadcasted_iota(jnp.int32, (segment, count), 0)
-    cols = lax.broadcasted_iota(jnp.int32, (segment, count), 1)
-    for number in range(2 * req_dev):
+    def fill(number):
         ahead = live_length(meta, first + number) - start
+        rows = lax.broadcasted_iota(jnp.int32, (segment, count), 0)
+        cols = lax.broadcasted_iota(jnp.int32, (segment, count), 1)
         shift = jnp.where(rows - cols == ahead, 1.0, 0.0).astype(BF16)
         local = number // req_dev == side
         place_of = number % req_dev
@@ -352,14 +351,20 @@
         )
         moved = jnp.dot(shift, new, preferred_element_type=F32)
         old = lax.broadcasted_iota(jnp.int32, (segment, LANES), 0) < ahead
-        fetch(number, lambda copy: copy.wait())
+        dst = kept_sc.at[number, :, pl.ds(0, segment), :]
+        pltpu.make_async_copy(dst, dst, sem.at[number]).wait()
         for head in range(kv_heads):
             kept = kept_sc[number, head, pl.ds(skip, segment), :].astype(F32)
             part = moved[:, head * LANES : head * LANES + LANES]
             out_sc[number, head] = jnp.where(old, kept, part).astype(BF16)
         write(number).start()
-    for number in range(2 * req_dev):
-        write(number).wait()
+
+    for number in numbers:
+        fetch(number)
+    for number in numbers:
+        here(number, functools.partial(fill, number))
+    for number in numbers:
+        here(number, lambda number=number: write(number).wait())
 
 
 def permuted(value, axis, mask):
@@ -419,12 +424,11 @@
     side = lax.axis_index("req") % 2
     tp_place = lax.axis_index("tp")
 
-    def part(which):
+    def part(source, which):
         start = (which * tp_count + tp_place) * segment
-        return lax.dynamic_slice_in_dim(stored[0], start, segment, 1)
-
-    own_part, other_part = part(side), part(1 - side)
-    partner_part = permuted(other_part, "req", 1)
+        return lax.dynamic_slice_in_dim(source[0], start, segment, 1)
+
+    partner_part = permuted(part(stored, 1 - side), "req", 1)
     q = pl.pallas_call(
         functools.partial(query_kernel, req_dev, q_chunk),
         grid=(req_dev,),
@@ -445,8 +449,8 @@
     )(continuing, cache_len, tokens, gain_row, w_query_rows, q_gain_row, table)
     q_mid = exchanged(q).reshape(requests, q_chunk, LANES)
 
-    partner_part = lax.optimization_barrier((partner_part, q))[0]
-    both = jnp.stack([own_part, partner_part])
+    partner_part, later = lax.optimization_barrier((partner_part, stored, q))[:2]
+    both = jnp.stack([part(later, side), partner_part])
     planes = n_req // 2
     hops = planes == 4
 
@@ -467,6 +471,8 @@
     w_c = permuted(w_out, "tp", 1)
     w_xc = permuted(w_x, "tp", 1)
 
+    later = lax.optimization_barrier((stored, q_mid))[0]
+    pair = lax.dynamic_slice_in_dim(later[0], tp_place * heads // groups, 2, 0)
     fresh = pl.pallas_call(
         functools.partial(fresh_kernel, req_dev),
         grid=(req_dev,),
@@ -484,7 +490,7 @@
         compiler_params=params(),
         cost_estimate=HINT,
         name="fresh",
-    )(meta, tokens, gain_row, key_value_weight, k_gain_row, table, q)
+    )(meta, tokens, gain_row, key_value_weight, k_gain_row, table, pair)
 
     q_out = pl.pallas_call(
         functools.partial(route_query_kernel, requests),
@@ -518,22 +524,39 @@
     far = pl.pallas_call(
         functools.partial(row_kernel, requests, count, heads, groups, o_chunk),
         out_shape=jax.ShapeDtypeStruct((n_req, o_chunk, LANES), BF16),
-        in_specs=[SMEM, vmem_spec, any_spec],
+        in_specs=[SMEM, vmem_spec, vmem_spec],
         out_specs=vmem_spec,
-        scratch_shapes=[
-            pltpu.VMEM((2, span, LANES), BF16),
-            pltpu.SemaphoreType.DMA((2,)),
-        ],
-        compiler_params=params(60),
+        compiler_params=params(40),
         cost_estimate=cost(4 * heads * count * span * 256, 32 << 20),
         name="attend_row",
-    )(meta, q_row, stored)
+    )(meta, q_row, pair)
 
     far_mid = exchanged(far)
     if hops:
         far_mid = lax.optimization_barrier((far_mid, far_middle, outward, fresh_partner, near))[0]
         far_outward = crossed(far_middle, [(1, 0), (2, 3)])
         blocks = [both, beside, middle, far_middle, outward, far_outward]
+    def fill_cache(steps, blocks, after, aliases):
+        return pl.pallas_call(
+            functools.partial(cache_kernel, req_dev, span, steps),
+            in_specs=[SMEM] + [any_spec] * len(blocks) + [vmem_spec, vmem_spec, any_spec],
+            out_specs=any_spec,
+            scratch_shapes=[
+                pltpu.VMEM((2 * req_dev, kv_heads, 2 * segment, LANES), BF16),
+                pltpu.VMEM((2 * req_dev, kv_heads, segment, LANES), BF16),
+                pltpu.SemaphoreType.DMA((2 * req_dev,)),
+                pltpu.SemaphoreType.DMA((2 * req_dev,)),
+            ],
+            out_shape=jax.ShapeDtypeStruct((2 * req_dev, kv_heads, segment, LANES), BF16),
+            input_output_aliases=aliases,
+            compiler_params=params(),
+            cost_estimate=HINT,
+            name="cache",
+        )(meta, *blocks, fresh, fresh_partner, after)
+
+    if hops:
+        cache = fill_cache(tuple(range(5)), blocks[:5], far_mid, {})
+
     far_out = pl.pallas_call(
         functools.partial(route_result_kernel, requests),
         out_shape=jax.ShapeDtypeStruct((requests, o_chunk, LANES), BF16),
@@ -544,6 +567,8 @@
         name="route_result",
     )(meta, far_mid)
     far_home = exchanged(far_out.reshape(n_req, req_dev, o_chunk, LANES))
+    if hops:
+        far_home = lax.optimization_barrier((far_home, cache))[0]
 
     mixed = pl.pallas_call(
         functools.partial(merge_kernel, req_dev),
@@ -582,21 +607,10 @@
     m_xc = permuted(m_x, "tp", 1)
     layer = project(m_x, m_xc, w_x, w_xc, partial, BF16, "project_rest")
 
-    cache = pl.pallas_call(
-        functools.partial(cache_kernel, req_dev, span),
-        in_specs=[SMEM] + [any_spec] * len(blocks) + [vmem_spec, vmem_spec, any_spec],
-        out_specs=any_spec,
-        scratch_shapes=[
-            pltpu.VMEM((2 * req_dev, kv_heads, 2 * segment, LANES), BF16),
-            pltpu.VMEM((2 * req_dev, kv_heads, segment, LANES), BF16),
-            pltpu.SemaphoreType.DMA((2 * req_dev,)),
-            pltpu.SemaphoreType.DMA((2 * req_dev,)),
-        ],
-        out_shape=jax.ShapeDtypeStruct((2 * req_dev, kv_heads, segment, LANES), BF16),
-        compiler_params=params(60),
-        cost_estimate=HINT,
-        name="cache",
-    )(meta, *blocks, fresh, fresh_partner, layer)
+    if hops:
+        cache = fill_cache((5,), [far_outward], cache, {4: 0})
+    else:
+        cache = fill_cache((0,), blocks, layer, {})
     return (layer, cache)
 
 

time: 110 us -> 108 us (0.982)
  waiting for transfers between devices: 31.2 us -> 19.3 us
  local copies, waits for them, and re-layouts: 5.68 us -> 14.3 us
  starting transfers between devices: 33.1 us -> 34.8 us
    unnamed x26 -> x34, local copies, waits for them, and re-layouts: 3.79 us -> 14.1 us
    all_to_all x4, waiting for transfers between devices: 24.3 us -> 15.7 us  [exchanged(): return lax.all_to_all(value, 'req', split_axis=0, concat_axis=0, tiled=True)]
    ppermute x8, waiting for transfers between devices: 6.9 us -> 3.25 us  [permuted(): return lax.ppermute(value, axis, pairs)]
    pallas_call x1 -> x2, Pallas kernels: 4.35 us -> 6.98 us  [fill_cache(): pl.pallas_call(functools.partial(cache_kernel, req_dev, span, steps), in_...]
    pallas_call x1, Pallas kernels: 7.43 us -> 5.18 us  [on_device(): pl.pallas_call(functools.partial(row_kernel, requests, count, heads, grou...]
    dynamic_slice x1 -> x3, local copies, waits for them, and re-layouts: 1.9 us -> 0.13 us  [the longest x1 0.07 us: on_device(): pair = lax.dynamic_slice_in_dim(later[0], tp_place * heads // groups, 2, 0)]
    ppermute x5, starting transfers between devices: 7.84 us -> 9.57 us  [crossed(): return lax.ppermute(value, 'req', pairs)]
  transfers between devices with their start and end apart: 17 -> 17, of which waited for: 7 -> 6; matrix products, arithmetic and copies ran while one was open for 2% -> 2% of each run, Pallas kernels for 29% -> 29%
where the time goes in v4:
time: 108 us
  Pallas kernels  36.3 us (34%)
  starting transfers between devices  34.8 us (32%)
  waiting for transfers between devices  19.3 us (18%)
  local copies, waits for them, and re-layouts  14.3 us (13%)
  other arithmetic  1.96 us (2%)
    all_to_all x4, starting transfers between devices, exchanged(): return lax.all_to_all(value, 'req', split_axis=0, concat_axis=0, tiled=True)  17.7 us
    all_to_all x4, waiting for transfers between devices, exchanged(): return lax.all_to_all(value, 'req', split_axis=0, concat_axis=0, tiled=True)  15.7 us
    unnamed x34, local copies, waits for them, and re-layouts  14.1 us
    ppermute x5, starting transfers between devices, crossed(): return lax.ppermute(value, 'req', pairs)  9.57 us
    pallas_call x2, Pallas kernels, project(): pl.pallas_call(functools.partial(project_kernel, 512), grid=(req_dev,), o...  8.4 us
    ppermute x8, starting transfers between devices, permuted(): return lax.ppermute(value, axis, pairs)  7.55 us
    pallas_call x2, Pallas kernels, fill_cache(): pl.pallas_call(functools.partial(cache_kernel, req_dev, span, steps), in_...  6.98 us
    pallas_call x1, Pallas kernels, on_device(): pl.pallas_call(functools.partial(row_kernel, requests, count, heads, grou...  5.18 us
  transfers between devices with their start and end apart: 17, of which 6 were waited for; matrix products, arithmetic and copies ran while one was open for 2% of the time, Pallas kernels for 29%

profile of v4, /device:TPU:0, one launch (start us, length us, event | category | flops | bytes accessed | tf_op | source)
XLA Modules:
  0.0 107.5 jit_solution(10000108671965202742)
XLA Ops:
  0.7 1.7 %copy-done = bf16[1,5,2048,128]{3,2,1,0:T(8,128)(2,1)S(1)} copy-done((bf16[1,5,2048,128]{3,2,1,0:T(8,128)(2,1)S(1)}, bf16[1,5,2048,128]{3,2,1,0:T(8,128)(2,1)}, u32[]{:S(2)}) %copy-start) | copy-done | bytes 2621464
  2.4 3.0 %collective-permute-start = (bf16[5,288,128]{2,1,0:T(8,128)(2,1)S(1)}, bf16[5,288,128]{2,1,0:T(8,128)(2,1)}, u32[]{:S(2)}, u32[]{:S(2)}) collective-permute-start(bf16[5,288,128]{2,1,0:T(8,128)(2,1)S(1)} %dynamic-slice_bitcast_fusion.1), channel_id=1, source_target_pairs={{0,4},{4,0},{8,12},{12,8},{16,20},{20,16},{24,28},{28,24},{1,5},{5... | collective-permute-start | bytes 1105928 | tf_op jit(solution)/shard_map/ppermute | solution.py:372
  5.4 5.1 %query.1.q = bf16[8,2,80,128]{3,2,1,0:T(8,128)(2,1)} custom-call(s32[16]{0:T(128)} %cont.1, s32[16]{0:T(128)} %clen.1, bf16[2,256,2048]{2,1,0:T(8,128)(2,1)} %base.1, f32[1,2048]{1,0:T(1,128)} %bitcast.16, bf16[320,2048]{1,0:T(8,128)(2,1)} %bitcast.19, f32[1,64]{1,0:T(1,128)} %bitcast.22, f32[2,408,128]{2,1,0:T(8,128)} %constant.49.clone.table), custom_call_target="tpu_custom_call" | custom-call | flops 805306368 | bytes 6291456 | tf_op jit(solution)/shard_map/query/pallas_call | solution.py:432
  10.5 5.0 %all-to-all-start = ((bf16[8,2,80,128]{3,2,1,0:T(8,128)(2,1)}), bf16[8,2,80,128]{3,2,1,0:T(8,128)(2,1)S(1)}, u32[]{:S(2)}, u32[]{:S(2)}) async-start(bf16[8,2,80,128]{3,2,1,0:T(8,128)(2,1)} %query.1.q), calls=%async_computation | async-start | bytes 655360 | tf_op jit(solution)/shard_map/all_to_all | solution.py:376
  15.6 1.9 %pad_maximum_fusion.refs_0_ = bf16[2,5,288,128]{3,2,1,0:T(8,128)(2,1)} fusion(bf16[1,5,288,128]{3,2,1,0:T(8,128)(2,1)} %bitcast.8, bf16[1,5,288,128]{3,2,1,0:T(8,128)(2,1)S(1)} %constant_dynamic-slice_fusion), kind=kLoop, calls=%fused_computation.1 | loop fusion | flops 368640 | bytes 1474560 | tf_op jit(solution)/shard_map/stack | solution.py:453
  17.6 1.5 %collective-permute-start.2 = (bf16[2,5,288,128]{3,2,1,0:T(8,128)(2,1)}, bf16[2,5,288,128]{3,2,1,0:T(8,128)(2,1)}, u32[]{:S(2)}, u32[]{:S(2)}) collective-permute-start(bf16[2,5,288,128]{3,2,1,0:T(8,128)(2,1)} %pad_maximum_fusion.refs_0_), channel_id=1, source_target_pairs={{8,16},{12,20},{16,8},{20,12},{9,17},{13,21},{17,9},{21,13},{10,18... | collective-permute-start | bytes 2211848 | tf_op jit(solution)/shard_map/ppermute | solution.py:459
  19.1 3.9 %collective-permute-start.1 = (bf16[2,5,288,128]{3,2,1,0:T(8,128)(2,1)}, bf16[2,5,288,128]{3,2,1,0:T(8,128)(2,1)}, u32[]{:S(2)}, u32[]{:S(2)}) collective-permute-start(bf16[2,5,288,128]{3,2,1,0:T(8,128)(2,1)} %pad_maximum_fusion.refs_0_), channel_id=1, source_target_pairs={{0,8},{4,12},{8,0},{12,4},{16,24},{20,28},{24,16},{28,20},{1,9},{5... | collective-permute-start | bytes 2211848 | tf_op jit(solution)/shard_map/ppermute | solution.py:459
  23.0 1.5 %collective-permute-start.10 = (bf16[320,2048]{1,0:T(8,128)(2,1)}, bf16[320,2048]{1,0:T(8,128)(2,1)}, u32[]{:S(2)}, u32[]{:S(2)}) collective-permute-start(bf16[320,2048]{1,0:T(8,128)(2,1)} %w_a.1), channel_id=1, source_target_pairs={{0,2},{1,3},{2,0},{3,1},{4,6},{5,7},{6,4},{7,5},{8,10},{9,11},{10,... | collective-permute-start | bytes 3932168 | tf_op jit(solution)/shard_map/ppermute | solution.py:372
  24.5 2.4 %all-to-all-done = bf16[8,2,80,128]{3,2,1,0:T(8,128)(2,1)S(1)} async-done(((bf16[8,2,80,128]{3,2,1,0:T(8,128)(2,1)}), bf16[8,2,80,128]{3,2,1,0:T(8,128)(2,1)S(1)}, u32[]{:S(2)}, u32[]{:S(2)}) %all-to-all-start) | async-done | bytes 327712 | tf_op jit(solution)/shard_map/all_to_all | solution.py:376
  26.9 1.4 %route_query.1 = bf16[8,80,128]{2,1,0:T(8,128)(2,1)} custom-call(s32[3,16]{1,0:T(4,128)S(1)} %pad_add_fusion.meta, bf16[16,80,128]{2,1,0:T(8,128)(2,1)S(1)} %bitcast.15), custom_call_target="tpu_custom_call" | custom-call | bytes 1048576 | tf_op jit(solution)/shard_map/route_query/pallas_call | solution.py:495
  28.3 3.4 %all-to-all-start.1 = ((bf16[8,80,128]{2,1,0:T(8,128)(2,1)}), bf16[8,80,128]{2,1,0:T(8,128)(2,1)S(1)}, u32[]{:S(2)}, u32[]{:S(2)}) async-start(bf16[8,80,128]{2,1,0:T(8,128)(2,1)} %route_query.1), calls=%async_computation.1 | async-start | bytes 327680 | tf_op jit(solution)/shard_map/all_to_all | solution.py:376
  31.8 1.5 %copy-done.1 = bf16[2,256,2048]{2,1,0:T(8,128)(2,1)S(1)} copy-done((bf16[2,256,2048]{2,1,0:T(8,128)(2,1)S(1)}, bf16[2,256,2048]{2,1,0:T(8,128)(2,1)}, u32[]{:S(2)}) %copy-start.1) | copy-done | bytes 2097176
  33.3 1.7 %copy-done.8 = bf16[2048,640]{1,0:T(8,128)(2,1)S(1)} copy-done((bf16[2048,640]{1,0:T(8,128)(2,1)S(1)}, bf16[2048,640]{1,0:T(8,128)(2,1)}, u32[]{:S(2)}) %copy-start.8) | copy-done | bytes 2621464
  36.0 3.9 %fresh.1.refs_5_.refs_1_ = bf16[2,5,256,128]{3,2,1,0:T(8,128)(2,1)S(1)} custom-call(s32[3,16]{1,0:T(4,128)S(1)} %pad_add_fusion.meta, bf16[2,256,2048]{2,1,0:T(8,128)(2,1)S(1)} %copy-done.1, f32[1,2048]{1,0:T(1,128)S(1)} %bitcast.17, bf16[2048,640]{1,0:T(8,128)(2,1)S(1)} %copy-done.8, f32[1,64]{1,0:T(1,128)S(1)} %bitcast.18, f32[2,408,128]{2,1,0:T(8,128)S(1)} %copy-done.9, ...), custom_call_target="tpu_custom_call" | custom-call | bytes 1024 | tf_op jit(solution)/shard_map/fresh/pallas_call | solution.py:476
  40.9 4.2 %all-to-all-done.1.q = bf16[8,80,128]{2,1,0:T(8,128)(2,1)S(1)} async-done(((bf16[8,80,128]{2,1,0:T(8,128)(2,1)}), bf16[8,80,128]{2,1,0:T(8,128)(2,1)S(1)}, u32[]{:S(2)}, u32[]{:S(2)}) %all-to-all-start.1) | async-done | bytes 163872 | tf_op jit(solution)/shard_map/all_to_all | solution.py:376
  45.1 1.6 %collective-permute-start.3 = (bf16[2,5,288,128]{3,2,1,0:T(8,128)(2,1)}, bf16[2,5,288,128]{3,2,1,0:T(8,128)(2,1)}, u32[]{:S(2)}, u32[]{:S(2)}) collective-permute-start(bf16[2,5,288,128]{3,2,1,0:T(8,128)(2,1)} %collective-permute-done.1.refs_1_), channel_id=1, source_target_pairs={{8,16},{12,20},{16,8},{20,12},{9,17},{13,21},{17,9},{21,13},{10,18... | collective-permute-start | bytes 2211848 | tf_op jit(solution)/shard_map/ppermute | solution.py:459
  48.0 1.3 %collective-permute-start.5 = (bf16[2,5,256,128]{3,2,1,0:T(8,128)(2,1)S(1)}, bf16[2,5,256,128]{3,2,1,0:T(8,128)(2,1)}, u32[]{:S(2)}, u32[]{:S(2)}) collective-permute-start(bf16[2,5,256,128]{3,2,1,0:T(8,128)(2,1)S(1)} %fresh.1.refs_5_.refs_1_), channel_id=1, source_target_pairs={{0,4},{4,0},{8,12},{12,8},{16,20},{20,16},{24,28},{28,24},{1,5},{5... | collective-permute-start | bytes 1966088 | tf_op jit(solution)/shard_map/ppermute | solution.py:372
  50.5 5.2 %attend_row.1 = bf16[8,96,128]{2,1,0:T(8,128)(2,1)S(1)} custom-call(s32[3,16]{1,0:T(4,128)S(1)} %pad_add_fusion.meta, bf16[8,80,128]{2,1,0:T(8,128)(2,1)S(1)} %all-to-all-done.1.q, bf16[2,2048,128]{2,1,0:T(8,128)(2,1)S(1)} %copy-done.4), custom_call_target="tpu_custom_call" | custom-call | flops 2684354560 | bytes 33554432 | tf_op jit(solution)/shard_map/attend_row/pallas_call | solution.py:524
  56.4 5.2 %all-to-all-start.2 = ((bf16[8,96,128]{2,1,0:T(8,128)(2,1)}), bf16[8,96,128]{2,1,0:T(8,128)(2,1)S(1)}, u32[]{:S(2)}, u32[]{:S(2)}) async-start(bf16[8,96,128]{2,1,0:T(8,128)(2,1)} %copy-done.11), calls=%async_computation.2 | async-start | bytes 393216 | tf_op jit(solution)/shard_map/all_to_all | solution.py:376
  62.6 2.8 %attend_new.1.near = f32[2,3,256,128]{3,2,1,0:T(8,128)S(1)} custom-call(bf16[8,2,80,128]{3,2,1,0:T(8,128)(2,1)S(1)} %copy-done.7, bf16[2,5,256,128]{3,2,1,0:T(8,128)(2,1)S(1)} %fresh.1.refs_5_.refs_1_), custom_call_target="tpu_custom_call" | custom-call | bytes 1024 | tf_op jit(solution)/shard_map/attend_new/pallas_call | solution.py:510
  66.3 3.2 %all-to-all-done.2.src.refs_7_ = bf16[8,96,128]{2,1,0:T(8,128)(2,1)S(1)} async-done(((bf16[8,96,128]{2,1,0:T(8,128)(2,1)}), bf16[8,96,128]{2,1,0:T(8,128)(2,1)S(1)}, u32[]{:S(2)}, u32[]{:S(2)}) %all-to-all-start.2) | async-done | bytes 196640 | tf_op jit(solution)/shard_map/all_to_all | solution.py:376
  70.9 4.1 %all-to-all-start.3 = ((bf16[8,2,96,128]{3,2,1,0:T(8,128)(2,1)}), bf16[8,2,96,128]{3,2,1,0:T(8,128)(2,1)}, u32[]{:S(2)}, u32[]{:S(2)}) async-start(bf16[8,2,96,128]{3,2,1,0:T(8,128)(2,1)} %bitcast.14), calls=%async_computation.3 | async-start | bytes 786432 | tf_op jit(solution)/shard_map/all_to_all | solution.py:376
  75.1 1.3 %collective-permute-start.12 = (bf16[2,5,288,128]{3,2,1,0:T(8,128)(2,1)}, bf16[2,5,288,128]{3,2,1,0:T(8,128)(2,1)}, u32[]{:S(2)}, u32[]{:S(2)}) collective-permute-start(bf16[2,5,288,128]{3,2,1,0:T(8,128)(2,1)} %collective-permute-done.3.refs_3_), channel_id=1, source_target_pairs={{8,0},{12,4},{16,24},{20,28},{9,1},{13,5},{17,25},{21,29},{10,2},{... | collective-permute-start | bytes 2211848 | tf_op jit(solution)/shard_map/ppermute | solution.py:459
  76.4 4.0 %cache.2.refs_3_ = bf16[4,5,288,128]{3,2,1,0:T(8,128)(2,1)} custom-call(s32[3,16]{1,0:T(4,128)S(1)} %pad_add_fusion.meta, bf16[2,5,288,128]{3,2,1,0:T(8,128)(2,1)} %pad_maximum_fusion.refs_0_, bf16[2,5,288,128]{3,2,1,0:T(8,128)(2,1)} %collective-permute-done.1.refs_1_, bf16[2,5,288,128]{3,2,1,0:T(8,128)(2,1)} %collective-permute-done.2.refs_2_, ...), custom_call_target="tpu_custom_call" | custom-call | bytes 1024 | tf_op jit(solution)/shard_map/cache/pallas_call | solution.py:540
  80.3 5.8 %all-to-all-done.3.far = bf16[8,2,96,128]{3,2,1,0:T(8,128)(2,1)} async-done(((bf16[8,2,96,128]{3,2,1,0:T(8,128)(2,1)}), bf16[8,2,96,128]{3,2,1,0:T(8,128)(2,1)}, u32[]{:S(2)}, u32[]{:S(2)}) %all-to-all-start.3) | async-done | bytes 393248 | tf_op jit(solution)/shard_map/all_to_all | solution.py:376
  87.3 1.9 %merge.1.m_a = bf16[2,640,128]{2,1,0:T(8,128)(2,1)S(1)} custom-call(s32[3,16]{1,0:T(4,128)S(1)} %pad_add_fusion.meta, bf16[8,2,96,128]{3,2,1,0:T(8,128)(2,1)} %all-to-all-done.3.far, f32[2,3,256,128]{3,2,1,0:T(8,128)S(1)} %copy-done.6), custom_call_target="tpu_custom_call" | custom-call | bytes 1024 | tf_op jit(solution)/shard_map/merge/pallas_call | solution.py:573
  89.3 1.6 %collective-permute-start.6 = (bf16[2,640,128]{2,1,0:T(8,128)(2,1)S(1)}, bf16[2,640,128]{2,1,0:T(8,128)(2,1)S(1)}, u32[]{:S(2)}, u32[]{:S(2)}) collective-permute-start(bf16[2,640,128]{2,1,0:T(8,128)(2,1)S(1)} %merge.1.m_a), channel_id=1, source_target_pairs={{0,2},{1,3},{2,0},{3,1},{4,6},{5,7},{6,4},{7,5},{8,10},{9,11},{10,... | collective-permute-start | bytes 983048 | tf_op jit(solution)/shard_map/ppermute | solution.py:372
  90.9 1.6 %copy-done.2 = bf16[2,256,2048]{2,1,0:T(8,128)(2,1)S(1)} copy-done((bf16[2,256,2048]{2,1,0:T(8,128)(2,1)S(1)}, bf16[2,256,2048]{2,1,0:T(8,128)(2,1)}, u32[]{:S(2)}) %copy-start.2) | copy-done | bytes 2097176
  92.5 3.7 %project_chip.1.base = f32[2,256,2048]{2,1,0:T(8,128)S(1)} custom-call(bf16[2,640,128]{2,1,0:T(8,128)(2,1)S(1)} %merge.1.m_a, bf16[2,640,128]{2,1,0:T(8,128)(2,1)S(1)} %collective-permute-done.7.m_b, bf16[320,2048]{1,0:T(8,128)(2,1)} %w_a.1, bf16[320,2048]{1,0:T(8,128)(2,1)} %collective-permute-done.8.w_b, bf16[2,256,2048]{2,1,0:T(8,128)(2,1)S(1)} %copy-done.2), custom_call_target="tpu_custom_call" | custom-call | bytes 1024 | tf_op jit(solution)/shard_map/project_chip/pallas_call | solution.py:593
  96.2 3.2 %collective-permute-done.6.m_a = bf16[2,640,128]{2,1,0:T(8,128)(2,1)S(1)} collective-permute-done((bf16[2,640,128]{2,1,0:T(8,128)(2,1)S(1)}, bf16[2,640,128]{2,1,0:T(8,128)(2,1)S(1)}, u32[]{:S(2)}, u32[]{:S(2)}) %collective-permute-start.6) | collective-permute-done | bytes 327712 | tf_op jit(solution)/shard_map/ppermute | solution.py:372
  99.8 3.0 %cache.3 = bf16[4,5,288,128]{3,2,1,0:T(8,128)(2,1)} custom-call(s32[3,16]{1,0:T(4,128)S(1)} %pad_add_fusion.meta, bf16[2,5,288,128]{3,2,1,0:T(8,128)(2,1)} %collective-permute-done.12.refs_0_, bf16[2,5,256,128]{3,2,1,0:T(8,128)(2,1)S(1)} %fresh.1.refs_5_.refs_1_, ...), custom_call_target="tpu_custom_call", output_to_operand_aliasing={{}: (4, {})} | custom-call | bytes 1024 | tf_op jit(solution)/shard_map/cache/pallas_call | solution.py:540
  102.8 4.7 %project_rest.1 = bf16[2,256,2048]{2,1,0:T(8,128)(2,1)} custom-call(bf16[2,640,128]{2,1,0:T(8,128)(2,1)S(1)} %collective-permute-done.6.m_a, bf16[2,640,128]{2,1,0:T(8,128)(2,1)S(1)} %collective-permute-done.9.m_b, bf16[320,2048]{1,0:T(8,128)(2,1)} %collective-permute-done.10.w_a, bf16[320,2048]{1,0:T(8,128)(2,1)} %collective-permute-done.11.w_b, ...), custom_call_target="tpu_custom_call" | custom-call | bytes 1024 | tf_op jit(solution)/shard_map/project_rest/pallas_call | solution.py:593
  (52 shorter events, 10.2 us)
Async XLA Ops:
  0.6 1.7 %copy-start = (bf16[1,5,2048,128]{3,2,1,0:T(8,128)(2,1)S(1)}, bf16[1,5,2048,128]{3,2,1,0:T(8,128)(2,1)}, u32[]{:S(2)}) copy-start(bf16[1,5,2048,128]{3,2,1,0:T(8,128)(2,1)} %param.19) | copy-start | bytes 7864324
  2.4 13.2 %collective-permute-start = (bf16[5,288,128]{2,1,0:T(8,128)(2,1)S(1)}, bf16[5,288,128]{2,1,0:T(8,128)(2,1)}, u32[]{:S(2)}, u32[]{:S(2)}) collective-permute-start(bf16[5,288,128]{2,1,0:T(8,128)(2,1)S(1)} %dynamic-slice_bitcast_fusion.1), channel_id=1, source_target_pairs={{0,4},{4,0},{8,12},{12,8},{16,20},{20,16},{24,28},{28,24},{1,5},{5... | collective-permute-start | bytes 1105928 | tf_op jit(solution)/shard_map/ppermute | solution.py:372
  10.5 14.0 %copy-start.14 = (s32[16]{0:T(128)S(1)}, s32[16]{0:T(128)}, u32[]{:S(2)}) copy-start(s32[16]{0:T(128)} %clen.1) | copy-start | bytes 196
  10.5 14.0 %copy-start.15 = (s32[16]{0:T(128)S(1)}, s32[16]{0:T(128)}, u32[]{:S(2)}) copy-start(s32[16]{0:T(128)} %cont.1) | copy-start | bytes 196
  10.5 14.0 %copy-start.16 = (s32[16]{0:T(128)S(1)}, s32[16]{0:T(128)}, u32[]{:S(2)}) copy-start(s32[16]{0:T(128)} %param.21) | copy-start | bytes 196
  10.5 16.3 %all-to-all-start = ((bf16[8,2,80,128]{3,2,1,0:T(8,128)(2,1)}), bf16[8,2,80,128]{3,2,1,0:T(8,128)(2,1)S(1)}, u32[]{:S(2)}, u32[]{:S(2)}) async-start(bf16[8,2,80,128]{3,2,1,0:T(8,128)(2,1)} %query.1.q), calls=%async_computation | async-start | bytes 655360 | tf_op jit(solution)/shard_map/all_to_all | solution.py:376
  15.6 16.2 %copy-start.12 = (f32[2048]{0:T(1024)S(1)}, f32[2048]{0:T(1024)}, u32[]{:S(2)}) copy-start(f32[2048]{0:T(1024)} %param.13) | copy-start | bytes 24580
  15.6 16.2 %copy-start.13 = (f32[64]{0:T(128)S(1)}, f32[64]{0:T(128)}, u32[]{:S(2)}) copy-start(f32[64]{0:T(128)} %param.18) | copy-start | bytes 772
  17.6 27.5 %collective-permute-start.2 = (bf16[2,5,288,128]{3,2,1,0:T(8,128)(2,1)}, bf16[2,5,288,128]{3,2,1,0:T(8,128)(2,1)}, u32[]{:S(2)}, u32[]{:S(2)}) collective-permute-start(bf16[2,5,288,128]{3,2,1,0:T(8,128)(2,1)} %pad_maximum_fusion.refs_0_), channel_id=1, source_target_pairs={{8,16},{12,20},{16,8},{20,12},{9,17},{13,21},{17,9},{21,13},{10,18... | collective-permute-start | bytes 2211848 | tf_op jit(solution)/shard_map/ppermute | solution.py:459
  19.1 26.0 %collective-permute-start.1 = (bf16[2,5,288,128]{3,2,1,0:T(8,128)(2,1)}, bf16[2,5,288,128]{3,2,1,0:T(8,128)(2,1)}, u32[]{:S(2)}, u32[]{:S(2)}) collective-permute-start(bf16[2,5,288,128]{3,2,1,0:T(8,128)(2,1)} %pad_maximum_fusion.refs_0_), channel_id=1, source_target_pairs={{0,8},{4,12},{8,0},{12,4},{16,24},{20,28},{24,16},{28,20},{1,9},{5... | collective-permute-start | bytes 2211848 | tf_op jit(solution)/shard_map/ppermute | solution.py:459
  23.0 51.9 %collective-permute-start.10 = (bf16[320,2048]{1,0:T(8,128)(2,1)}, bf16[320,2048]{1,0:T(8,128)(2,1)}, u32[]{:S(2)}, u32[]{:S(2)}) collective-permute-start(bf16[320,2048]{1,0:T(8,128)(2,1)} %w_a.1), channel_id=1, source_target_pairs={{0,2},{1,3},{2,0},{3,1},{4,6},{5,7},{6,4},{7,5},{8,10},{9,11},{10,... | collective-permute-start | bytes 3932168 | tf_op jit(solution)/shard_map/ppermute | solution.py:372
  28.3 16.9 %all-to-all-start.1 = ((bf16[8,80,128]{2,1,0:T(8,128)(2,1)}), bf16[8,80,128]{2,1,0:T(8,128)(2,1)S(1)}, u32[]{:S(2)}, u32[]{:S(2)}) async-start(bf16[8,80,128]{2,1,0:T(8,128)(2,1)} %route_query.1), calls=%async_computation.1 | async-start | bytes 327680 | tf_op jit(solution)/shard_map/all_to_all | solution.py:376
  31.7 1.6 %copy-start.1 = (bf16[2,256,2048]{2,1,0:T(8,128)(2,1)S(1)}, bf16[2,256,2048]{2,1,0:T(8,128)(2,1)}, u32[]{:S(2)}) copy-start(bf16[2,256,2048]{2,1,0:T(8,128)(2,1)} %base.1) | copy-start | bytes 6291460
  33.3 1.7 %copy-start.8 = (bf16[2048,640]{1,0:T(8,128)(2,1)S(1)}, bf16[2048,640]{1,0:T(8,128)(2,1)}, u32[]{:S(2)}) copy-start(bf16[2048,640]{1,0:T(8,128)(2,1)} %w.1) | copy-start | bytes 7864324
  35.0 1.0 copy-start.9
  39.9 1.0 copy-start.3
  45.1 24.4 %collective-permute-start.3 = (bf16[2,5,288,128]{3,2,1,0:T(8,128)(2,1)}, bf16[2,5,288,128]{3,2,1,0:T(8,128)(2,1)}, u32[]{:S(2)}, u32[]{:S(2)}) collective-permute-start(bf16[2,5,288,128]{3,2,1,0:T(8,128)(2,1)} %collective-permute-done.1.refs_1_), channel_id=1, source_target_pairs={{8,16},{12,20},{16,8},{20,12},{9,17},{13,21},{17,9},{21,13},{10,18... | collective-permute-start | bytes 2211848 | tf_op jit(solution)/shard_map/ppermute | solution.py:459
  46.7 22.8 %collective-permute-start.4 = (bf16[2,5,288,128]{3,2,1,0:T(8,128)(2,1)}, bf16[2,5,288,128]{3,2,1,0:T(8,128)(2,1)}, u32[]{:S(2)}, u32[]{:S(2)}) collective-permute-start(bf16[2,5,288,128]{3,2,1,0:T(8,128)(2,1)} %collective-permute-done.2.refs_2_), channel_id=1, source_target_pairs={{8,0},{12,4},{16,24},{20,28},{9,1},{13,5},{17,25},{21,29},{10,2},{... | collective-permute-start | bytes 2211848 | tf_op jit(solution)/shard_map/ppermute | solution.py:459
  48.0 18.3 %collective-permute-start.5 = (bf16[2,5,256,128]{3,2,1,0:T(8,128)(2,1)S(1)}, bf16[2,5,256,128]{3,2,1,0:T(8,128)(2,1)}, u32[]{:S(2)}, u32[]{:S(2)}) collective-permute-start(bf16[2,5,256,128]{3,2,1,0:T(8,128)(2,1)S(1)} %fresh.1.refs_5_.refs_1_), channel_id=1, source_target_pairs={{0,4},{4,0},{8,12},{12,8},{16,20},{20,16},{24,28},{28,24},{1,5},{5... | collective-permute-start | bytes 1966088 | tf_op jit(solution)/shard_map/ppermute | solution.py:372
  49.3 1.2 %copy-start.4 = (bf16[2,2048,128]{2,1,0:T(8,128)(2,1)S(1)}, bf16[2,2048,128]{2,1,0:T(8,128)(2,1)}, u32[]{:S(2)}) copy-start(bf16[2,2048,128]{2,1,0:T(8,128)(2,1)} %copy-done.3) | copy-start | bytes 3145732
  56.4 13.1 %all-to-all-start.2 = ((bf16[8,96,128]{2,1,0:T(8,128)(2,1)}), bf16[8,96,128]{2,1,0:T(8,128)(2,1)S(1)}, u32[]{:S(2)}, u32[]{:S(2)}) async-start(bf16[8,96,128]{2,1,0:T(8,128)(2,1)} %copy-done.11), calls=%async_computation.2 | async-start | bytes 393216 | tf_op jit(solution)/shard_map/all_to_all | solution.py:376
  61.6 29.3 %collective-permute-start.8 = (bf16[320,2048]{1,0:T(8,128)(2,1)}, bf16[320,2048]{1,0:T(8,128)(2,1)}, u32[]{:S(2)}, u32[]{:S(2)}) collective-permute-start(bf16[320,2048]{1,0:T(8,128)(2,1)} %w_a.1), channel_id=1, source_target_pairs={{0,1},{1,0},{2,3},{3,2},{4,5},{5,4},{6,7},{7,6},{8,9},{9,8},{10,11... | collective-permute-start | bytes 3932168 | tf_op jit(solution)/shard_map/ppermute | solution.py:372
  61.6 1.0 copy-start.7
  65.4 0.9 copy-start.5
  70.9 15.3 %all-to-all-start.3 = ((bf16[8,2,96,128]{3,2,1,0:T(8,128)(2,1)}), bf16[8,2,96,128]{3,2,1,0:T(8,128)(2,1)}, u32[]{:S(2)}, u32[]{:S(2)}) async-start(bf16[8,2,96,128]{3,2,1,0:T(8,128)(2,1)} %bitcast.14), calls=%async_computation.3 | async-start | bytes 786432 | tf_op jit(solution)/shard_map/all_to_all | solution.py:376
  75.0 27.8 %collective-permute-start.11 = (bf16[320,2048]{1,0:T(8,128)(2,1)}, bf16[320,2048]{1,0:T(8,128)(2,1)}, u32[]{:S(2)}, u32[]{:S(2)}) collective-permute-start(bf16[320,2048]{1,0:T(8,128)(2,1)} %collective-permute-done.10.w_a), channel_id=1, source_target_pairs={{0,1},{1,0},{2,3},{3,2},{4,5},{5,4},{6,7},{7,6},{8,9},{9,8},{10,11... | collective-permute-start | bytes 3932168 | tf_op jit(solution)/shard_map/ppermute | solution.py:372
  75.1 24.7 %collective-permute-start.12 = (bf16[2,5,288,128]{3,2,1,0:T(8,128)(2,1)}, bf16[2,5,288,128]{3,2,1,0:T(8,128)(2,1)}, u32[]{:S(2)}, u32[]{:S(2)}) collective-permute-start(bf16[2,5,288,128]{3,2,1,0:T(8,128)(2,1)} %collective-permute-done.3.refs_3_), channel_id=1, source_target_pairs={{8,0},{12,4},{16,24},{20,28},{9,1},{13,5},{17,25},{21,29},{10,2},{... | collective-permute-start | bytes 2211848 | tf_op jit(solution)/shard_map/ppermute | solution.py:459
  86.2 1.1 %copy-start.6 = (f32[2,3,256,128]{3,2,1,0:T(8,128)S(1)}, f32[2,3,256,128]{3,2,1,0:T(8,128)}, u32[]{:S(2)}) copy-start(f32[2,3,256,128]{3,2,1,0:T(8,128)} %copy-done.5) | copy-start | bytes 2359300
  89.2 1.7 %collective-permute-start.7 = (bf16[2,640,128]{2,1,0:T(8,128)(2,1)S(1)}, bf16[2,640,128]{2,1,0:T(8,128)(2,1)S(1)}, u32[]{:S(2)}, u32[]{:S(2)}) collective-permute-start(bf16[2,640,128]{2,1,0:T(8,128)(2,1)S(1)} %merge.1.m_a), channel_id=1, source_target_pairs={{0,1},{1,0},{2,3},{3,2},{4,5},{5,4},{6,7},{7,6},{8,9},{9,8},{10,11... | collective-permute-start | bytes 983048 | tf_op jit(solution)/shard_map/ppermute | solution.py:372
  89.3 10.1 %collective-permute-start.6 = (bf16[2,640,128]{2,1,0:T(8,128)(2,1)S(1)}, bf16[2,640,128]{2,1,0:T(8,128)(2,1)S(1)}, u32[]{:S(2)}, u32[]{:S(2)}) collective-permute-start(bf16[2,640,128]{2,1,0:T(8,128)(2,1)S(1)} %merge.1.m_a), channel_id=1, source_target_pairs={{0,2},{1,3},{2,0},{3,1},{4,6},{5,7},{6,4},{7,5},{8,10},{9,11},{10,... | collective-permute-start | bytes 983048 | tf_op jit(solution)/shard_map/ppermute | solution.py:372
  90.9 1.6 %copy-start.2 = (bf16[2,256,2048]{2,1,0:T(8,128)(2,1)S(1)}, bf16[2,256,2048]{2,1,0:T(8,128)(2,1)}, u32[]{:S(2)}) copy-start(bf16[2,256,2048]{2,1,0:T(8,128)(2,1)} %base.1) | copy-start | bytes 6291460
  99.4 3.4 %collective-permute-start.9 = (bf16[2,640,128]{2,1,0:T(8,128)(2,1)S(1)}, bf16[2,640,128]{2,1,0:T(8,128)(2,1)S(1)}, u32[]{:S(2)}, u32[]{:S(2)}) collective-permute-start(bf16[2,640,128]{2,1,0:T(8,128)(2,1)S(1)} %collective-permute-done.6.m_a), channel_id=1, source_target_pairs={{0,1},{1,0},{2,3},{3,2},{4,5},{5,4},{6,7},{7,6},{8,9},{9,8},{10,11... | collective-permute-start | bytes 983048 | tf_op jit(solution)/shard_map/ppermute | solution.py:372
  (2 other events, 1.4 us)

commit v5 on v4

--- a/solution.py
+++ b/solution.py
@@ -504,7 +504,7 @@
     q_row, beside, middle, _ = lax.optimization_barrier((exchanged(q_out), beside, middle, fresh))
     if hops:
         far_middle = crossed(beside, [(1, 2), (2, 1)])
-        outward = crossed(middle, [(1, 0), (2, 3)])
+        outward = crossed(middle, outer)
     fresh_partner = permuted(fresh, "req", 1)
 
     near = pl.pallas_call(
@@ -534,7 +534,7 @@
     far_mid = exchanged(far)
     if hops:
         far_mid = lax.optimization_barrier((far_mid, far_middle, outward, fresh_partner, near))[0]
-        far_outward = crossed(far_middle, [(1, 0), (2, 3)])
+        far_outward = crossed(far_middle, outer)
         blocks = [both, beside, middle, far_middle, outward, far_outward]
     def fill_cache(steps, blocks, after, aliases):
         return pl.pallas_call(

time: 108 us -> 107 us (level)
  Pallas kernels: 36.3 us -> 34.7 us
    pallas_call x2, Pallas kernels: 6.98 us -> 5.42 us  [fill_cache(): pl.pallas_call(functools.partial(cache_kernel, req_dev, span, steps), in_...]
    ppermute x5, starting transfers between devices: 9.57 us -> 10.9 us  [crossed(): return lax.ppermute(value, 'req', pairs)]
  transfers between devices with their start and end apart: 17 -> 17, of which waited for: 6 -> 7; matrix products, arithmetic and copies ran while one was open for 2% -> 2% of each run, Pallas kernels for 29% -> 28%
where the time goes in v5:
time: 107 us; the launch traced here: 105 us
  starting transfers between devices  34.7 us (32%)
  Pallas kernels  34.7 us (32%)
  waiting for transfers between devices  19 us (18%)
  local copies, waits for them, and re-layouts  14.3 us (13%)
  other arithmetic  1.96 us (2%)
    all_to_all x4, starting transfers between devices, exchanged(): return lax.all_to_all(value, 'req', split_axis=0, concat_axis=0, tiled=True)  17.3 us
    all_to_all x4, waiting for transfers between devices, exchanged(): return lax.all_to_all(value, 'req', split_axis=0, concat_axis=0, tiled=True)  15.3 us
    unnamed x34, local copies, waits for them, and re-layouts  14.1 us
    ppermute x5, starting transfers between devices, crossed(): return lax.ppermute(value, 'req', pairs)  10.9 us
    pallas_call x2, Pallas kernels, project(): pl.pallas_call(functools.partial(project_kernel, 512), grid=(req_dev,), o...  8.37 us
    ppermute x8, starting transfers between devices, permuted(): return lax.ppermute(value, axis, pairs)  6.56 us
    pallas_call x2, Pallas kernels, fill_cache(): pl.pallas_call(functools.partial(cache_kernel, req_dev, span, steps), in_...  5.42 us
    pallas_call x1, Pallas kernels, on_device(): pl.pallas_call(functools.partial(row_kernel, requests, count, heads, grou...  5.18 us
  transfers between devices with their start and end apart: 17, of which 7 were waited for; matrix products, arithmetic and copies ran while one was open for 2% of the time, Pallas kernels for 28%

profile of v5, /device:TPU:0, one launch (start us, length us, event | category | flops | bytes accessed | tf_op | source)
XLA Modules:
  0.0 105.5 jit_solution(16985334105617343954)
XLA Ops:
  0.7 1.7 %copy-done = bf16[1,5,2048,128]{3,2,1,0:T(8,128)(2,1)S(1)} copy-done((bf16[1,5,2048,128]{3,2,1,0:T(8,128)(2,1)S(1)}, bf16[1,5,2048,128]{3,2,1,0:T(8,128)(2,1)}, u32[]{:S(2)}) %copy-start) | copy-done | bytes 2621464
  2.4 3.0 %collective-permute-start = (bf16[5,288,128]{2,1,0:T(8,128)(2,1)S(1)}, bf16[5,288,128]{2,1,0:T(8,128)(2,1)}, u32[]{:S(2)}, u32[]{:S(2)}) collective-permute-start(bf16[5,288,128]{2,1,0:T(8,128)(2,1)S(1)} %dynamic-slice_bitcast_fusion.1), channel_id=1, source_target_pairs={{0,4},{4,0},{8,12},{12,8},{16,20},{20,16},{24,28},{28,24},{1,5},{5... | collective-permute-start | bytes 1105928 | tf_op jit(solution)/shard_map/ppermute | solution.py:372
  5.4 5.1 %query.1.q = bf16[8,2,80,128]{3,2,1,0:T(8,128)(2,1)} custom-call(s32[16]{0:T(128)} %cont.1, s32[16]{0:T(128)} %clen.1, bf16[2,256,2048]{2,1,0:T(8,128)(2,1)} %base.1, f32[1,2048]{1,0:T(1,128)} %bitcast.16, bf16[320,2048]{1,0:T(8,128)(2,1)} %bitcast.19, f32[1,64]{1,0:T(1,128)} %bitcast.22, f32[2,408,128]{2,1,0:T(8,128)} %constant.49.clone.table), custom_call_target="tpu_custom_call" | custom-call | flops 805306368 | bytes 6291456 | tf_op jit(solution)/shard_map/query/pallas_call | solution.py:432
  10.5 5.0 %all-to-all-start = ((bf16[8,2,80,128]{3,2,1,0:T(8,128)(2,1)}), bf16[8,2,80,128]{3,2,1,0:T(8,128)(2,1)S(1)}, u32[]{:S(2)}, u32[]{:S(2)}) async-start(bf16[8,2,80,128]{3,2,1,0:T(8,128)(2,1)} %query.1.q), calls=%async_computation | async-start | bytes 655360 | tf_op jit(solution)/shard_map/all_to_all | solution.py:376
  15.6 1.9 %pad_maximum_fusion.refs_0_ = bf16[2,5,288,128]{3,2,1,0:T(8,128)(2,1)} fusion(bf16[1,5,288,128]{3,2,1,0:T(8,128)(2,1)} %bitcast.8, bf16[1,5,288,128]{3,2,1,0:T(8,128)(2,1)S(1)} %constant_dynamic-slice_fusion), kind=kLoop, calls=%fused_computation.1 | loop fusion | flops 368640 | bytes 1474560 | tf_op jit(solution)/shard_map/stack | solution.py:453
  17.6 1.5 %collective-permute-start.2 = (bf16[2,5,288,128]{3,2,1,0:T(8,128)(2,1)}, bf16[2,5,288,128]{3,2,1,0:T(8,128)(2,1)}, u32[]{:S(2)}, u32[]{:S(2)}) collective-permute-start(bf16[2,5,288,128]{3,2,1,0:T(8,128)(2,1)} %pad_maximum_fusion.refs_0_), channel_id=1, source_target_pairs={{8,16},{12,20},{16,8},{20,12},{9,17},{13,21},{17,9},{21,13},{10,18... | collective-permute-start | bytes 2211848 | tf_op jit(solution)/shard_map/ppermute | solution.py:459
  19.1 3.9 %collective-permute-start.1 = (bf16[2,5,288,128]{3,2,1,0:T(8,128)(2,1)}, bf16[2,5,288,128]{3,2,1,0:T(8,128)(2,1)}, u32[]{:S(2)}, u32[]{:S(2)}) collective-permute-start(bf16[2,5,288,128]{3,2,1,0:T(8,128)(2,1)} %pad_maximum_fusion.refs_0_), channel_id=1, source_target_pairs={{0,8},{4,12},{8,0},{12,4},{16,24},{20,28},{24,16},{28,20},{1,9},{5... | collective-permute-start | bytes 2211848 | tf_op jit(solution)/shard_map/ppermute | solution.py:459
  23.0 1.5 %collective-permute-start.10 = (bf16[320,2048]{1,0:T(8,128)(2,1)}, bf16[320,2048]{1,0:T(8,128)(2,1)}, u32[]{:S(2)}, u32[]{:S(2)}) collective-permute-start(bf16[320,2048]{1,0:T(8,128)(2,1)} %w_a.1), channel_id=1, source_target_pairs={{0,2},{1,3},{2,0},{3,1},{4,6},{5,7},{6,4},{7,5},{8,10},{9,11},{10,... | collective-permute-start | bytes 3932168 | tf_op jit(solution)/shard_map/ppermute | solution.py:372
  24.5 2.4 %all-to-all-done = bf16[8,2,80,128]{3,2,1,0:T(8,128)(2,1)S(1)} async-done(((bf16[8,2,80,128]{3,2,1,0:T(8,128)(2,1)}), bf16[8,2,80,128]{3,2,1,0:T(8,128)(2,1)S(1)}, u32[]{:S(2)}, u32[]{:S(2)}) %all-to-all-start) | async-done | bytes 327712 | tf_op jit(solution)/shard_map/all_to_all | solution.py:376
  26.9 1.4 %route_query.1 = bf16[8,80,128]{2,1,0:T(8,128)(2,1)} custom-call(s32[3,16]{1,0:T(4,128)S(1)} %pad_add_fusion.meta, bf16[16,80,128]{2,1,0:T(8,128)(2,1)S(1)} %bitcast.15), custom_call_target="tpu_custom_call" | custom-call | bytes 1048576 | tf_op jit(solution)/shard_map/route_query/pallas_call | solution.py:495
  28.3 3.4 %all-to-all-start.1 = ((bf16[8,80,128]{2,1,0:T(8,128)(2,1)}), bf16[8,80,128]{2,1,0:T(8,128)(2,1)S(1)}, u32[]{:S(2)}, u32[]{:S(2)}) async-start(bf16[8,80,128]{2,1,0:T(8,128)(2,1)} %route_query.1), calls=%async_computation.1 | async-start | bytes 327680 | tf_op jit(solution)/shard_map/all_to_all | solution.py:376
  31.8 1.5 %copy-done.1 = bf16[2,256,2048]{2,1,0:T(8,128)(2,1)S(1)} copy-done((bf16[2,256,2048]{2,1,0:T(8,128)(2,1)S(1)}, bf16[2,256,2048]{2,1,0:T(8,128)(2,1)}, u32[]{:S(2)}) %copy-start.1) | copy-done | bytes 2097176
  33.3 1.7 %copy-done.8 = bf16[2048,640]{1,0:T(8,128)(2,1)S(1)} copy-done((bf16[2048,640]{1,0:T(8,128)(2,1)S(1)}, bf16[2048,640]{1,0:T(8,128)(2,1)}, u32[]{:S(2)}) %copy-start.8) | copy-done | bytes 2621464
  36.0 3.9 %fresh.1.refs_5_.refs_1_ = bf16[2,5,256,128]{3,2,1,0:T(8,128)(2,1)S(1)} custom-call(s32[3,16]{1,0:T(4,128)S(1)} %pad_add_fusion.meta, bf16[2,256,2048]{2,1,0:T(8,128)(2,1)S(1)} %copy-done.1, f32[1,2048]{1,0:T(1,128)S(1)} %bitcast.17, bf16[2048,640]{1,0:T(8,128)(2,1)S(1)} %copy-done.8, f32[1,64]{1,0:T(1,128)S(1)} %bitcast.18, f32[2,408,128]{2,1,0:T(8,128)S(1)} %copy-done.9, ...), custom_call_target="tpu_custom_call" | custom-call | bytes 1024 | tf_op jit(solution)/shard_map/fresh/pallas_call | solution.py:476
  40.9 4.2 %all-to-all-done.1.q = bf16[8,80,128]{2,1,0:T(8,128)(2,1)S(1)} async-done(((bf16[8,80,128]{2,1,0:T(8,128)(2,1)}), bf16[8,80,128]{2,1,0:T(8,128)(2,1)S(1)}, u32[]{:S(2)}, u32[]{:S(2)}) %all-to-all-start.1) | async-done | bytes 163872 | tf_op jit(solution)/shard_map/all_to_all | solution.py:376
  45.1 1.6 %collective-permute-start.3 = (bf16[2,5,288,128]{3,2,1,0:T(8,128)(2,1)}, bf16[2,5,288,128]{3,2,1,0:T(8,128)(2,1)}, u32[]{:S(2)}, u32[]{:S(2)}) collective-permute-start(bf16[2,5,288,128]{3,2,1,0:T(8,128)(2,1)} %collective-permute-done.1.refs_1_), channel_id=1, source_target_pairs={{8,16},{12,20},{16,8},{20,12},{9,17},{13,21},{17,9},{21,13},{10,18... | collective-permute-start | bytes 2211848 | tf_op jit(solution)/shard_map/ppermute | solution.py:459
  46.7 2.0 %collective-permute-start.4 = (bf16[2,5,288,128]{3,2,1,0:T(8,128)(2,1)}, bf16[2,5,288,128]{3,2,1,0:T(8,128)(2,1)}, u32[]{:S(2)}, u32[]{:S(2)}) collective-permute-start(bf16[2,5,288,128]{3,2,1,0:T(8,128)(2,1)} %collective-permute-done.2.refs_2_), channel_id=1, source_target_pairs={{0,8},{4,12},{8,0},{12,4},{16,24},{20,28},{24,16},{28,20},{1,9},{5... | collective-permute-start | bytes 2211848 | tf_op jit(solution)/shard_map/ppermute | solution.py:459
  50.2 5.2 %attend_row.1 = bf16[8,96,128]{2,1,0:T(8,128)(2,1)S(1)} custom-call(s32[3,16]{1,0:T(4,128)S(1)} %pad_add_fusion.meta, bf16[8,80,128]{2,1,0:T(8,128)(2,1)S(1)} %all-to-all-done.1.q, bf16[2,2048,128]{2,1,0:T(8,128)(2,1)S(1)} %copy-done.4), custom_call_target="tpu_custom_call" | custom-call | flops 2684354560 | bytes 33554432 | tf_op jit(solution)/shard_map/attend_row/pallas_call | solution.py:524
  56.1 4.8 %all-to-all-start.2 = ((bf16[8,96,128]{2,1,0:T(8,128)(2,1)}), bf16[8,96,128]{2,1,0:T(8,128)(2,1)S(1)}, u32[]{:S(2)}, u32[]{:S(2)}) async-start(bf16[8,96,128]{2,1,0:T(8,128)(2,1)} %copy-done.11), calls=%async_computation.2 | async-start | bytes 393216 | tf_op jit(solution)/shard_map/all_to_all | solution.py:376
  61.8 2.8 %attend_new.1.near = f32[2,3,256,128]{3,2,1,0:T(8,128)S(1)} custom-call(bf16[8,2,80,128]{3,2,1,0:T(8,128)(2,1)S(1)} %copy-done.7, bf16[2,5,256,128]{3,2,1,0:T(8,128)(2,1)S(1)} %fresh.1.refs_5_.refs_1_), custom_call_target="tpu_custom_call" | custom-call | bytes 1024 | tf_op jit(solution)/shard_map/attend_new/pallas_call | solution.py:510
  65.6 3.1 %all-to-all-done.2.src.refs_7_ = bf16[8,96,128]{2,1,0:T(8,128)(2,1)S(1)} async-done(((bf16[8,96,128]{2,1,0:T(8,128)(2,1)}), bf16[8,96,128]{2,1,0:T(8,128)(2,1)S(1)}, u32[]{:S(2)}, u32[]{:S(2)}) %all-to-all-start.2) | async-done | bytes 196640 | tf_op jit(solution)/shard_map/all_to_all | solution.py:376
  70.0 4.1 %all-to-all-start.3 = ((bf16[8,2,96,128]{3,2,1,0:T(8,128)(2,1)}), bf16[8,2,96,128]{3,2,1,0:T(8,128)(2,1)}, u32[]{:S(2)}, u32[]{:S(2)}) async-start(bf16[8,2,96,128]{3,2,1,0:T(8,128)(2,1)} %bitcast.14), calls=%async_computation.3 | async-start | bytes 786432 | tf_op jit(solution)/shard_map/all_to_all | solution.py:376
  74.2 1.9 %collective-permute-start.12 = (bf16[2,5,288,128]{3,2,1,0:T(8,128)(2,1)}, bf16[2,5,288,128]{3,2,1,0:T(8,128)(2,1)}, u32[]{:S(2)}, u32[]{:S(2)}) collective-permute-start(bf16[2,5,288,128]{3,2,1,0:T(8,128)(2,1)} %collective-permute-done.3.refs_3_), channel_id=1, source_target_pairs={{0,8},{4,12},{8,0},{12,4},{16,24},{20,28},{24,16},{28,20},{1,9},{5... | collective-permute-start | bytes 2211848 | tf_op jit(solution)/shard_map/ppermute | solution.py:459
  76.1 4.2 %cache.2.refs_3_ = bf16[4,5,288,128]{3,2,1,0:T(8,128)(2,1)} custom-call(s32[3,16]{1,0:T(4,128)S(1)} %pad_add_fusion.meta, bf16[2,5,288,128]{3,2,1,0:T(8,128)(2,1)} %pad_maximum_fusion.refs_0_, bf16[2,5,288,128]{3,2,1,0:T(8,128)(2,1)} %collective-permute-done.1.refs_1_, bf16[2,5,288,128]{3,2,1,0:T(8,128)(2,1)} %collective-permute-done.2.refs_2_, ...), custom_call_target="tpu_custom_call" | custom-call | bytes 1024 | tf_op jit(solution)/shard_map/cache/pallas_call | solution.py:540
  80.3 5.7 %all-to-all-done.3.far = bf16[8,2,96,128]{3,2,1,0:T(8,128)(2,1)} async-done(((bf16[8,2,96,128]{3,2,1,0:T(8,128)(2,1)}), bf16[8,2,96,128]{3,2,1,0:T(8,128)(2,1)}, u32[]{:S(2)}, u32[]{:S(2)}) %all-to-all-start.3) | async-done | bytes 393248 | tf_op jit(solution)/shard_map/all_to_all | solution.py:376
  87.1 1.9 %merge.1.m_a = bf16[2,640,128]{2,1,0:T(8,128)(2,1)S(1)} custom-call(s32[3,16]{1,0:T(4,128)S(1)} %pad_add_fusion.meta, bf16[8,2,96,128]{3,2,1,0:T(8,128)(2,1)} %all-to-all-done.3.far, f32[2,3,256,128]{3,2,1,0:T(8,128)S(1)} %copy-done.6), custom_call_target="tpu_custom_call" | custom-call | bytes 1024 | tf_op jit(solution)/shard_map/merge/pallas_call | solution.py:573
  89.0 1.5 %collective-permute-start.6 = (bf16[2,640,128]{2,1,0:T(8,128)(2,1)S(1)}, bf16[2,640,128]{2,1,0:T(8,128)(2,1)S(1)}, u32[]{:S(2)}, u32[]{:S(2)}) collective-permute-start(bf16[2,640,128]{2,1,0:T(8,128)(2,1)S(1)} %merge.1.m_a), channel_id=1, source_target_pairs={{0,2},{1,3},{2,0},{3,1},{4,6},{5,7},{6,4},{7,5},{8,10},{9,11},{10,... | collective-permute-start | bytes 983048 | tf_op jit(solution)/shard_map/ppermute | solution.py:372
  90.7 1.6 %copy-done.2 = bf16[2,256,2048]{2,1,0:T(8,128)(2,1)S(1)} copy-done((bf16[2,256,2048]{2,1,0:T(8,128)(2,1)S(1)}, bf16[2,256,2048]{2,1,0:T(8,128)(2,1)}, u32[]{:S(2)}) %copy-start.2) | copy-done | bytes 2097176
  92.2 3.7 %project_chip.1.base = f32[2,256,2048]{2,1,0:T(8,128)S(1)} custom-call(bf16[2,640,128]{2,1,0:T(8,128)(2,1)S(1)} %merge.1.m_a, bf16[2,640,128]{2,1,0:T(8,128)(2,1)S(1)} %collective-permute-done.7.m_b, bf16[320,2048]{1,0:T(8,128)(2,1)} %w_a.1, bf16[320,2048]{1,0:T(8,128)(2,1)} %collective-permute-done.8.w_b, bf16[2,256,2048]{2,1,0:T(8,128)(2,1)S(1)} %copy-done.2), custom_call_target="tpu_custom_call" | custom-call | bytes 1024 | tf_op jit(solution)/shard_map/project_chip/pallas_call | solution.py:593
  96.0 3.2 %collective-permute-done.6.m_a = bf16[2,640,128]{2,1,0:T(8,128)(2,1)S(1)} collective-permute-done((bf16[2,640,128]{2,1,0:T(8,128)(2,1)S(1)}, bf16[2,640,128]{2,1,0:T(8,128)(2,1)S(1)}, u32[]{:S(2)}, u32[]{:S(2)}) %collective-permute-start.6) | collective-permute-done | bytes 327712 | tf_op jit(solution)/shard_map/ppermute | solution.py:372
  99.2 1.3 %cache.3 = bf16[4,5,288,128]{3,2,1,0:T(8,128)(2,1)} custom-call(s32[3,16]{1,0:T(4,128)S(1)} %pad_add_fusion.meta, bf16[2,5,288,128]{3,2,1,0:T(8,128)(2,1)} %collective-permute-done.12.refs_0_, bf16[2,5,256,128]{3,2,1,0:T(8,128)(2,1)S(1)} %fresh.1.refs_5_.refs_1_, ...), custom_call_target="tpu_custom_call", output_to_operand_aliasing={{}: (4, {})} | custom-call | bytes 1024 | tf_op jit(solution)/shard_map/cache/pallas_call | solution.py:540
  100.8 4.7 %project_rest.1 = bf16[2,256,2048]{2,1,0:T(8,128)(2,1)} custom-call(bf16[2,640,128]{2,1,0:T(8,128)(2,1)S(1)} %collective-permute-done.6.m_a, bf16[2,640,128]{2,1,0:T(8,128)(2,1)S(1)} %collective-permute-done.9.m_b, bf16[320,2048]{1,0:T(8,128)(2,1)} %collective-permute-done.10.w_a, bf16[320,2048]{1,0:T(8,128)(2,1)} %collective-permute-done.11.w_b, ...), custom_call_target="tpu_custom_call" | custom-call | bytes 1024 | tf_op jit(solution)/shard_map/project_rest/pallas_call | solution.py:593
  (52 shorter events, 9.3 us)
Async XLA Ops:
  0.6 1.7 %copy-start = (bf16[1,5,2048,128]{3,2,1,0:T(8,128)(2,1)S(1)}, bf16[1,5,2048,128]{3,2,1,0:T(8,128)(2,1)}, u32[]{:S(2)}) copy-start(bf16[1,5,2048,128]{3,2,1,0:T(8,128)(2,1)} %param.19) | copy-start | bytes 7864324
  2.4 13.2 %collective-permute-start = (bf16[5,288,128]{2,1,0:T(8,128)(2,1)S(1)}, bf16[5,288,128]{2,1,0:T(8,128)(2,1)}, u32[]{:S(2)}, u32[]{:S(2)}) collective-permute-start(bf16[5,288,128]{2,1,0:T(8,128)(2,1)S(1)} %dynamic-slice_bitcast_fusion.1), channel_id=1, source_target_pairs={{0,4},{4,0},{8,12},{12,8},{16,20},{20,16},{24,28},{28,24},{1,5},{5... | collective-permute-start | bytes 1105928 | tf_op jit(solution)/shard_map/ppermute | solution.py:372
  10.5 14.0 %copy-start.14 = (s32[16]{0:T(128)S(1)}, s32[16]{0:T(128)}, u32[]{:S(2)}) copy-start(s32[16]{0:T(128)} %clen.1) | copy-start | bytes 196
  10.5 14.0 %copy-start.15 = (s32[16]{0:T(128)S(1)}, s32[16]{0:T(128)}, u32[]{:S(2)}) copy-start(s32[16]{0:T(128)} %cont.1) | copy-start | bytes 196
  10.5 14.0 %copy-start.16 = (s32[16]{0:T(128)S(1)}, s32[16]{0:T(128)}, u32[]{:S(2)}) copy-start(s32[16]{0:T(128)} %param.21) | copy-start | bytes 196
  10.5 16.3 %all-to-all-start = ((bf16[8,2,80,128]{3,2,1,0:T(8,128)(2,1)}), bf16[8,2,80,128]{3,2,1,0:T(8,128)(2,1)S(1)}, u32[]{:S(2)}, u32[]{:S(2)}) async-start(bf16[8,2,80,128]{3,2,1,0:T(8,128)(2,1)} %query.1.q), calls=%async_computation | async-start | bytes 655360 | tf_op jit(solution)/shard_map/all_to_all | solution.py:376
  15.6 16.2 %copy-start.12 = (f32[2048]{0:T(1024)S(1)}, f32[2048]{0:T(1024)}, u32[]{:S(2)}) copy-start(f32[2048]{0:T(1024)} %param.13) | copy-start | bytes 24580
  15.6 16.2 %copy-start.13 = (f32[64]{0:T(128)S(1)}, f32[64]{0:T(128)}, u32[]{:S(2)}) copy-start(f32[64]{0:T(128)} %param.18) | copy-start | bytes 772
  17.6 27.5 %collective-permute-start.2 = (bf16[2,5,288,128]{3,2,1,0:T(8,128)(2,1)}, bf16[2,5,288,128]{3,2,1,0:T(8,128)(2,1)}, u32[]{:S(2)}, u32[]{:S(2)}) collective-permute-start(bf16[2,5,288,128]{3,2,1,0:T(8,128)(2,1)} %pad_maximum_fusion.refs_0_), channel_id=1, source_target_pairs={{8,16},{12,20},{16,8},{20,12},{9,17},{13,21},{17,9},{21,13},{10,18... | collective-permute-start | bytes 2211848 | tf_op jit(solution)/shard_map/ppermute | solution.py:459
  19.1 26.0 %collective-permute-start.1 = (bf16[2,5,288,128]{3,2,1,0:T(8,128)(2,1)}, bf16[2,5,288,128]{3,2,1,0:T(8,128)(2,1)}, u32[]{:S(2)}, u32[]{:S(2)}) collective-permute-start(bf16[2,5,288,128]{3,2,1,0:T(8,128)(2,1)} %pad_maximum_fusion.refs_0_), channel_id=1, source_target_pairs={{0,8},{4,12},{8,0},{12,4},{16,24},{20,28},{24,16},{28,20},{1,9},{5... | collective-permute-start | bytes 2211848 | tf_op jit(solution)/shard_map/ppermute | solution.py:459
  23.0 51.1 %collective-permute-start.10 = (bf16[320,2048]{1,0:T(8,128)(2,1)}, bf16[320,2048]{1,0:T(8,128)(2,1)}, u32[]{:S(2)}, u32[]{:S(2)}) collective-permute-start(bf16[320,2048]{1,0:T(8,128)(2,1)} %w_a.1), channel_id=1, source_target_pairs={{0,2},{1,3},{2,0},{3,1},{4,6},{5,7},{6,4},{7,5},{8,10},{9,11},{10,... | collective-permute-start | bytes 3932168 | tf_op jit(solution)/shard_map/ppermute | solution.py:372
  28.3 16.9 %all-to-all-start.1 = ((bf16[8,80,128]{2,1,0:T(8,128)(2,1)}), bf16[8,80,128]{2,1,0:T(8,128)(2,1)S(1)}, u32[]{:S(2)}, u32[]{:S(2)}) async-start(bf16[8,80,128]{2,1,0:T(8,128)(2,1)} %route_query.1), calls=%async_computation.1 | async-start | bytes 327680 | tf_op jit(solution)/shard_map/all_to_all | solution.py:376
  31.7 1.6 %copy-start.1 = (bf16[2,256,2048]{2,1,0:T(8,128)(2,1)S(1)}, bf16[2,256,2048]{2,1,0:T(8,128)(2,1)}, u32[]{:S(2)}) copy-start(bf16[2,256,2048]{2,1,0:T(8,128)(2,1)} %base.1) | copy-start | bytes 6291460
  33.3 1.7 %copy-start.8 = (bf16[2048,640]{1,0:T(8,128)(2,1)S(1)}, bf16[2048,640]{1,0:T(8,128)(2,1)}, u32[]{:S(2)}) copy-start(bf16[2048,640]{1,0:T(8,128)(2,1)} %w.1) | copy-start | bytes 7864324
  35.0 1.0 copy-start.9
  39.9 1.0 copy-start.3
  45.1 23.5 %collective-permute-start.3 = (bf16[2,5,288,128]{3,2,1,0:T(8,128)(2,1)}, bf16[2,5,288,128]{3,2,1,0:T(8,128)(2,1)}, u32[]{:S(2)}, u32[]{:S(2)}) collective-permute-start(bf16[2,5,288,128]{3,2,1,0:T(8,128)(2,1)} %collective-permute-done.1.refs_1_), channel_id=1, source_target_pairs={{8,16},{12,20},{16,8},{20,12},{9,17},{13,21},{17,9},{21,13},{10,18... | collective-permute-start | bytes 2211848 | tf_op jit(solution)/shard_map/ppermute | solution.py:459
  46.7 22.0 %collective-permute-start.4 = (bf16[2,5,288,128]{3,2,1,0:T(8,128)(2,1)}, bf16[2,5,288,128]{3,2,1,0:T(8,128)(2,1)}, u32[]{:S(2)}, u32[]{:S(2)}) collective-permute-start(bf16[2,5,288,128]{3,2,1,0:T(8,128)(2,1)} %collective-permute-done.2.refs_2_), channel_id=1, source_target_pairs={{0,8},{4,12},{8,0},{12,4},{16,24},{20,28},{24,16},{28,20},{1,9},{5... | collective-permute-start | bytes 2211848 | tf_op jit(solution)/shard_map/ppermute | solution.py:459
  48.7 16.9 %collective-permute-start.5 = (bf16[2,5,256,128]{3,2,1,0:T(8,128)(2,1)S(1)}, bf16[2,5,256,128]{3,2,1,0:T(8,128)(2,1)}, u32[]{:S(2)}, u32[]{:S(2)}) collective-permute-start(bf16[2,5,256,128]{3,2,1,0:T(8,128)(2,1)S(1)} %fresh.1.refs_5_.refs_1_), channel_id=1, source_target_pairs={{0,4},{4,0},{8,12},{12,8},{16,20},{20,16},{24,28},{28,24},{1,5},{5... | collective-permute-start | bytes 1966088 | tf_op jit(solution)/shard_map/ppermute | solution.py:372
  49.0 1.2 %copy-start.4 = (bf16[2,2048,128]{2,1,0:T(8,128)(2,1)S(1)}, bf16[2,2048,128]{2,1,0:T(8,128)(2,1)}, u32[]{:S(2)}) copy-start(bf16[2,2048,128]{2,1,0:T(8,128)(2,1)} %copy-done.3) | copy-start | bytes 3145732
  56.1 12.5 %all-to-all-start.2 = ((bf16[8,96,128]{2,1,0:T(8,128)(2,1)}), bf16[8,96,128]{2,1,0:T(8,128)(2,1)S(1)}, u32[]{:S(2)}, u32[]{:S(2)}) async-start(bf16[8,96,128]{2,1,0:T(8,128)(2,1)} %copy-done.11), calls=%async_computation.2 | async-start | bytes 393216 | tf_op jit(solution)/shard_map/all_to_all | solution.py:376
  60.9 29.7 %collective-permute-start.8 = (bf16[320,2048]{1,0:T(8,128)(2,1)}, bf16[320,2048]{1,0:T(8,128)(2,1)}, u32[]{:S(2)}, u32[]{:S(2)}) collective-permute-start(bf16[320,2048]{1,0:T(8,128)(2,1)} %w_a.1), channel_id=1, source_target_pairs={{0,1},{1,0},{2,3},{3,2},{4,5},{5,4},{6,7},{7,6},{8,9},{9,8},{10,11... | collective-permute-start | bytes 3932168 | tf_op jit(solution)/shard_map/ppermute | solution.py:372
  60.9 1.0 copy-start.7
  64.7 0.9 copy-start.5
  70.0 15.9 %all-to-all-start.3 = ((bf16[8,2,96,128]{3,2,1,0:T(8,128)(2,1)}), bf16[8,2,96,128]{3,2,1,0:T(8,128)(2,1)}, u32[]{:S(2)}, u32[]{:S(2)}) async-start(bf16[8,2,96,128]{3,2,1,0:T(8,128)(2,1)} %bitcast.14), calls=%async_computation.3 | async-start | bytes 786432 | tf_op jit(solution)/shard_map/all_to_all | solution.py:376
  74.1 26.3 %collective-permute-start.11 = (bf16[320,2048]{1,0:T(8,128)(2,1)}, bf16[320,2048]{1,0:T(8,128)(2,1)}, u32[]{:S(2)}, u32[]{:S(2)}) collective-permute-start(bf16[320,2048]{1,0:T(8,128)(2,1)} %collective-permute-done.10.w_a), channel_id=1, source_target_pairs={{0,1},{1,0},{2,3},{3,2},{4,5},{5,4},{6,7},{7,6},{8,9},{9,8},{10,11... | collective-permute-start | bytes 3932168 | tf_op jit(solution)/shard_map/ppermute | solution.py:372
  74.2 25.0 %collective-permute-start.12 = (bf16[2,5,288,128]{3,2,1,0:T(8,128)(2,1)}, bf16[2,5,288,128]{3,2,1,0:T(8,128)(2,1)}, u32[]{:S(2)}, u32[]{:S(2)}) collective-permute-start(bf16[2,5,288,128]{3,2,1,0:T(8,128)(2,1)} %collective-permute-done.3.refs_3_), channel_id=1, source_target_pairs={{0,8},{4,12},{8,0},{12,4},{16,24},{20,28},{24,16},{28,20},{1,9},{5... | collective-permute-start | bytes 2211848 | tf_op jit(solution)/shard_map/ppermute | solution.py:459
  85.9 1.1 %copy-start.6 = (f32[2,3,256,128]{3,2,1,0:T(8,128)S(1)}, f32[2,3,256,128]{3,2,1,0:T(8,128)}, u32[]{:S(2)}) copy-start(f32[2,3,256,128]{3,2,1,0:T(8,128)} %copy-done.5) | copy-start | bytes 2359300
  89.0 1.7 %collective-permute-start.7 = (bf16[2,640,128]{2,1,0:T(8,128)(2,1)S(1)}, bf16[2,640,128]{2,1,0:T(8,128)(2,1)S(1)}, u32[]{:S(2)}, u32[]{:S(2)}) collective-permute-start(bf16[2,640,128]{2,1,0:T(8,128)(2,1)S(1)} %merge.1.m_a), channel_id=1, source_target_pairs={{0,1},{1,0},{2,3},{3,2},{4,5},{5,4},{6,7},{7,6},{8,9},{9,8},{10,11... | collective-permute-start | bytes 983048 | tf_op jit(solution)/shard_map/ppermute | solution.py:372
  89.0 10.1 %collective-permute-start.6 = (bf16[2,640,128]{2,1,0:T(8,128)(2,1)S(1)}, bf16[2,640,128]{2,1,0:T(8,128)(2,1)S(1)}, u32[]{:S(2)}, u32[]{:S(2)}) collective-permute-start(bf16[2,640,128]{2,1,0:T(8,128)(2,1)S(1)} %merge.1.m_a), channel_id=1, source_target_pairs={{0,2},{1,3},{2,0},{3,1},{4,6},{5,7},{6,4},{7,5},{8,10},{9,11},{10,... | collective-permute-start | bytes 983048 | tf_op jit(solution)/shard_map/ppermute | solution.py:372
  90.7 1.6 %copy-start.2 = (bf16[2,256,2048]{2,1,0:T(8,128)(2,1)S(1)}, bf16[2,256,2048]{2,1,0:T(8,128)(2,1)}, u32[]{:S(2)}) copy-start(bf16[2,256,2048]{2,1,0:T(8,128)(2,1)} %base.1) | copy-start | bytes 6291460
  99.2 1.6 %collective-permute-start.9 = (bf16[2,640,128]{2,1,0:T(8,128)(2,1)S(1)}, bf16[2,640,128]{2,1,0:T(8,128)(2,1)S(1)}, u32[]{:S(2)}, u32[]{:S(2)}) collective-permute-start(bf16[2,640,128]{2,1,0:T(8,128)(2,1)S(1)} %collective-permute-done.6.m_a), channel_id=1, source_target_pairs={{0,1},{1,0},{2,3},{3,2},{4,5},{5,4},{6,7},{7,6},{8,9},{9,8},{10,11... | collective-permute-start | bytes 983048 | tf_op jit(solution)/shard_map/ppermute | solution.py:372
  (2 other events, 1.4 us)

commit v6 on v5

--- a/solution.py
+++ b/solution.py
@@ -275,7 +275,8 @@
     mixed[0] = jnp.concatenate([done[0], done[1], last], axis=0).astype(BF16)
 
 
-def project_kernel(block, m_a, m_b, w_a, w_b, base, out, lhs):
+def project_kernel(block, m_a, m_b, *refs):
+    ws, (base, out, lhs) = refs[:-3], refs[-3:]
     count, width = out.shape[1:]
     half = count // 2
     lanes = lane_iota(half)
@@ -289,12 +290,29 @@
     lhs[half:, 512:] = jnp.where(lanes < 64, pltpu.roll(left, 64, 1), right).astype(BF16)
     for start in range(0, width, block):
         part = pl.ds(start, block)
-        weights = jnp.concatenate(
-            [w_a[:256, part], w_b[:256, part], w_a[256:, part], w_b[256:, part]], axis=0
-        )
+        if len(ws) == 1:
+            weights = ws[0][:, part]
+        else:
+            weights = jnp.concatenate(
+                [w[rows, part] for rows in (pl.ds(0, 256), pl.ds(256, 64)) for w in ws], axis=0
+            )
         total = base[0, :, part].astype(F32)
         total += jnp.dot(lhs[...], weights, preferred_element_type=F32)
         out[0, :, part] = total.astype(out.dtype)
+
+
+def stage_kernel(w_a, w_b, after, out, sem):
+    del after
+    copies, place = [], 0
+    for rows in (pl.ds(0, 256), pl.ds(256, 64)):
+        for w in (w_a, w_b):
+            dst = out.at[pl.ds(place, rows.size), :]
+            copies.append(pltpu.make_async_copy(w.at[rows, :], dst, sem.at[len(copies)]))
+            place += rows.size
+    for copy in copies:
+        copy.start()
+    for copy in copies:
+        copy.wait()
 
 
 def held(plane, here):
@@ -588,24 +606,34 @@
     m_x = permuted(mixed, "tp", tp_count // 2)
     m_c = permuted(mixed, "tp", 1)
 
-    def project(m_a, m_b, w_a, w_b, base, dtype, name):
+    def project(m_a, m_b, ws, base, dtype, name):
         m_spec = pl.BlockSpec((1, q_rows, LANES), lambda b: (b, 0, 0))
         return pl.pallas_call(
             functools.partial(project_kernel, 512),
             grid=(req_dev,),
             out_shape=jax.ShapeDtypeStruct(tokens.shape, dtype),
-            in_specs=[m_spec] * 2 + [full(w_out.shape)] * 2 + [token_spec],
+            in_specs=[m_spec] * 2 + [full(w.shape) for w in ws] + [token_spec],
             out_specs=token_spec,
             scratch_shapes=[pltpu.VMEM((count, 640), BF16)],
             compiler_params=params(),
             cost_estimate=HINT,
             name=name,
-        )(m_a, m_b, w_a, w_b, base)
-
-    partial = project(mixed, m_c, w_out, w_c, tokens, F32, "project_chip")
-    m_x = lax.optimization_barrier((m_x, partial))[0]
+        )(m_a, m_b, *ws, base)
+
+    partial = project(mixed, m_c, (w_out, w_c), tokens, F32, "project_chip")
+    staged = pl.pallas_call(
+        stage_kernel,
+        out_shape=jax.ShapeDtypeStruct((2 * w_out.shape[0], width), BF16),
+        in_specs=[any_spec] * 3,
+        out_specs=vmem_spec,
+        scratch_shapes=[pltpu.SemaphoreType.DMA((4,))],
+        compiler_params=params(),
+        cost_estimate=HINT,
+        name="stage",
+    )(w_x, w_xc, partial)
+    m_x = lax.optimization_barrier((m_x, partial, staged))[0]
     m_xc = permuted(m_x, "tp", 1)
-    layer = project(m_x, m_xc, w_x, w_xc, partial, BF16, "project_rest")
+    layer = project(m_x, m_xc, (staged,), partial, BF16, "project_rest")
 
     if hops:
         cache = fill_cache((5,), [far_outward], cache, {4: 0})

time: 107 us -> 106 us (level); the launches traced: 105 us -> 106 us
  Pallas kernels: 34.7 us -> 35.8 us
    pallas_call x2, Pallas kernels: 8.37 us -> 6.28 us  [project(): pl.pallas_call(functools.partial(project_kernel, 512), grid=(req_dev,), o...]
    pallas_call x0 -> x1, Pallas kernels: none -> 1.7 us  [on_device(): pl.pallas_call(stage_kernel, out_shape=jax.ShapeDtypeStruct((2 * w_out.sh...]
    ppermute x8, waiting for transfers between devices: 3.64 us -> 2.15 us  [permuted(): return lax.ppermute(value, axis, pairs)]
    pallas_call x2, Pallas kernels: 5.42 us -> 6.8 us  [fill_cache(): pl.pallas_call(functools.partial(cache_kernel, req_dev, span, steps), in_...]
    unnamed x34 -> x36, local copies, waits for them, and re-layouts: 14.1 us -> 14.1 us
  transfers between devices with their start and end apart: 17 -> 17, of which waited for: 7 -> 6; matrix products, arithmetic and copies ran while one was open for 2% -> 2% of each run, Pallas kernels for 28% -> 31%
where the time goes in v6:
time: 106 us
  Pallas kernels  35.8 us (34%)
  starting transfers between devices  34.9 us (33%)
  waiting for transfers between devices  18 us (17%)
  local copies, waits for them, and re-layouts  14.3 us (13%)
  other arithmetic  1.97 us (2%)
    all_to_all x4, starting transfers between devices, exchanged(): return lax.all_to_all(value, 'req', split_axis=0, concat_axis=0, tiled=True)  17.2 us
    all_to_all x4, waiting for transfers between devices, exchanged(): return lax.all_to_all(value, 'req', split_axis=0, concat_axis=0, tiled=True)  15.8 us
    unnamed x36, local copies, waits for them, and re-layouts  14.1 us
    ppermute x5, starting transfers between devices, crossed(): return lax.ppermute(value, 'req', pairs)  10.9 us
    ppermute x8, starting transfers between devices, permuted(): return lax.ppermute(value, axis, pairs)  6.9 us
    pallas_call x2, Pallas kernels, fill_cache(): pl.pallas_call(functools.partial(cache_kernel, req_dev, span, steps), in_...  6.8 us
    pallas_call x2, Pallas kernels, project(): pl.pallas_call(functools.partial(project_kernel, 512), grid=(req_dev,), o...  6.28 us
    pallas_call x1, Pallas kernels, on_device(): pl.pallas_call(functools.partial(row_kernel, requests, count, heads, grou...  5.18 us
  transfers between devices with their start and end apart: 17, of which 6 were waited for; matrix products, arithmetic and copies ran while one was open for 2% of the time, Pallas kernels for 31%

profile of v6, /device:TPU:0, one launch (start us, length us, event | category | flops | bytes accessed | tf_op | source)
XLA Modules:
  0.0 105.9 jit_solution(1603077177674510398)
XLA Ops:
  0.7 1.7 %copy-done = bf16[1,5,2048,128]{3,2,1,0:T(8,128)(2,1)S(1)} copy-done((bf16[1,5,2048,128]{3,2,1,0:T(8,128)(2,1)S(1)}, bf16[1,5,2048,128]{3,2,1,0:T(8,128)(2,1)}, u32[]{:S(2)}) %copy-start) | copy-done | bytes 2621464
  2.4 3.0 %collective-permute-start = (bf16[5,288,128]{2,1,0:T(8,128)(2,1)S(1)}, bf16[5,288,128]{2,1,0:T(8,128)(2,1)}, u32[]{:S(2)}, u32[]{:S(2)}) collective-permute-start(bf16[5,288,128]{2,1,0:T(8,128)(2,1)S(1)} %dynamic-slice_bitcast_fusion.1), channel_id=1, source_target_pairs={{0,4},{4,0},{8,12},{12,8},{16,20},{20,16},{24,28},{28,24},{1,5},{5... | collective-permute-start | bytes 1105928 | tf_op jit(solution)/shard_map/ppermute | solution.py:390
  5.4 5.1 %query.1.q = bf16[8,2,80,128]{3,2,1,0:T(8,128)(2,1)} custom-call(s32[16]{0:T(128)} %cont.1, s32[16]{0:T(128)} %clen.1, bf16[2,256,2048]{2,1,0:T(8,128)(2,1)} %refs_2_.1, f32[1,2048]{1,0:T(1,128)} %bitcast.16, bf16[320,2048]{1,0:T(8,128)(2,1)} %bitcast.19, f32[1,64]{1,0:T(1,128)} %bitcast.22, f32[2,408,128]{2,1,0:T(8,128)} %constant.49.clone.table), custom_call_target="tpu_custom_call" | custom-call | flops 805306368 | bytes 6291456 | tf_op jit(solution)/shard_map/query/pallas_call | solution.py:450
  10.5 5.0 %all-to-all-start = ((bf16[8,2,80,128]{3,2,1,0:T(8,128)(2,1)}), bf16[8,2,80,128]{3,2,1,0:T(8,128)(2,1)S(1)}, u32[]{:S(2)}, u32[]{:S(2)}) async-start(bf16[8,2,80,128]{3,2,1,0:T(8,128)(2,1)} %query.1.q), calls=%async_computation | async-start | bytes 655360 | tf_op jit(solution)/shard_map/all_to_all | solution.py:394
  15.6 1.5 %collective-permute-start.9 = (bf16[320,2048]{1,0:T(8,128)(2,1)}, bf16[320,2048]{1,0:T(8,128)(2,1)}, u32[]{:S(2)}, u32[]{:S(2)}) collective-permute-start(bf16[320,2048]{1,0:T(8,128)(2,1)} %refs_0_.1), channel_id=1, source_target_pairs={{0,2},{1,3},{2,0},{3,1},{4,6},{5,7},{6,4},{7,5},{8,10},{9,11},{10,... | collective-permute-start | bytes 3932168 | tf_op jit(solution)/shard_map/ppermute | solution.py:390
  17.1 2.0 %pad_maximum_fusion.refs_0_ = bf16[2,5,288,128]{3,2,1,0:T(8,128)(2,1)} fusion(bf16[1,5,288,128]{3,2,1,0:T(8,128)(2,1)} %bitcast.8, bf16[1,5,288,128]{3,2,1,0:T(8,128)(2,1)S(1)} %constant_dynamic-slice_fusion), kind=kLoop, calls=%fused_computation.1 | loop fusion | flops 368640 | bytes 1474560 | tf_op jit(solution)/shard_map/stack | solution.py:471
  19.1 1.5 %collective-permute-start.2 = (bf16[2,5,288,128]{3,2,1,0:T(8,128)(2,1)}, bf16[2,5,288,128]{3,2,1,0:T(8,128)(2,1)}, u32[]{:S(2)}, u32[]{:S(2)}) collective-permute-start(bf16[2,5,288,128]{3,2,1,0:T(8,128)(2,1)} %pad_maximum_fusion.refs_0_), channel_id=1, source_target_pairs={{8,16},{12,20},{16,8},{20,12},{9,17},{13,21},{17,9},{21,13},{10,18... | collective-permute-start | bytes 2211848 | tf_op jit(solution)/shard_map/ppermute | solution.py:477
  20.6 3.9 %collective-permute-start.1 = (bf16[2,5,288,128]{3,2,1,0:T(8,128)(2,1)}, bf16[2,5,288,128]{3,2,1,0:T(8,128)(2,1)}, u32[]{:S(2)}, u32[]{:S(2)}) collective-permute-start(bf16[2,5,288,128]{3,2,1,0:T(8,128)(2,1)} %pad_maximum_fusion.refs_0_), channel_id=1, source_target_pairs={{0,8},{4,12},{8,0},{12,4},{16,24},{20,28},{24,16},{28,20},{1,9},{5... | collective-permute-start | bytes 2211848 | tf_op jit(solution)/shard_map/ppermute | solution.py:477
  24.5 1.9 %all-to-all-done = bf16[8,2,80,128]{3,2,1,0:T(8,128)(2,1)S(1)} async-done(((bf16[8,2,80,128]{3,2,1,0:T(8,128)(2,1)}), bf16[8,2,80,128]{3,2,1,0:T(8,128)(2,1)S(1)}, u32[]{:S(2)}, u32[]{:S(2)}) %all-to-all-start) | async-done | bytes 327712 | tf_op jit(solution)/shard_map/all_to_all | solution.py:394
  26.4 1.4 %route_query.1 = bf16[8,80,128]{2,1,0:T(8,128)(2,1)} custom-call(s32[3,16]{1,0:T(4,128)S(1)} %pad_add_fusion.meta, bf16[16,80,128]{2,1,0:T(8,128)(2,1)S(1)} %bitcast.15), custom_call_target="tpu_custom_call" | custom-call | bytes 1048576 | tf_op jit(solution)/shard_map/route_query/pallas_call | solution.py:513
  27.8 3.4 %all-to-all-start.1 = ((bf16[8,80,128]{2,1,0:T(8,128)(2,1)}), bf16[8,80,128]{2,1,0:T(8,128)(2,1)S(1)}, u32[]{:S(2)}, u32[]{:S(2)}) async-start(bf16[8,80,128]{2,1,0:T(8,128)(2,1)} %route_query.1), calls=%async_computation.1 | async-start | bytes 327680 | tf_op jit(solution)/shard_map/all_to_all | solution.py:394
  31.3 1.5 %copy-done.1 = bf16[2,256,2048]{2,1,0:T(8,128)(2,1)S(1)} copy-done((bf16[2,256,2048]{2,1,0:T(8,128)(2,1)S(1)}, bf16[2,256,2048]{2,1,0:T(8,128)(2,1)}, u32[]{:S(2)}) %copy-start.1) | copy-done | bytes 2097176
  32.8 1.7 %copy-done.8 = bf16[2048,640]{1,0:T(8,128)(2,1)S(1)} copy-done((bf16[2048,640]{1,0:T(8,128)(2,1)S(1)}, bf16[2048,640]{1,0:T(8,128)(2,1)}, u32[]{:S(2)}) %copy-start.8) | copy-done | bytes 2621464
  35.6 3.9 %fresh.1.refs_5_.refs_1_ = bf16[2,5,256,128]{3,2,1,0:T(8,128)(2,1)S(1)} custom-call(s32[3,16]{1,0:T(4,128)S(1)} %pad_add_fusion.meta, bf16[2,256,2048]{2,1,0:T(8,128)(2,1)S(1)} %copy-done.1, f32[1,2048]{1,0:T(1,128)S(1)} %bitcast.17, bf16[2048,640]{1,0:T(8,128)(2,1)S(1)} %copy-done.8, f32[1,64]{1,0:T(1,128)S(1)} %bitcast.18, f32[2,408,128]{2,1,0:T(8,128)S(1)} %copy-done.9, ...), custom_call_target="tpu_custom_call" | custom-call | bytes 1024 | tf_op jit(solution)/shard_map/fresh/pallas_call | solution.py:494
  40.5 4.7 %all-to-all-done.1.q = bf16[8,80,128]{2,1,0:T(8,128)(2,1)S(1)} async-done(((bf16[8,80,128]{2,1,0:T(8,128)(2,1)}), bf16[8,80,128]{2,1,0:T(8,128)(2,1)S(1)}, u32[]{:S(2)}, u32[]{:S(2)}) %all-to-all-start.1) | async-done | bytes 163872 | tf_op jit(solution)/shard_map/all_to_all | solution.py:394
  45.1 1.5 %collective-permute-start.3 = (bf16[2,5,288,128]{3,2,1,0:T(8,128)(2,1)}, bf16[2,5,288,128]{3,2,1,0:T(8,128)(2,1)}, u32[]{:S(2)}, u32[]{:S(2)}) collective-permute-start(bf16[2,5,288,128]{3,2,1,0:T(8,128)(2,1)} %collective-permute-done.1.refs_1_), channel_id=1, source_target_pairs={{8,16},{12,20},{16,8},{20,12},{9,17},{13,21},{17,9},{21,13},{10,18... | collective-permute-start | bytes 2211848 | tf_op jit(solution)/shard_map/ppermute | solution.py:477
  46.7 2.0 %collective-permute-start.4 = (bf16[2,5,288,128]{3,2,1,0:T(8,128)(2,1)}, bf16[2,5,288,128]{3,2,1,0:T(8,128)(2,1)}, u32[]{:S(2)}, u32[]{:S(2)}) collective-permute-start(bf16[2,5,288,128]{3,2,1,0:T(8,128)(2,1)} %collective-permute-done.2.refs_2_), channel_id=1, source_target_pairs={{0,8},{4,12},{8,0},{12,4},{16,24},{20,28},{24,16},{28,20},{1,9},{5... | collective-permute-start | bytes 2211848 | tf_op jit(solution)/shard_map/ppermute | solution.py:477
  50.3 5.2 %attend_row.1 = bf16[8,96,128]{2,1,0:T(8,128)(2,1)S(1)} custom-call(s32[3,16]{1,0:T(4,128)S(1)} %pad_add_fusion.meta, bf16[8,80,128]{2,1,0:T(8,128)(2,1)S(1)} %all-to-all-done.1.q, bf16[2,2048,128]{2,1,0:T(8,128)(2,1)S(1)} %copy-done.4), custom_call_target="tpu_custom_call" | custom-call | flops 2684354560 | bytes 33554432 | tf_op jit(solution)/shard_map/attend_row/pallas_call | solution.py:542
  56.2 4.7 %all-to-all-start.2 = ((bf16[8,96,128]{2,1,0:T(8,128)(2,1)}), bf16[8,96,128]{2,1,0:T(8,128)(2,1)S(1)}, u32[]{:S(2)}, u32[]{:S(2)}) async-start(bf16[8,96,128]{2,1,0:T(8,128)(2,1)} %copy-done.12), calls=%async_computation.2 | async-start | bytes 393216 | tf_op jit(solution)/shard_map/all_to_all | solution.py:394
  62.3 2.8 %attend_new.1.near = f32[2,3,256,128]{3,2,1,0:T(8,128)S(1)} custom-call(bf16[8,2,80,128]{3,2,1,0:T(8,128)(2,1)S(1)} %copy-done.7, bf16[2,5,256,128]{3,2,1,0:T(8,128)(2,1)S(1)} %fresh.1.refs_5_.refs_1_), custom_call_target="tpu_custom_call" | custom-call | bytes 1024 | tf_op jit(solution)/shard_map/attend_new/pallas_call | solution.py:528
  66.1 2.8 %all-to-all-done.2.src.refs_7_ = bf16[8,96,128]{2,1,0:T(8,128)(2,1)S(1)} async-done(((bf16[8,96,128]{2,1,0:T(8,128)(2,1)}), bf16[8,96,128]{2,1,0:T(8,128)(2,1)S(1)}, u32[]{:S(2)}, u32[]{:S(2)}) %all-to-all-start.2) | async-done | bytes 196640 | tf_op jit(solution)/shard_map/all_to_all | solution.py:394
  70.2 4.1 %all-to-all-start.3 = ((bf16[8,2,96,128]{3,2,1,0:T(8,128)(2,1)}), bf16[8,2,96,128]{3,2,1,0:T(8,128)(2,1)}, u32[]{:S(2)}, u32[]{:S(2)}) async-start(bf16[8,2,96,128]{3,2,1,0:T(8,128)(2,1)} %bitcast.14), calls=%async_computation.3 | async-start | bytes 786432 | tf_op jit(solution)/shard_map/all_to_all | solution.py:394
  74.3 1.9 %collective-permute-start.12 = (bf16[2,5,288,128]{3,2,1,0:T(8,128)(2,1)}, bf16[2,5,288,128]{3,2,1,0:T(8,128)(2,1)}, u32[]{:S(2)}, u32[]{:S(2)}) collective-permute-start(bf16[2,5,288,128]{3,2,1,0:T(8,128)(2,1)} %collective-permute-done.3.refs_3_), channel_id=1, source_target_pairs={{0,8},{4,12},{8,0},{12,4},{16,24},{20,28},{24,16},{28,20},{1,9},{5... | collective-permute-start | bytes 2211848 | tf_op jit(solution)/shard_map/ppermute | solution.py:477
  76.2 3.4 %cache.2.refs_3_ = bf16[4,5,288,128]{3,2,1,0:T(8,128)(2,1)} custom-call(s32[3,16]{1,0:T(4,128)S(1)} %pad_add_fusion.meta, bf16[2,5,288,128]{3,2,1,0:T(8,128)(2,1)} %pad_maximum_fusion.refs_0_, bf16[2,5,288,128]{3,2,1,0:T(8,128)(2,1)} %collective-permute-done.1.refs_1_, bf16[2,5,288,128]{3,2,1,0:T(8,128)(2,1)} %collective-permute-done.2.refs_2_, ...), custom_call_target="tpu_custom_call" | custom-call | bytes 1024 | tf_op jit(solution)/shard_map/cache/pallas_call | solution.py:558
  79.6 6.5 %all-to-all-done.3.far = bf16[8,2,96,128]{3,2,1,0:T(8,128)(2,1)} async-done(((bf16[8,2,96,128]{3,2,1,0:T(8,128)(2,1)}), bf16[8,2,96,128]{3,2,1,0:T(8,128)(2,1)}, u32[]{:S(2)}, u32[]{:S(2)}) %all-to-all-start.3) | async-done | bytes 393248 | tf_op jit(solution)/shard_map/all_to_all | solution.py:394
  87.2 2.0 %merge.1.m_a = bf16[2,640,128]{2,1,0:T(8,128)(2,1)S(1)} custom-call(s32[3,16]{1,0:T(4,128)S(1)} %pad_add_fusion.meta, bf16[8,2,96,128]{3,2,1,0:T(8,128)(2,1)} %all-to-all-done.3.far, f32[2,3,256,128]{3,2,1,0:T(8,128)S(1)} %copy-done.6), custom_call_target="tpu_custom_call" | custom-call | bytes 1024 | tf_op jit(solution)/shard_map/merge/pallas_call | solution.py:591
  90.9 1.6 %copy-done.2 = bf16[2,256,2048]{2,1,0:T(8,128)(2,1)S(1)} copy-done((bf16[2,256,2048]{2,1,0:T(8,128)(2,1)S(1)}, bf16[2,256,2048]{2,1,0:T(8,128)(2,1)}, u32[]{:S(2)}) %copy-start.2) | copy-done | bytes 2097176
  92.5 3.3 %project_chip.1.after.refs_1_ = f32[2,256,2048]{2,1,0:T(8,128)S(1)} custom-call(bf16[2,640,128]{2,1,0:T(8,128)(2,1)S(1)} %merge.1.m_a, bf16[2,640,128]{2,1,0:T(8,128)(2,1)S(1)} %collective-permute-done.7.m_b, bf16[320,2048]{1,0:T(8,128)(2,1)S(1)} %copy-done.11, bf16[320,2048]{1,0:T(8,128)(2,1)} %collective-permute-done.8.refs_1_, ...), custom_call_target="tpu_custom_call" | custom-call | bytes 1024 | tf_op jit(solution)/shard_map/project_chip/pallas_call | solution.py:611
  95.9 1.7 %stage.1.refs_0_ = bf16[640,2048]{1,0:T(8,128)(2,1)S(1)} custom-call(bf16[320,2048]{1,0:T(8,128)(2,1)} %collective-permute-done.9.w_a, bf16[320,2048]{1,0:T(8,128)(2,1)} %collective-permute-done.10.w_b, f32[2,256,2048]{2,1,0:T(8,128)S(1)} %project_chip.1.after.refs_1_), custom_call_target="tpu_custom_call" | custom-call | bytes 1024 | tf_op jit(solution)/shard_map/stage/pallas_call | solution.py:624
  97.6 1.9 %collective-permute-done.6.m_a = bf16[2,640,128]{2,1,0:T(8,128)(2,1)S(1)} collective-permute-done((bf16[2,640,128]{2,1,0:T(8,128)(2,1)S(1)}, bf16[2,640,128]{2,1,0:T(8,128)(2,1)S(1)}, u32[]{:S(2)}, u32[]{:S(2)}) %collective-permute-start.6) | collective-permute-done | bytes 327712 | tf_op jit(solution)/shard_map/ppermute | solution.py:390
  99.5 3.4 %cache.3 = bf16[4,5,288,128]{3,2,1,0:T(8,128)(2,1)} custom-call(s32[3,16]{1,0:T(4,128)S(1)} %pad_add_fusion.meta, bf16[2,5,288,128]{3,2,1,0:T(8,128)(2,1)} %collective-permute-done.12.refs_0_, bf16[2,5,256,128]{3,2,1,0:T(8,128)(2,1)S(1)} %fresh.1.refs_5_.refs_1_, ...), custom_call_target="tpu_custom_call", output_to_operand_aliasing={{}: (4, {})} | custom-call | bytes 1024 | tf_op jit(solution)/shard_map/cache/pallas_call | solution.py:558
  102.9 3.0 %project_rest.1 = bf16[2,256,2048]{2,1,0:T(8,128)(2,1)} custom-call(bf16[2,640,128]{2,1,0:T(8,128)(2,1)S(1)} %collective-permute-done.6.m_a, bf16[2,640,128]{2,1,0:T(8,128)(2,1)S(1)} %collective-permute-done.11.m_b, bf16[640,2048]{1,0:T(8,128)(2,1)S(1)} %stage.1.refs_0_, f32[2,256,2048]{2,1,0:T(8,128)S(1)} %project_chip.1.after.refs_1_), custom_call_target="tpu_custom_call" | custom-call | bytes 1024 | tf_op jit(solution)/shard_map/project_rest/pallas_call | solution.py:611
  (55 shorter events, 11.0 us)
Async XLA Ops:
  0.6 1.7 %copy-start = (bf16[1,5,2048,128]{3,2,1,0:T(8,128)(2,1)S(1)}, bf16[1,5,2048,128]{3,2,1,0:T(8,128)(2,1)}, u32[]{:S(2)}) copy-start(bf16[1,5,2048,128]{3,2,1,0:T(8,128)(2,1)} %param.19) | copy-start | bytes 7864324
  2.4 14.7 %collective-permute-start = (bf16[5,288,128]{2,1,0:T(8,128)(2,1)S(1)}, bf16[5,288,128]{2,1,0:T(8,128)(2,1)}, u32[]{:S(2)}, u32[]{:S(2)}) collective-permute-start(bf16[5,288,128]{2,1,0:T(8,128)(2,1)S(1)} %dynamic-slice_bitcast_fusion.1), channel_id=1, source_target_pairs={{0,4},{4,0},{8,12},{12,8},{16,20},{20,16},{24,28},{28,24},{1,5},{5... | collective-permute-start | bytes 1105928 | tf_op jit(solution)/shard_map/ppermute | solution.py:390
  10.5 14.0 %copy-start.15 = (s32[16]{0:T(128)S(1)}, s32[16]{0:T(128)}, u32[]{:S(2)}) copy-start(s32[16]{0:T(128)} %clen.1) | copy-start | bytes 196
  10.5 14.0 %copy-start.16 = (s32[16]{0:T(128)S(1)}, s32[16]{0:T(128)}, u32[]{:S(2)}) copy-start(s32[16]{0:T(128)} %cont.1) | copy-start | bytes 196
  10.5 14.0 %copy-start.17 = (s32[16]{0:T(128)S(1)}, s32[16]{0:T(128)}, u32[]{:S(2)}) copy-start(s32[16]{0:T(128)} %param.21) | copy-start | bytes 196
  10.5 15.9 %all-to-all-start = ((bf16[8,2,80,128]{3,2,1,0:T(8,128)(2,1)}), bf16[8,2,80,128]{3,2,1,0:T(8,128)(2,1)S(1)}, u32[]{:S(2)}, u32[]{:S(2)}) async-start(bf16[8,2,80,128]{3,2,1,0:T(8,128)(2,1)} %query.1.q), calls=%async_computation | async-start | bytes 655360 | tf_op jit(solution)/shard_map/all_to_all | solution.py:394
  15.6 45.3 %collective-permute-start.9 = (bf16[320,2048]{1,0:T(8,128)(2,1)}, bf16[320,2048]{1,0:T(8,128)(2,1)}, u32[]{:S(2)}, u32[]{:S(2)}) collective-permute-start(bf16[320,2048]{1,0:T(8,128)(2,1)} %refs_0_.1), channel_id=1, source_target_pairs={{0,2},{1,3},{2,0},{3,1},{4,6},{5,7},{6,4},{7,5},{8,10},{9,11},{10,... | collective-permute-start | bytes 3932168 | tf_op jit(solution)/shard_map/ppermute | solution.py:390
  17.1 14.2 %copy-start.13 = (f32[2048]{0:T(1024)S(1)}, f32[2048]{0:T(1024)}, u32[]{:S(2)}) copy-start(f32[2048]{0:T(1024)} %param.13) | copy-start | bytes 24580
  17.1 14.2 %copy-start.14 = (f32[64]{0:T(128)S(1)}, f32[64]{0:T(128)}, u32[]{:S(2)}) copy-start(f32[64]{0:T(128)} %param.18) | copy-start | bytes 772
  19.1 26.1 %collective-permute-start.2 = (bf16[2,5,288,128]{3,2,1,0:T(8,128)(2,1)}, bf16[2,5,288,128]{3,2,1,0:T(8,128)(2,1)}, u32[]{:S(2)}, u32[]{:S(2)}) collective-permute-start(bf16[2,5,288,128]{3,2,1,0:T(8,128)(2,1)} %pad_maximum_fusion.refs_0_), channel_id=1, source_target_pairs={{8,16},{12,20},{16,8},{20,12},{9,17},{13,21},{17,9},{21,13},{10,18... | collective-permute-start | bytes 2211848 | tf_op jit(solution)/shard_map/ppermute | solution.py:477
  20.6 24.5 %collective-permute-start.1 = (bf16[2,5,288,128]{3,2,1,0:T(8,128)(2,1)}, bf16[2,5,288,128]{3,2,1,0:T(8,128)(2,1)}, u32[]{:S(2)}, u32[]{:S(2)}) collective-permute-start(bf16[2,5,288,128]{3,2,1,0:T(8,128)(2,1)} %pad_maximum_fusion.refs_0_), channel_id=1, source_target_pairs={{0,8},{4,12},{8,0},{12,4},{16,24},{20,28},{24,16},{28,20},{1,9},{5... | collective-permute-start | bytes 2211848 | tf_op jit(solution)/shard_map/ppermute | solution.py:477
  27.8 17.3 %all-to-all-start.1 = ((bf16[8,80,128]{2,1,0:T(8,128)(2,1)}), bf16[8,80,128]{2,1,0:T(8,128)(2,1)S(1)}, u32[]{:S(2)}, u32[]{:S(2)}) async-start(bf16[8,80,128]{2,1,0:T(8,128)(2,1)} %route_query.1), calls=%async_computation.1 | async-start | bytes 327680 | tf_op jit(solution)/shard_map/all_to_all | solution.py:394
  31.2 1.6 %copy-start.1 = (bf16[2,256,2048]{2,1,0:T(8,128)(2,1)S(1)}, bf16[2,256,2048]{2,1,0:T(8,128)(2,1)}, u32[]{:S(2)}) copy-start(bf16[2,256,2048]{2,1,0:T(8,128)(2,1)} %refs_2_.1) | copy-start | bytes 6291460
  32.8 1.7 %copy-start.8 = (bf16[2048,640]{1,0:T(8,128)(2,1)S(1)}, bf16[2048,640]{1,0:T(8,128)(2,1)}, u32[]{:S(2)}) copy-start(bf16[2048,640]{1,0:T(8,128)(2,1)} %w.1) | copy-start | bytes 7864324
  34.6 1.0 copy-start.9
  39.5 1.0 copy-start.3
  45.1 23.7 %collective-permute-start.3 = (bf16[2,5,288,128]{3,2,1,0:T(8,128)(2,1)}, bf16[2,5,288,128]{3,2,1,0:T(8,128)(2,1)}, u32[]{:S(2)}, u32[]{:S(2)}) collective-permute-start(bf16[2,5,288,128]{3,2,1,0:T(8,128)(2,1)} %collective-permute-done.1.refs_1_), channel_id=1, source_target_pairs={{8,16},{12,20},{16,8},{20,12},{9,17},{13,21},{17,9},{21,13},{10,18... | collective-permute-start | bytes 2211848 | tf_op jit(solution)/shard_map/ppermute | solution.py:477
  46.7 22.2 %collective-permute-start.4 = (bf16[2,5,288,128]{3,2,1,0:T(8,128)(2,1)}, bf16[2,5,288,128]{3,2,1,0:T(8,128)(2,1)}, u32[]{:S(2)}, u32[]{:S(2)}) collective-permute-start(bf16[2,5,288,128]{3,2,1,0:T(8,128)(2,1)} %collective-permute-done.2.refs_2_), channel_id=1, source_target_pairs={{0,8},{4,12},{8,0},{12,4},{16,24},{20,28},{24,16},{28,20},{1,9},{5... | collective-permute-start | bytes 2211848 | tf_op jit(solution)/shard_map/ppermute | solution.py:477
  48.7 17.4 %collective-permute-start.5 = (bf16[2,5,256,128]{3,2,1,0:T(8,128)(2,1)S(1)}, bf16[2,5,256,128]{3,2,1,0:T(8,128)(2,1)}, u32[]{:S(2)}, u32[]{:S(2)}) collective-permute-start(bf16[2,5,256,128]{3,2,1,0:T(8,128)(2,1)S(1)} %fresh.1.refs_5_.refs_1_), channel_id=1, source_target_pairs={{0,4},{4,0},{8,12},{12,8},{16,20},{20,16},{24,28},{28,24},{1,5},{5... | collective-permute-start | bytes 1966088 | tf_op jit(solution)/shard_map/ppermute | solution.py:390
  49.1 1.2 %copy-start.4 = (bf16[2,2048,128]{2,1,0:T(8,128)(2,1)S(1)}, bf16[2,2048,128]{2,1,0:T(8,128)(2,1)}, u32[]{:S(2)}) copy-start(bf16[2,2048,128]{2,1,0:T(8,128)(2,1)} %copy-done.3) | copy-start | bytes 3145732
  56.2 12.6 %all-to-all-start.2 = ((bf16[8,96,128]{2,1,0:T(8,128)(2,1)}), bf16[8,96,128]{2,1,0:T(8,128)(2,1)S(1)}, u32[]{:S(2)}, u32[]{:S(2)}) async-start(bf16[8,96,128]{2,1,0:T(8,128)(2,1)} %copy-done.12), calls=%async_computation.2 | async-start | bytes 393216 | tf_op jit(solution)/shard_map/all_to_all | solution.py:394
  60.9 29.8 %collective-permute-start.8 = (bf16[320,2048]{1,0:T(8,128)(2,1)}, bf16[320,2048]{1,0:T(8,128)(2,1)}, u32[]{:S(2)}, u32[]{:S(2)}) collective-permute-start(bf16[320,2048]{1,0:T(8,128)(2,1)} %refs_0_.1), channel_id=1, source_target_pairs={{0,1},{1,0},{2,3},{3,2},{4,5},{5,4},{6,7},{7,6},{8,9},{9,8},{10,11... | collective-permute-start | bytes 3932168 | tf_op jit(solution)/shard_map/ppermute | solution.py:390
  60.9 35.0 %collective-permute-start.10 = (bf16[320,2048]{1,0:T(8,128)(2,1)}, bf16[320,2048]{1,0:T(8,128)(2,1)}, u32[]{:S(2)}, u32[]{:S(2)}) collective-permute-start(bf16[320,2048]{1,0:T(8,128)(2,1)} %collective-permute-done.9.w_a), channel_id=1, source_target_pairs={{0,1},{1,0},{2,3},{3,2},{4,5},{5,4},{6,7},{7,6},{8,9},{9,8},{10,11... | collective-permute-start | bytes 3932168 | tf_op jit(solution)/shard_map/ppermute | solution.py:390
  61.4 1.0 copy-start.7
  70.2 15.9 %all-to-all-start.3 = ((bf16[8,2,96,128]{3,2,1,0:T(8,128)(2,1)}), bf16[8,2,96,128]{3,2,1,0:T(8,128)(2,1)}, u32[]{:S(2)}, u32[]{:S(2)}) async-start(bf16[8,2,96,128]{3,2,1,0:T(8,128)(2,1)} %bitcast.14), calls=%async_computation.3 | async-start | bytes 786432 | tf_op jit(solution)/shard_map/all_to_all | solution.py:394
  74.3 25.2 %collective-permute-start.12 = (bf16[2,5,288,128]{3,2,1,0:T(8,128)(2,1)}, bf16[2,5,288,128]{3,2,1,0:T(8,128)(2,1)}, u32[]{:S(2)}, u32[]{:S(2)}) collective-permute-start(bf16[2,5,288,128]{3,2,1,0:T(8,128)(2,1)} %collective-permute-done.3.refs_3_), channel_id=1, source_target_pairs={{0,8},{4,12},{8,0},{12,4},{16,24},{20,28},{24,16},{28,20},{1,9},{5... | collective-permute-start | bytes 2211848 | tf_op jit(solution)/shard_map/ppermute | solution.py:477
  86.1 1.1 %copy-start.6 = (f32[2,3,256,128]{3,2,1,0:T(8,128)S(1)}, f32[2,3,256,128]{3,2,1,0:T(8,128)}, u32[]{:S(2)}) copy-start(f32[2,3,256,128]{3,2,1,0:T(8,128)} %copy-done.5) | copy-start | bytes 2359300
  87.2 3.7 %copy-start.11 = (bf16[320,2048]{1,0:T(8,128)(2,1)S(1)}, bf16[320,2048]{1,0:T(8,128)(2,1)}, u32[]{:S(2)}) copy-start(bf16[320,2048]{1,0:T(8,128)(2,1)} %refs_0_.1) | copy-start | bytes 3932164
  89.2 1.7 %collective-permute-start.7 = (bf16[2,640,128]{2,1,0:T(8,128)(2,1)S(1)}, bf16[2,640,128]{2,1,0:T(8,128)(2,1)S(1)}, u32[]{:S(2)}, u32[]{:S(2)}) collective-permute-start(bf16[2,640,128]{2,1,0:T(8,128)(2,1)S(1)} %merge.1.m_a), channel_id=1, source_target_pairs={{0,1},{1,0},{2,3},{3,2},{4,5},{5,4},{6,7},{7,6},{8,9},{9,8},{10,11... | collective-permute-start | bytes 983048 | tf_op jit(solution)/shard_map/ppermute | solution.py:390
  89.3 10.1 %collective-permute-start.6 = (bf16[2,640,128]{2,1,0:T(8,128)(2,1)S(1)}, bf16[2,640,128]{2,1,0:T(8,128)(2,1)S(1)}, u32[]{:S(2)}, u32[]{:S(2)}) collective-permute-start(bf16[2,640,128]{2,1,0:T(8,128)(2,1)S(1)} %merge.1.m_a), channel_id=1, source_target_pairs={{0,2},{1,3},{2,0},{3,1},{4,6},{5,7},{6,4},{7,5},{8,10},{9,11},{10,... | collective-permute-start | bytes 983048 | tf_op jit(solution)/shard_map/ppermute | solution.py:390
  90.9 1.6 %copy-start.2 = (bf16[2,256,2048]{2,1,0:T(8,128)(2,1)S(1)}, bf16[2,256,2048]{2,1,0:T(8,128)(2,1)}, u32[]{:S(2)}) copy-start(bf16[2,256,2048]{2,1,0:T(8,128)(2,1)} %refs_2_.1) | copy-start | bytes 6291460
  99.5 3.4 %collective-permute-start.11 = (bf16[2,640,128]{2,1,0:T(8,128)(2,1)S(1)}, bf16[2,640,128]{2,1,0:T(8,128)(2,1)S(1)}, u32[]{:S(2)}, u32[]{:S(2)}) collective-permute-start(bf16[2,640,128]{2,1,0:T(8,128)(2,1)S(1)} %collective-permute-done.6.m_a), channel_id=1, source_target_pairs={{0,1},{1,0},{2,3},{3,2},{4,5},{5,4},{6,7},{7,6},{8,9},{9,8},{10,11... | collective-permute-start | bytes 983048 | tf_op jit(solution)/shard_map/ppermute | solution.py:390
  (3 other events, 2.3 us)

commit v7 on v6

--- a/solution.py
+++ b/solution.py
@@ -544,7 +544,7 @@
         out_shape=jax.ShapeDtypeStruct((n_req, o_chunk, LANES), BF16),
         in_specs=[SMEM, vmem_spec, vmem_spec],
         out_specs=vmem_spec,
-        compiler_params=params(40),
+        compiler_params=params(60),
         cost_estimate=cost(4 * heads * count * span * 256, 32 << 20),
         name="attend_row",
     )(meta, q_row, pair)
@@ -631,13 +631,15 @@
         cost_estimate=HINT,
         name="stage",
     )(w_x, w_xc, partial)
+    if hops:
+        last = lax.optimization_barrier((far_outward, staged))[0]
+        cache = fill_cache((5,), [last], cache, {4: 0})
+        m_x = lax.optimization_barrier((m_x, cache))[0]
     m_x = lax.optimization_barrier((m_x, partial, staged))[0]
     m_xc = permuted(m_x, "tp", 1)
     layer = project(m_x, m_xc, (staged,), partial, BF16, "project_rest")
 
-    if hops:
-        cache = fill_cache((5,), [far_outward], cache, {4: 0})
-    else:
+    if not hops:
         cache = fill_cache((0,), blocks, layer, {})
     return (layer, cache)
 

time: 106 us -> 106 us (level)
  local copies, waits for them, and re-layouts: 14.3 us -> 12.4 us
  Pallas kernels: 35.8 us -> 37.3 us
    unnamed x36 -> x38, local copies, waits for them, and re-layouts: 14.1 us -> 12.3 us
    pallas_call x1, Pallas kernels: 5.18 us -> 6.69 us  [on_device(): pl.pallas_call(functools.partial(row_kernel, requests, count, heads, grou...]
  transfers between devices with their start and end apart: 17 -> 17, of which waited for: 6 -> 7; matrix products, arithmetic and copies ran while one was open for 2% -> 2% of each run, Pallas kernels for 31% -> 32%
where the time goes in v7:
time: 106 us
  Pallas kernels  37.3 us (35%)
  starting transfers between devices  34.8 us (33%)
  waiting for transfers between devices  18.3 us (17%)
  local copies, waits for them, and re-layouts  12.4 us (12%)
  other arithmetic  1.98 us (2%)
    all_to_all x4, starting transfers between devices, exchanged(): return lax.all_to_all(value, 'req', split_axis=0, concat_axis=0, tiled=True)  17.3 us
    all_to_all x4, waiting for transfers between devices, exchanged(): return lax.all_to_all(value, 'req', split_axis=0, concat_axis=0, tiled=True)  15.7 us
    unnamed x38, local copies, waits for them, and re-layouts  12.3 us
    ppermute x5, starting transfers between devices, crossed(): return lax.ppermute(value, 'req', pairs)  10.9 us
    pallas_call x2, Pallas kernels, fill_cache(): pl.pallas_call(functools.partial(cache_kernel, req_dev, span, steps), in_...  6.81 us
    pallas_call x1, Pallas kernels, on_device(): pl.pallas_call(functools.partial(row_kernel, requests, count, heads, grou...  6.69 us
    ppermute x8, starting transfers between devices, permuted(): return lax.ppermute(value, axis, pairs)  6.67 us
    pallas_call x2, Pallas kernels, project(): pl.pallas_call(functools.partial(project_kernel, 512), grid=(req_dev,), o...  6.26 us
  transfers between devices with their start and end apart: 17, of which 7 were waited for; matrix products, arithmetic and copies ran while one was open for 2% of the time, Pallas kernels for 32%

profile of v7, /device:TPU:0, one launch (start us, length us, event | category | flops | bytes accessed | tf_op | source)
XLA Modules:
  0.0 105.7 jit_solution(7089730751959274965)
XLA Ops:
  0.7 1.7 %copy-done = bf16[1,5,2048,128]{3,2,1,0:T(8,128)(2,1)S(1)} copy-done((bf16[1,5,2048,128]{3,2,1,0:T(8,128)(2,1)S(1)}, bf16[1,5,2048,128]{3,2,1,0:T(8,128)(2,1)}, u32[]{:S(2)}) %copy-start) | copy-done | bytes 2621464
  2.4 3.0 %collective-permute-start = (bf16[5,288,128]{2,1,0:T(8,128)(2,1)S(1)}, bf16[5,288,128]{2,1,0:T(8,128)(2,1)}, u32[]{:S(2)}, u32[]{:S(2)}) collective-permute-start(bf16[5,288,128]{2,1,0:T(8,128)(2,1)S(1)} %dynamic-slice_bitcast_fusion.1), channel_id=1, source_target_pairs={{0,4},{4,0},{8,12},{12,8},{16,20},{20,16},{24,28},{28,24},{1,5},{5... | collective-permute-start | bytes 1105928 | tf_op jit(solution)/shard_map/ppermute | solution.py:390
  5.4 5.1 %query.1.q = bf16[8,2,80,128]{3,2,1,0:T(8,128)(2,1)} custom-call(s32[16]{0:T(128)} %cont.1, s32[16]{0:T(128)} %clen.1, bf16[2,256,2048]{2,1,0:T(8,128)(2,1)} %refs_2_.1, f32[1,2048]{1,0:T(1,128)} %bitcast.16, bf16[320,2048]{1,0:T(8,128)(2,1)} %bitcast.19, f32[1,64]{1,0:T(1,128)} %bitcast.22, f32[2,408,128]{2,1,0:T(8,128)} %constant.49.clone.table), custom_call_target="tpu_custom_call" | custom-call | flops 805306368 | bytes 6291456 | tf_op jit(solution)/shard_map/query/pallas_call | solution.py:450
  10.5 5.0 %all-to-all-start = ((bf16[8,2,80,128]{3,2,1,0:T(8,128)(2,1)}), bf16[8,2,80,128]{3,2,1,0:T(8,128)(2,1)S(1)}, u32[]{:S(2)}, u32[]{:S(2)}) async-start(bf16[8,2,80,128]{3,2,1,0:T(8,128)(2,1)} %query.1.q), calls=%async_computation | async-start | bytes 655360 | tf_op jit(solution)/shard_map/all_to_all | solution.py:394
  15.6 1.5 %collective-permute-start.8 = (bf16[320,2048]{1,0:T(8,128)(2,1)}, bf16[320,2048]{1,0:T(8,128)(2,1)}, u32[]{:S(2)}, u32[]{:S(2)}) collective-permute-start(bf16[320,2048]{1,0:T(8,128)(2,1)} %refs_0_.1), channel_id=1, source_target_pairs={{0,2},{1,3},{2,0},{3,1},{4,6},{5,7},{6,4},{7,5},{8,10},{9,11},{10,... | collective-permute-start | bytes 3932168 | tf_op jit(solution)/shard_map/ppermute | solution.py:390
  17.1 2.0 %pad_maximum_fusion.refs_0_ = bf16[2,5,288,128]{3,2,1,0:T(8,128)(2,1)} fusion(bf16[1,5,288,128]{3,2,1,0:T(8,128)(2,1)} %bitcast.8, bf16[1,5,288,128]{3,2,1,0:T(8,128)(2,1)S(1)} %constant_dynamic-slice_fusion), kind=kLoop, calls=%fused_computation.1 | loop fusion | flops 368640 | bytes 1474560 | tf_op jit(solution)/shard_map/stack | solution.py:471
  19.1 1.5 %collective-permute-start.2 = (bf16[2,5,288,128]{3,2,1,0:T(8,128)(2,1)}, bf16[2,5,288,128]{3,2,1,0:T(8,128)(2,1)}, u32[]{:S(2)}, u32[]{:S(2)}) collective-permute-start(bf16[2,5,288,128]{3,2,1,0:T(8,128)(2,1)} %pad_maximum_fusion.refs_0_), channel_id=1, source_target_pairs={{8,16},{12,20},{16,8},{20,12},{9,17},{13,21},{17,9},{21,13},{10,18... | collective-permute-start | bytes 2211848 | tf_op jit(solution)/shard_map/ppermute | solution.py:477
  20.6 3.9 %collective-permute-start.1 = (bf16[2,5,288,128]{3,2,1,0:T(8,128)(2,1)}, bf16[2,5,288,128]{3,2,1,0:T(8,128)(2,1)}, u32[]{:S(2)}, u32[]{:S(2)}) collective-permute-start(bf16[2,5,288,128]{3,2,1,0:T(8,128)(2,1)} %pad_maximum_fusion.refs_0_), channel_id=1, source_target_pairs={{0,8},{4,12},{8,0},{12,4},{16,24},{20,28},{24,16},{28,20},{1,9},{5... | collective-permute-start | bytes 2211848 | tf_op jit(solution)/shard_map/ppermute | solution.py:477
  24.6 1.9 %all-to-all-done = bf16[8,2,80,128]{3,2,1,0:T(8,128)(2,1)S(1)} async-done(((bf16[8,2,80,128]{3,2,1,0:T(8,128)(2,1)}), bf16[8,2,80,128]{3,2,1,0:T(8,128)(2,1)S(1)}, u32[]{:S(2)}, u32[]{:S(2)}) %all-to-all-start) | async-done | bytes 327712 | tf_op jit(solution)/shard_map/all_to_all | solution.py:394
  26.4 1.4 %route_query.1 = bf16[8,80,128]{2,1,0:T(8,128)(2,1)} custom-call(s32[3,16]{1,0:T(4,128)S(1)} %pad_add_fusion.meta, bf16[16,80,128]{2,1,0:T(8,128)(2,1)S(1)} %bitcast.15), custom_call_target="tpu_custom_call" | custom-call | bytes 1048576 | tf_op jit(solution)/shard_map/route_query/pallas_call | solution.py:513
  27.8 3.4 %all-to-all-start.1 = ((bf16[8,80,128]{2,1,0:T(8,128)(2,1)}), bf16[8,80,128]{2,1,0:T(8,128)(2,1)S(1)}, u32[]{:S(2)}, u32[]{:S(2)}) async-start(bf16[8,80,128]{2,1,0:T(8,128)(2,1)} %route_query.1), calls=%async_computation.1 | async-start | bytes 327680 | tf_op jit(solution)/shard_map/all_to_all | solution.py:394
  31.3 1.5 %copy-done.1 = bf16[2,256,2048]{2,1,0:T(8,128)(2,1)S(1)} copy-done((bf16[2,256,2048]{2,1,0:T(8,128)(2,1)S(1)}, bf16[2,256,2048]{2,1,0:T(8,128)(2,1)}, u32[]{:S(2)}) %copy-start.1) | copy-done | bytes 2097176
  32.8 1.7 %copy-done.7 = bf16[2048,640]{1,0:T(8,128)(2,1)S(1)} copy-done((bf16[2048,640]{1,0:T(8,128)(2,1)S(1)}, bf16[2048,640]{1,0:T(8,128)(2,1)}, u32[]{:S(2)}) %copy-start.7) | copy-done | bytes 2621464
  35.6 3.9 %fresh.1.refs_5_.refs_1_ = bf16[2,5,256,128]{3,2,1,0:T(8,128)(2,1)S(1)} custom-call(s32[3,16]{1,0:T(4,128)S(1)} %pad_add_fusion.meta, bf16[2,256,2048]{2,1,0:T(8,128)(2,1)S(1)} %copy-done.1, f32[1,2048]{1,0:T(1,128)S(1)} %bitcast.17, bf16[2048,640]{1,0:T(8,128)(2,1)S(1)} %copy-done.7, f32[1,64]{1,0:T(1,128)S(1)} %bitcast.18, f32[2,408,128]{2,1,0:T(8,128)S(1)} %copy-done.8, ...), custom_call_target="tpu_custom_call" | custom-call | bytes 1024 | tf_op jit(solution)/shard_map/fresh/pallas_call | solution.py:494
  40.5 4.7 %all-to-all-done.1.q = bf16[8,80,128]{2,1,0:T(8,128)(2,1)S(1)} async-done(((bf16[8,80,128]{2,1,0:T(8,128)(2,1)}), bf16[8,80,128]{2,1,0:T(8,128)(2,1)S(1)}, u32[]{:S(2)}, u32[]{:S(2)}) %all-to-all-start.1) | async-done | bytes 163872 | tf_op jit(solution)/shard_map/all_to_all | solution.py:394
  45.1 1.5 %collective-permute-start.3 = (bf16[2,5,288,128]{3,2,1,0:T(8,128)(2,1)}, bf16[2,5,288,128]{3,2,1,0:T(8,128)(2,1)}, u32[]{:S(2)}, u32[]{:S(2)}) collective-permute-start(bf16[2,5,288,128]{3,2,1,0:T(8,128)(2,1)} %collective-permute-done.1.refs_1_), channel_id=1, source_target_pairs={{8,16},{12,20},{16,8},{20,12},{9,17},{13,21},{17,9},{21,13},{10,18... | collective-permute-start | bytes 2211848 | tf_op jit(solution)/shard_map/ppermute | solution.py:477
  46.7 2.0 %collective-permute-start.4 = (bf16[2,5,288,128]{3,2,1,0:T(8,128)(2,1)}, bf16[2,5,288,128]{3,2,1,0:T(8,128)(2,1)}, u32[]{:S(2)}, u32[]{:S(2)}) collective-permute-start(bf16[2,5,288,128]{3,2,1,0:T(8,128)(2,1)} %collective-permute-done.2.refs_2_), channel_id=1, source_target_pairs={{0,8},{4,12},{8,0},{12,4},{16,24},{20,28},{24,16},{28,20},{1,9},{5... | collective-permute-start | bytes 2211848 | tf_op jit(solution)/shard_map/ppermute | solution.py:477
  49.1 6.7 %attend_row.1 = bf16[8,96,128]{2,1,0:T(8,128)(2,1)} custom-call(s32[3,16]{1,0:T(4,128)} %copy-done.11, bf16[8,80,128]{2,1,0:T(8,128)(2,1)} %copy-done.15, bf16[2,2048,128]{2,1,0:T(8,128)(2,1)} %copy-done.3), custom_call_target="tpu_custom_call" | custom-call | flops 2684354560 | bytes 33554432 | tf_op jit(solution)/shard_map/attend_row/pallas_call | solution.py:542
  55.8 4.8 %all-to-all-start.2 = ((bf16[8,96,128]{2,1,0:T(8,128)(2,1)}), bf16[8,96,128]{2,1,0:T(8,128)(2,1)S(1)}, u32[]{:S(2)}, u32[]{:S(2)}) async-start(bf16[8,96,128]{2,1,0:T(8,128)(2,1)} %attend_row.1), calls=%async_computation.2 | async-start | bytes 393216 | tf_op jit(solution)/shard_map/all_to_all | solution.py:394
  62.1 2.8 %attend_new.1.near = f32[2,3,256,128]{3,2,1,0:T(8,128)S(1)} custom-call(bf16[8,2,80,128]{3,2,1,0:T(8,128)(2,1)S(1)} %copy-done.6, bf16[2,5,256,128]{3,2,1,0:T(8,128)(2,1)S(1)} %fresh.1.refs_5_.refs_1_), custom_call_target="tpu_custom_call" | custom-call | bytes 1024 | tf_op jit(solution)/shard_map/attend_new/pallas_call | solution.py:528
  65.8 3.0 %all-to-all-done.2.src.refs_7_ = bf16[8,96,128]{2,1,0:T(8,128)(2,1)S(1)} async-done(((bf16[8,96,128]{2,1,0:T(8,128)(2,1)}), bf16[8,96,128]{2,1,0:T(8,128)(2,1)S(1)}, u32[]{:S(2)}, u32[]{:S(2)}) %all-to-all-start.2) | async-done | bytes 196640 | tf_op jit(solution)/shard_map/all_to_all | solution.py:394
  70.2 4.1 %all-to-all-start.3 = ((bf16[8,2,96,128]{3,2,1,0:T(8,128)(2,1)}), bf16[8,2,96,128]{3,2,1,0:T(8,128)(2,1)}, u32[]{:S(2)}, u32[]{:S(2)}) async-start(bf16[8,2,96,128]{3,2,1,0:T(8,128)(2,1)} %bitcast.14), calls=%async_computation.3 | async-start | bytes 786432 | tf_op jit(solution)/shard_map/all_to_all | solution.py:394
  74.3 1.9 %collective-permute-start.7 = (bf16[2,5,288,128]{3,2,1,0:T(8,128)(2,1)}, bf16[2,5,288,128]{3,2,1,0:T(8,128)(2,1)}, u32[]{:S(2)}, u32[]{:S(2)}) collective-permute-start(bf16[2,5,288,128]{3,2,1,0:T(8,128)(2,1)} %collective-permute-done.3.refs_3_), channel_id=1, source_target_pairs={{0,8},{4,12},{8,0},{12,4},{16,24},{20,28},{24,16},{28,20},{1,9},{5... | collective-permute-start | bytes 2211848 | tf_op jit(solution)/shard_map/ppermute | solution.py:477
  76.2 3.8 %cache.2.refs_3_ = bf16[4,5,288,128]{3,2,1,0:T(8,128)(2,1)} custom-call(s32[3,16]{1,0:T(4,128)S(1)} %copy-done.12, bf16[2,5,288,128]{3,2,1,0:T(8,128)(2,1)} %pad_maximum_fusion.refs_0_, bf16[2,5,288,128]{3,2,1,0:T(8,128)(2,1)} %collective-permute-done.1.refs_1_, bf16[2,5,288,128]{3,2,1,0:T(8,128)(2,1)} %collective-permute-done.2.refs_2_, ...), custom_call_target="tpu_custom_call" | custom-call | bytes 1024 | tf_op jit(solution)/shard_map/cache/pallas_call | solution.py:558
  80.0 6.2 %all-to-all-done.3.far = bf16[8,2,96,128]{3,2,1,0:T(8,128)(2,1)} async-done(((bf16[8,2,96,128]{3,2,1,0:T(8,128)(2,1)}), bf16[8,2,96,128]{3,2,1,0:T(8,128)(2,1)}, u32[]{:S(2)}, u32[]{:S(2)}) %all-to-all-start.3) | async-done | bytes 393248 | tf_op jit(solution)/shard_map/all_to_all | solution.py:394
  87.3 2.0 %merge.1.m_a = bf16[2,640,128]{2,1,0:T(8,128)(2,1)S(1)} custom-call(s32[3,16]{1,0:T(4,128)S(1)} %copy-done.12, bf16[8,2,96,128]{3,2,1,0:T(8,128)(2,1)} %all-to-all-done.3.far, f32[2,3,256,128]{3,2,1,0:T(8,128)S(1)} %copy-done.5), custom_call_target="tpu_custom_call" | custom-call | bytes 1024 | tf_op jit(solution)/shard_map/merge/pallas_call | solution.py:591
  91.0 1.6 %copy-done.2 = bf16[2,256,2048]{2,1,0:T(8,128)(2,1)S(1)} copy-done((bf16[2,256,2048]{2,1,0:T(8,128)(2,1)S(1)}, bf16[2,256,2048]{2,1,0:T(8,128)(2,1)}, u32[]{:S(2)}) %copy-start.2) | copy-done | bytes 2097176
  92.6 3.3 %project_chip.1.after.refs_1_ = f32[2,256,2048]{2,1,0:T(8,128)S(1)} custom-call(bf16[2,640,128]{2,1,0:T(8,128)(2,1)S(1)} %merge.1.m_a, bf16[2,640,128]{2,1,0:T(8,128)(2,1)S(1)} %collective-permute-done.10.m_b, bf16[320,2048]{1,0:T(8,128)(2,1)S(1)} %copy-done.10, bf16[320,2048]{1,0:T(8,128)(2,1)} %collective-permute-done.11.refs_1_, ...), custom_call_target="tpu_custom_call" | custom-call | bytes 1024 | tf_op jit(solution)/shard_map/project_chip/pallas_call | solution.py:611
  95.9 1.7 %stage.1.refs_0_ = bf16[640,2048]{1,0:T(8,128)(2,1)S(1)} custom-call(bf16[320,2048]{1,0:T(8,128)(2,1)} %collective-permute-done.8.w_a, bf16[320,2048]{1,0:T(8,128)(2,1)} %collective-permute-done.9.w_b, f32[2,256,2048]{2,1,0:T(8,128)S(1)} %project_chip.1.after.refs_1_), custom_call_target="tpu_custom_call" | custom-call | bytes 1024 | tf_op jit(solution)/shard_map/stage/pallas_call | solution.py:624
  98.0 3.0 %cache.3 = bf16[4,5,288,128]{3,2,1,0:T(8,128)(2,1)} custom-call(s32[3,16]{1,0:T(4,128)S(1)} %copy-done.12, bf16[2,5,288,128]{3,2,1,0:T(8,128)(2,1)} %collective-permute-done.7.refs_0_, bf16[2,5,256,128]{3,2,1,0:T(8,128)(2,1)S(1)} %fresh.1.refs_5_.refs_1_, ...), custom_call_target="tpu_custom_call", output_to_operand_aliasing={{}: (4, {})} | custom-call | bytes 1024 | tf_op jit(solution)/shard_map/cache/pallas_call | solution.py:558
  101.1 1.6 %collective-permute-done.12.m_b = bf16[2,640,128]{2,1,0:T(8,128)(2,1)S(1)} collective-permute-done((bf16[2,640,128]{2,1,0:T(8,128)(2,1)S(1)}, bf16[2,640,128]{2,1,0:T(8,128)(2,1)S(1)}, u32[]{:S(2)}, u32[]{:S(2)}) %collective-permute-start.12) | collective-permute-done | bytes 327712 | tf_op jit(solution)/shard_map/ppermute | solution.py:390
  102.8 3.0 %project_rest.1 = bf16[2,256,2048]{2,1,0:T(8,128)(2,1)} custom-call(bf16[2,640,128]{2,1,0:T(8,128)(2,1)S(1)} %collective-permute-done.6.m_a, bf16[2,640,128]{2,1,0:T(8,128)(2,1)S(1)} %collective-permute-done.12.m_b, bf16[640,2048]{1,0:T(8,128)(2,1)S(1)} %stage.1.refs_0_, f32[2,256,2048]{2,1,0:T(8,128)S(1)} %project_chip.1.after.refs_1_), custom_call_target="tpu_custom_call" | custom-call | bytes 1024 | tf_op jit(solution)/shard_map/project_rest/pallas_call | solution.py:611
  (57 shorter events, 9.6 us)
Async XLA Ops:
  0.6 1.7 %copy-start = (bf16[1,5,2048,128]{3,2,1,0:T(8,128)(2,1)S(1)}, bf16[1,5,2048,128]{3,2,1,0:T(8,128)(2,1)}, u32[]{:S(2)}) copy-start(bf16[1,5,2048,128]{3,2,1,0:T(8,128)(2,1)} %param.19) | copy-start | bytes 7864324
  2.4 14.7 %collective-permute-start = (bf16[5,288,128]{2,1,0:T(8,128)(2,1)S(1)}, bf16[5,288,128]{2,1,0:T(8,128)(2,1)}, u32[]{:S(2)}, u32[]{:S(2)}) collective-permute-start(bf16[5,288,128]{2,1,0:T(8,128)(2,1)S(1)} %dynamic-slice_bitcast_fusion.1), channel_id=1, source_target_pairs={{0,4},{4,0},{8,12},{12,8},{16,20},{20,16},{24,28},{28,24},{1,5},{5... | collective-permute-start | bytes 1105928 | tf_op jit(solution)/shard_map/ppermute | solution.py:390
  10.5 14.0 %copy-start.16 = (s32[16]{0:T(128)S(1)}, s32[16]{0:T(128)}, u32[]{:S(2)}) copy-start(s32[16]{0:T(128)} %clen.1) | copy-start | bytes 196
  10.5 14.0 %copy-start.17 = (s32[16]{0:T(128)S(1)}, s32[16]{0:T(128)}, u32[]{:S(2)}) copy-start(s32[16]{0:T(128)} %cont.1) | copy-start | bytes 196
  10.5 14.0 %copy-start.18 = (s32[16]{0:T(128)S(1)}, s32[16]{0:T(128)}, u32[]{:S(2)}) copy-start(s32[16]{0:T(128)} %param.21) | copy-start | bytes 196
  10.5 15.9 %all-to-all-start = ((bf16[8,2,80,128]{3,2,1,0:T(8,128)(2,1)}), bf16[8,2,80,128]{3,2,1,0:T(8,128)(2,1)S(1)}, u32[]{:S(2)}, u32[]{:S(2)}) async-start(bf16[8,2,80,128]{3,2,1,0:T(8,128)(2,1)} %query.1.q), calls=%async_computation | async-start | bytes 655360 | tf_op jit(solution)/shard_map/all_to_all | solution.py:394
  15.6 45.1 %collective-permute-start.8 = (bf16[320,2048]{1,0:T(8,128)(2,1)}, bf16[320,2048]{1,0:T(8,128)(2,1)}, u32[]{:S(2)}, u32[]{:S(2)}) collective-permute-start(bf16[320,2048]{1,0:T(8,128)(2,1)} %refs_0_.1), channel_id=1, source_target_pairs={{0,2},{1,3},{2,0},{3,1},{4,6},{5,7},{6,4},{7,5},{8,10},{9,11},{10,... | collective-permute-start | bytes 3932168 | tf_op jit(solution)/shard_map/ppermute | solution.py:390
  17.1 14.2 %copy-start.13 = (f32[2048]{0:T(1024)S(1)}, f32[2048]{0:T(1024)}, u32[]{:S(2)}) copy-start(f32[2048]{0:T(1024)} %param.13) | copy-start | bytes 24580
  17.1 14.2 %copy-start.14 = (f32[64]{0:T(128)S(1)}, f32[64]{0:T(128)}, u32[]{:S(2)}) copy-start(f32[64]{0:T(128)} %param.18) | copy-start | bytes 772
  19.1 26.0 %collective-permute-start.2 = (bf16[2,5,288,128]{3,2,1,0:T(8,128)(2,1)}, bf16[2,5,288,128]{3,2,1,0:T(8,128)(2,1)}, u32[]{:S(2)}, u32[]{:S(2)}) collective-permute-start(bf16[2,5,288,128]{3,2,1,0:T(8,128)(2,1)} %pad_maximum_fusion.refs_0_), channel_id=1, source_target_pairs={{8,16},{12,20},{16,8},{20,12},{9,17},{13,21},{17,9},{21,13},{10,18... | collective-permute-start | bytes 2211848 | tf_op jit(solution)/shard_map/ppermute | solution.py:477
  20.6 24.5 %collective-permute-start.1 = (bf16[2,5,288,128]{3,2,1,0:T(8,128)(2,1)}, bf16[2,5,288,128]{3,2,1,0:T(8,128)(2,1)}, u32[]{:S(2)}, u32[]{:S(2)}) collective-permute-start(bf16[2,5,288,128]{3,2,1,0:T(8,128)(2,1)} %pad_maximum_fusion.refs_0_), channel_id=1, source_target_pairs={{0,8},{4,12},{8,0},{12,4},{16,24},{20,28},{24,16},{28,20},{1,9},{5... | collective-permute-start | bytes 2211848 | tf_op jit(solution)/shard_map/ppermute | solution.py:477
  24.6 14.9 %copy-start.11 = (s32[3,16]{1,0:T(4,128)}, s32[3,16]{1,0:T(4,128)S(1)}, u32[]{:S(2)}) copy-start(s32[3,16]{1,0:T(4,128)S(1)} %pad_add_fusion.meta) | copy-start | bytes 580
  27.8 17.3 %all-to-all-start.1 = ((bf16[8,80,128]{2,1,0:T(8,128)(2,1)}), bf16[8,80,128]{2,1,0:T(8,128)(2,1)S(1)}, u32[]{:S(2)}, u32[]{:S(2)}) async-start(bf16[8,80,128]{2,1,0:T(8,128)(2,1)} %route_query.1), calls=%async_computation.1 | async-start | bytes 327680 | tf_op jit(solution)/shard_map/all_to_all | solution.py:394
  31.2 1.6 %copy-start.1 = (bf16[2,256,2048]{2,1,0:T(8,128)(2,1)S(1)}, bf16[2,256,2048]{2,1,0:T(8,128)(2,1)}, u32[]{:S(2)}) copy-start(bf16[2,256,2048]{2,1,0:T(8,128)(2,1)} %refs_2_.1) | copy-start | bytes 6291460
  32.8 1.7 %copy-start.7 = (bf16[2048,640]{1,0:T(8,128)(2,1)S(1)}, bf16[2048,640]{1,0:T(8,128)(2,1)}, u32[]{:S(2)}) copy-start(bf16[2048,640]{1,0:T(8,128)(2,1)} %w.1) | copy-start | bytes 7864324
  34.5 1.0 copy-start.8
  45.1 4.0 %copy-start.15 = (bf16[8,80,128]{2,1,0:T(8,128)(2,1)}, bf16[8,80,128]{2,1,0:T(8,128)(2,1)S(1)}, u32[]{:S(2)}) copy-start(bf16[8,80,128]{2,1,0:T(8,128)(2,1)S(1)} %all-to-all-done.1.q) | copy-start | bytes 491524
  45.1 23.7 %collective-permute-start.3 = (bf16[2,5,288,128]{3,2,1,0:T(8,128)(2,1)}, bf16[2,5,288,128]{3,2,1,0:T(8,128)(2,1)}, u32[]{:S(2)}, u32[]{:S(2)}) collective-permute-start(bf16[2,5,288,128]{3,2,1,0:T(8,128)(2,1)} %collective-permute-done.1.refs_1_), channel_id=1, source_target_pairs={{8,16},{12,20},{16,8},{20,12},{9,17},{13,21},{17,9},{21,13},{10,18... | collective-permute-start | bytes 2211848 | tf_op jit(solution)/shard_map/ppermute | solution.py:477
  46.7 22.2 %collective-permute-start.4 = (bf16[2,5,288,128]{3,2,1,0:T(8,128)(2,1)}, bf16[2,5,288,128]{3,2,1,0:T(8,128)(2,1)}, u32[]{:S(2)}, u32[]{:S(2)}) collective-permute-start(bf16[2,5,288,128]{3,2,1,0:T(8,128)(2,1)} %collective-permute-done.2.refs_2_), channel_id=1, source_target_pairs={{0,8},{4,12},{8,0},{12,4},{16,24},{20,28},{24,16},{28,20},{1,9},{5... | collective-permute-start | bytes 2211848 | tf_op jit(solution)/shard_map/ppermute | solution.py:477
  48.7 17.1 %collective-permute-start.5 = (bf16[2,5,256,128]{3,2,1,0:T(8,128)(2,1)S(1)}, bf16[2,5,256,128]{3,2,1,0:T(8,128)(2,1)}, u32[]{:S(2)}, u32[]{:S(2)}) collective-permute-start(bf16[2,5,256,128]{3,2,1,0:T(8,128)(2,1)S(1)} %fresh.1.refs_5_.refs_1_), channel_id=1, source_target_pairs={{0,4},{4,0},{8,12},{12,8},{16,20},{20,16},{24,28},{28,24},{1,5},{5... | collective-permute-start | bytes 1966088 | tf_op jit(solution)/shard_map/ppermute | solution.py:390
  55.8 13.0 %copy-start.12 = (s32[3,16]{1,0:T(4,128)S(1)}, s32[3,16]{1,0:T(4,128)}, u32[]{:S(2)}) copy-start(s32[3,16]{1,0:T(4,128)} %copy-done.11) | copy-start | bytes 580
  55.8 13.0 %all-to-all-start.2 = ((bf16[8,96,128]{2,1,0:T(8,128)(2,1)}), bf16[8,96,128]{2,1,0:T(8,128)(2,1)S(1)}, u32[]{:S(2)}, u32[]{:S(2)}) async-start(bf16[8,96,128]{2,1,0:T(8,128)(2,1)} %attend_row.1), calls=%async_computation.2 | async-start | bytes 393216 | tf_op jit(solution)/shard_map/all_to_all | solution.py:394
  60.6 29.9 %collective-permute-start.11 = (bf16[320,2048]{1,0:T(8,128)(2,1)}, bf16[320,2048]{1,0:T(8,128)(2,1)}, u32[]{:S(2)}, u32[]{:S(2)}) collective-permute-start(bf16[320,2048]{1,0:T(8,128)(2,1)} %refs_0_.1), channel_id=1, source_target_pairs={{0,1},{1,0},{2,3},{3,2},{4,5},{5,4},{6,7},{7,6},{8,9},{9,8},{10,11... | collective-permute-start | bytes 3932168 | tf_op jit(solution)/shard_map/ppermute | solution.py:390
  60.6 35.3 %collective-permute-start.9 = (bf16[320,2048]{1,0:T(8,128)(2,1)}, bf16[320,2048]{1,0:T(8,128)(2,1)}, u32[]{:S(2)}, u32[]{:S(2)}) collective-permute-start(bf16[320,2048]{1,0:T(8,128)(2,1)} %collective-permute-done.8.w_a), channel_id=1, source_target_pairs={{0,1},{1,0},{2,3},{3,2},{4,5},{5,4},{6,7},{7,6},{8,9},{9,8},{10,11... | collective-permute-start | bytes 3932168 | tf_op jit(solution)/shard_map/ppermute | solution.py:390
  70.2 16.0 %all-to-all-start.3 = ((bf16[8,2,96,128]{3,2,1,0:T(8,128)(2,1)}), bf16[8,2,96,128]{3,2,1,0:T(8,128)(2,1)}, u32[]{:S(2)}, u32[]{:S(2)}) async-start(bf16[8,2,96,128]{3,2,1,0:T(8,128)(2,1)} %bitcast.14), calls=%async_computation.3 | async-start | bytes 786432 | tf_op jit(solution)/shard_map/all_to_all | solution.py:394
  74.3 23.7 %collective-permute-start.7 = (bf16[2,5,288,128]{3,2,1,0:T(8,128)(2,1)}, bf16[2,5,288,128]{3,2,1,0:T(8,128)(2,1)}, u32[]{:S(2)}, u32[]{:S(2)}) collective-permute-start(bf16[2,5,288,128]{3,2,1,0:T(8,128)(2,1)} %collective-permute-done.3.refs_3_), channel_id=1, source_target_pairs={{0,8},{4,12},{8,0},{12,4},{16,24},{20,28},{24,16},{28,20},{1,9},{5... | collective-permute-start | bytes 2211848 | tf_op jit(solution)/shard_map/ppermute | solution.py:477
  86.2 1.1 %copy-start.5 = (f32[2,3,256,128]{3,2,1,0:T(8,128)S(1)}, f32[2,3,256,128]{3,2,1,0:T(8,128)}, u32[]{:S(2)}) copy-start(f32[2,3,256,128]{3,2,1,0:T(8,128)} %copy-done.4) | copy-start | bytes 2359300
  87.3 3.7 %copy-start.10 = (bf16[320,2048]{1,0:T(8,128)(2,1)S(1)}, bf16[320,2048]{1,0:T(8,128)(2,1)}, u32[]{:S(2)}) copy-start(bf16[320,2048]{1,0:T(8,128)(2,1)} %refs_0_.1) | copy-start | bytes 3932164
  89.3 1.7 %collective-permute-start.10 = (bf16[2,640,128]{2,1,0:T(8,128)(2,1)S(1)}, bf16[2,640,128]{2,1,0:T(8,128)(2,1)S(1)}, u32[]{:S(2)}, u32[]{:S(2)}) collective-permute-start(bf16[2,640,128]{2,1,0:T(8,128)(2,1)S(1)} %merge.1.m_a), channel_id=1, source_target_pairs={{0,1},{1,0},{2,3},{3,2},{4,5},{5,4},{6,7},{7,6},{8,9},{9,8},{10,11... | collective-permute-start | bytes 983048 | tf_op jit(solution)/shard_map/ppermute | solution.py:390
  89.4 11.6 %collective-permute-start.6 = (bf16[2,640,128]{2,1,0:T(8,128)(2,1)S(1)}, bf16[2,640,128]{2,1,0:T(8,128)(2,1)S(1)}, u32[]{:S(2)}, u32[]{:S(2)}) collective-permute-start(bf16[2,640,128]{2,1,0:T(8,128)(2,1)S(1)} %merge.1.m_a), channel_id=1, source_target_pairs={{0,2},{1,3},{2,0},{3,1},{4,6},{5,7},{6,4},{7,5},{8,10},{9,11},{10,... | collective-permute-start | bytes 983048 | tf_op jit(solution)/shard_map/ppermute | solution.py:390
  91.0 1.6 %copy-start.2 = (bf16[2,256,2048]{2,1,0:T(8,128)(2,1)S(1)}, bf16[2,256,2048]{2,1,0:T(8,128)(2,1)}, u32[]{:S(2)}) copy-start(bf16[2,256,2048]{2,1,0:T(8,128)(2,1)} %refs_2_.1) | copy-start | bytes 6291460
  101.1 1.7 %collective-permute-start.12 = (bf16[2,640,128]{2,1,0:T(8,128)(2,1)S(1)}, bf16[2,640,128]{2,1,0:T(8,128)(2,1)S(1)}, u32[]{:S(2)}, u32[]{:S(2)}) collective-permute-start(bf16[2,640,128]{2,1,0:T(8,128)(2,1)S(1)} %collective-permute-done.6.m_a), channel_id=1, source_target_pairs={{0,1},{1,0},{2,3},{3,2},{4,5},{5,4},{6,7},{7,6},{8,9},{9,8},{10,11... | collective-permute-start | bytes 983048 | tf_op jit(solution)/shard_map/ppermute | solution.py:390
  (4 other events, 3.6 us)

commit v8 on v7

--- a/solution.py
+++ b/solution.py
@@ -534,7 +534,7 @@
             pl.BlockSpec((1, kv_heads, count, LANES), lambda b: (b, 0, 0, 0)),
         ],
         out_specs=pl.BlockSpec((1, 3, count, LANES), lambda b: (b, 0, 0, 0)),
-        compiler_params=params(),
+        compiler_params=params(60),
         cost_estimate=HINT,
         name="attend_new",
     )(q, fresh)

time: 106 us -> 105 us (level)
  waiting for transfers between devices: 18.3 us -> 16.2 us
  local copies, waits for them, and re-layouts: 12.4 us -> 10.7 us
  Pallas kernels: 37.3 us -> 38.7 us
    all_to_all x4, waiting for transfers between devices: 15.7 us -> 12.6 us  [exchanged(): return lax.all_to_all(value, 'req', split_axis=0, concat_axis=0, tiled=True)]
    pallas_call x1, Pallas kernels: 2.82 us -> 4.59 us  [on_device(): pl.pallas_call(functools.partial(local_kernel, groups), grid=(req_dev,),...]
    unnamed x38 -> x42, local copies, waits for them, and re-layouts: 12.3 us -> 10.6 us
    ppermute x5, waiting for transfers between devices: 0.37 us -> 1.85 us  [crossed(): return lax.ppermute(value, 'req', pairs)]
    pallas_call x2, Pallas kernels: 6.81 us -> 5.67 us  [fill_cache(): pl.pallas_call(functools.partial(cache_kernel, req_dev, span, steps), in_...]
  transfers between devices with their start and end apart: 17 -> 17, of which waited for: 7 -> 7; matrix products, arithmetic and copies ran while one was open for 2% -> 2% of each run, Pallas kernels for 32% -> 34%
where the time goes in v8:
time: 105 us; the launch traced here: 104 us
  Pallas kernels  38.7 us (37%)
  starting transfers between devices  35.3 us (34%)
  waiting for transfers between devices  16.2 us (15%)
  local copies, waits for them, and re-layouts  10.7 us (10%)
  other arithmetic  1.99 us (2%)
    all_to_all x4, starting transfers between devices, exchanged(): return lax.all_to_all(value, 'req', split_axis=0, concat_axis=0, tiled=True)  17.3 us
    all_to_all x4, waiting for transfers between devices, exchanged(): return lax.all_to_all(value, 'req', split_axis=0, concat_axis=0, tiled=True)  12.6 us
    ppermute x5, starting transfers between devices, crossed(): return lax.ppermute(value, 'req', pairs)  10.9 us
    unnamed x42, local copies, waits for them, and re-layouts  10.6 us
    ppermute x8, starting transfers between devices, permuted(): return lax.ppermute(value, axis, pairs)  7.16 us
    pallas_call x1, Pallas kernels, on_device(): pl.pallas_call(functools.partial(row_kernel, requests, count, heads, grou...  6.67 us
    pallas_call x2, Pallas kernels, project(): pl.pallas_call(functools.partial(project_kernel, 512), grid=(req_dev,), o...  6.26 us
    pallas_call x2, Pallas kernels, fill_cache(): pl.pallas_call(functools.partial(cache_kernel, req_dev, span, steps), in_...  5.67 us
  transfers between devices with their start and end apart: 17, of which 7 were waited for; matrix products, arithmetic and copies ran while one was open for 2% of the time, Pallas kernels for 34%

profile of v8, /device:TPU:0, one launch (start us, length us, event | category | flops | bytes accessed | tf_op | source)
XLA Modules:
  0.0 103.9 jit_solution(16458159646080311783)
XLA Ops:
  0.7 1.7 %copy-done = bf16[1,5,2048,128]{3,2,1,0:T(8,128)(2,1)S(1)} copy-done((bf16[1,5,2048,128]{3,2,1,0:T(8,128)(2,1)S(1)}, bf16[1,5,2048,128]{3,2,1,0:T(8,128)(2,1)}, u32[]{:S(2)}) %copy-start) | copy-done | bytes 2621464
  2.4 3.0 %collective-permute-start = (bf16[5,288,128]{2,1,0:T(8,128)(2,1)S(1)}, bf16[5,288,128]{2,1,0:T(8,128)(2,1)}, u32[]{:S(2)}, u32[]{:S(2)}) collective-permute-start(bf16[5,288,128]{2,1,0:T(8,128)(2,1)S(1)} %dynamic-slice_bitcast_fusion.1), channel_id=1, source_target_pairs={{0,4},{4,0},{8,12},{12,8},{16,20},{20,16},{24,28},{28,24},{1,5},{5... | collective-permute-start | bytes 1105928 | tf_op jit(solution)/shard_map/ppermute | solution.py:390
  5.4 5.1 %query.1.q = bf16[8,2,80,128]{3,2,1,0:T(8,128)(2,1)} custom-call(s32[16]{0:T(128)} %cont.1, s32[16]{0:T(128)} %clen.1, bf16[2,256,2048]{2,1,0:T(8,128)(2,1)} %refs_2_.1, f32[1,2048]{1,0:T(1,128)} %bitcast.15, bf16[320,2048]{1,0:T(8,128)(2,1)} %bitcast.18, f32[1,64]{1,0:T(1,128)} %bitcast.21, f32[2,408,128]{2,1,0:T(8,128)} %constant.49.clone.table), custom_call_target="tpu_custom_call" | custom-call | flops 805306368 | bytes 6291456 | tf_op jit(solution)/shard_map/query/pallas_call | solution.py:450
  10.6 5.0 %all-to-all-start = ((bf16[8,2,80,128]{3,2,1,0:T(8,128)(2,1)}), bf16[8,2,80,128]{3,2,1,0:T(8,128)(2,1)S(1)}, u32[]{:S(2)}, u32[]{:S(2)}) async-start(bf16[8,2,80,128]{3,2,1,0:T(8,128)(2,1)} %query.1.q), calls=%async_computation | async-start | bytes 655360 | tf_op jit(solution)/shard_map/all_to_all | solution.py:394
  15.6 1.5 %collective-permute-start.8 = (bf16[320,2048]{1,0:T(8,128)(2,1)}, bf16[320,2048]{1,0:T(8,128)(2,1)}, u32[]{:S(2)}, u32[]{:S(2)}) collective-permute-start(bf16[320,2048]{1,0:T(8,128)(2,1)} %refs_0_.1), channel_id=1, source_target_pairs={{0,2},{1,3},{2,0},{3,1},{4,6},{5,7},{6,4},{7,5},{8,10},{9,11},{10,... | collective-permute-start | bytes 3932168 | tf_op jit(solution)/shard_map/ppermute | solution.py:390
  17.1 2.0 %pad_maximum_fusion.refs_0_ = bf16[2,5,288,128]{3,2,1,0:T(8,128)(2,1)} fusion(bf16[1,5,288,128]{3,2,1,0:T(8,128)(2,1)} %bitcast.8, bf16[1,5,288,128]{3,2,1,0:T(8,128)(2,1)S(1)} %constant_dynamic-slice_fusion), kind=kLoop, calls=%fused_computation.1 | loop fusion | flops 368640 | bytes 1474560 | tf_op jit(solution)/shard_map/stack | solution.py:471
  19.1 1.5 %collective-permute-start.2 = (bf16[2,5,288,128]{3,2,1,0:T(8,128)(2,1)}, bf16[2,5,288,128]{3,2,1,0:T(8,128)(2,1)}, u32[]{:S(2)}, u32[]{:S(2)}) collective-permute-start(bf16[2,5,288,128]{3,2,1,0:T(8,128)(2,1)} %pad_maximum_fusion.refs_0_), channel_id=1, source_target_pairs={{8,16},{12,20},{16,8},{20,12},{9,17},{13,21},{17,9},{21,13},{10,18... | collective-permute-start | bytes 2211848 | tf_op jit(solution)/shard_map/ppermute | solution.py:477
  20.6 3.9 %collective-permute-start.1 = (bf16[2,5,288,128]{3,2,1,0:T(8,128)(2,1)}, bf16[2,5,288,128]{3,2,1,0:T(8,128)(2,1)}, u32[]{:S(2)}, u32[]{:S(2)}) collective-permute-start(bf16[2,5,288,128]{3,2,1,0:T(8,128)(2,1)} %pad_maximum_fusion.refs_0_), channel_id=1, source_target_pairs={{0,8},{4,12},{8,0},{12,4},{16,24},{20,28},{24,16},{28,20},{1,9},{5... | collective-permute-start | bytes 2211848 | tf_op jit(solution)/shard_map/ppermute | solution.py:477
  24.6 1.9 %all-to-all-done = bf16[8,2,80,128]{3,2,1,0:T(8,128)(2,1)S(1)} async-done(((bf16[8,2,80,128]{3,2,1,0:T(8,128)(2,1)}), bf16[8,2,80,128]{3,2,1,0:T(8,128)(2,1)S(1)}, u32[]{:S(2)}, u32[]{:S(2)}) %all-to-all-start) | async-done | bytes 327712 | tf_op jit(solution)/shard_map/all_to_all | solution.py:394
  27.8 3.4 %all-to-all-start.1 = ((bf16[8,80,128]{2,1,0:T(8,128)(2,1)}), bf16[8,80,128]{2,1,0:T(8,128)(2,1)S(1)}, u32[]{:S(2)}, u32[]{:S(2)}) async-start(bf16[8,80,128]{2,1,0:T(8,128)(2,1)} %route_query.1), calls=%async_computation.1 | async-start | bytes 327680 | tf_op jit(solution)/shard_map/all_to_all | solution.py:394
  31.4 1.5 %copy-done.1 = bf16[2,256,2048]{2,1,0:T(8,128)(2,1)S(1)} copy-done((bf16[2,256,2048]{2,1,0:T(8,128)(2,1)S(1)}, bf16[2,256,2048]{2,1,0:T(8,128)(2,1)}, u32[]{:S(2)}) %copy-start.1) | copy-done | bytes 2097176
  32.8 1.7 %copy-done.8 = bf16[2048,640]{1,0:T(8,128)(2,1)S(1)} copy-done((bf16[2048,640]{1,0:T(8,128)(2,1)S(1)}, bf16[2048,640]{1,0:T(8,128)(2,1)}, u32[]{:S(2)}) %copy-start.8) | copy-done | bytes 2621464
  35.6 3.9 %fresh.1.refs_5_.refs_1_ = bf16[2,5,256,128]{3,2,1,0:T(8,128)(2,1)S(1)} custom-call(s32[3,16]{1,0:T(4,128)S(1)} %pad_add_fusion.meta, bf16[2,256,2048]{2,1,0:T(8,128)(2,1)S(1)} %copy-done.1, f32[1,2048]{1,0:T(1,128)S(1)} %bitcast.16, bf16[2048,640]{1,0:T(8,128)(2,1)S(1)} %copy-done.8, f32[1,64]{1,0:T(1,128)S(1)} %bitcast.17, f32[2,408,128]{2,1,0:T(8,128)S(1)} %copy-done.11, ...), custom_call_target="tpu_custom_call" | custom-call | bytes 1024 | tf_op jit(solution)/shard_map/fresh/pallas_call | solution.py:494
  40.5 4.7 %all-to-all-done.1.q = bf16[8,80,128]{2,1,0:T(8,128)(2,1)S(1)} async-done(((bf16[8,80,128]{2,1,0:T(8,128)(2,1)}), bf16[8,80,128]{2,1,0:T(8,128)(2,1)S(1)}, u32[]{:S(2)}, u32[]{:S(2)}) %all-to-all-start.1) | async-done | bytes 163872 | tf_op jit(solution)/shard_map/all_to_all | solution.py:394
  45.1 1.5 %collective-permute-start.3 = (bf16[2,5,288,128]{3,2,1,0:T(8,128)(2,1)}, bf16[2,5,288,128]{3,2,1,0:T(8,128)(2,1)}, u32[]{:S(2)}, u32[]{:S(2)}) collective-permute-start(bf16[2,5,288,128]{3,2,1,0:T(8,128)(2,1)} %collective-permute-done.1.refs_1_), channel_id=1, source_target_pairs={{8,16},{12,20},{16,8},{20,12},{9,17},{13,21},{17,9},{21,13},{10,18... | collective-permute-start | bytes 2211848 | tf_op jit(solution)/shard_map/ppermute | solution.py:477
  46.7 2.0 %collective-permute-start.4 = (bf16[2,5,288,128]{3,2,1,0:T(8,128)(2,1)}, bf16[2,5,288,128]{3,2,1,0:T(8,128)(2,1)}, u32[]{:S(2)}, u32[]{:S(2)}) collective-permute-start(bf16[2,5,288,128]{3,2,1,0:T(8,128)(2,1)} %collective-permute-done.2.refs_2_), channel_id=1, source_target_pairs={{0,8},{4,12},{8,0},{12,4},{16,24},{20,28},{24,16},{28,20},{1,9},{5... | collective-permute-start | bytes 2211848 | tf_op jit(solution)/shard_map/ppermute | solution.py:477
  49.2 6.7 %attend_row.1 = bf16[8,96,128]{2,1,0:T(8,128)(2,1)} custom-call(s32[3,16]{1,0:T(4,128)} %copy-done.13, bf16[8,80,128]{2,1,0:T(8,128)(2,1)} %copy-done.17, bf16[2,2048,128]{2,1,0:T(8,128)(2,1)} %copy-done.6), custom_call_target="tpu_custom_call" | custom-call | flops 2684354560 | bytes 33554432 | tf_op jit(solution)/shard_map/attend_row/pallas_call | solution.py:542
  55.8 4.8 %all-to-all-start.2 = ((bf16[8,96,128]{2,1,0:T(8,128)(2,1)}), bf16[8,96,128]{2,1,0:T(8,128)(2,1)S(1)}, u32[]{:S(2)}, u32[]{:S(2)}) async-start(bf16[8,96,128]{2,1,0:T(8,128)(2,1)} %attend_row.1), calls=%async_computation.2 | async-start | bytes 393216 | tf_op jit(solution)/shard_map/all_to_all | solution.py:394
  61.1 4.6 %attend_new.1.near = f32[2,3,256,128]{3,2,1,0:T(8,128)} custom-call(bf16[8,2,80,128]{3,2,1,0:T(8,128)(2,1)} %query.1.q, bf16[2,5,256,128]{3,2,1,0:T(8,128)(2,1)} %copy-done.3), custom_call_target="tpu_custom_call" | custom-call | bytes 1024 | tf_op jit(solution)/shard_map/attend_new/pallas_call | solution.py:528
  65.7 2.7 %all-to-all-done.2.src.refs_7_ = bf16[8,96,128]{2,1,0:T(8,128)(2,1)S(1)} async-done(((bf16[8,96,128]{2,1,0:T(8,128)(2,1)}), bf16[8,96,128]{2,1,0:T(8,128)(2,1)S(1)}, u32[]{:S(2)}, u32[]{:S(2)}) %all-to-all-start.2) | async-done | bytes 196640 | tf_op jit(solution)/shard_map/all_to_all | solution.py:394
  69.8 4.1 %all-to-all-start.3 = ((bf16[8,2,96,128]{3,2,1,0:T(8,128)(2,1)}), bf16[8,2,96,128]{3,2,1,0:T(8,128)(2,1)}, u32[]{:S(2)}, u32[]{:S(2)}) async-start(bf16[8,2,96,128]{3,2,1,0:T(8,128)(2,1)} %bitcast.11), calls=%async_computation.3 | async-start | bytes 786432 | tf_op jit(solution)/shard_map/all_to_all | solution.py:394
  73.9 1.9 %collective-permute-start.7 = (bf16[2,5,288,128]{3,2,1,0:T(8,128)(2,1)}, bf16[2,5,288,128]{3,2,1,0:T(8,128)(2,1)}, u32[]{:S(2)}, u32[]{:S(2)}) collective-permute-start(bf16[2,5,288,128]{3,2,1,0:T(8,128)(2,1)} %collective-permute-done.3.refs_3_), channel_id=1, source_target_pairs={{0,8},{4,12},{8,0},{12,4},{16,24},{20,28},{24,16},{28,20},{1,9},{5... | collective-permute-start | bytes 2211848 | tf_op jit(solution)/shard_map/ppermute | solution.py:477
  77.8 4.4 %cache.2.refs_3_ = bf16[4,5,288,128]{3,2,1,0:T(8,128)(2,1)} custom-call(s32[3,16]{1,0:T(4,128)S(1)} %copy-done.14, bf16[2,5,288,128]{3,2,1,0:T(8,128)(2,1)} %pad_maximum_fusion.refs_0_, bf16[2,5,288,128]{3,2,1,0:T(8,128)(2,1)} %collective-permute-done.1.refs_1_, bf16[2,5,288,128]{3,2,1,0:T(8,128)(2,1)} %collective-permute-done.2.refs_2_, ...), custom_call_target="tpu_custom_call" | custom-call | bytes 1024 | tf_op jit(solution)/shard_map/cache/pallas_call | solution.py:558
  82.2 3.5 %all-to-all-done.3.far = bf16[8,2,96,128]{3,2,1,0:T(8,128)(2,1)} async-done(((bf16[8,2,96,128]{3,2,1,0:T(8,128)(2,1)}), bf16[8,2,96,128]{3,2,1,0:T(8,128)(2,1)}, u32[]{:S(2)}, u32[]{:S(2)}) %all-to-all-start.3) | async-done | bytes 393248 | tf_op jit(solution)/shard_map/all_to_all | solution.py:394
  85.7 2.0 %merge.1.m_a = bf16[2,640,128]{2,1,0:T(8,128)(2,1)S(1)} custom-call(s32[3,16]{1,0:T(4,128)S(1)} %copy-done.14, bf16[8,2,96,128]{3,2,1,0:T(8,128)(2,1)} %all-to-all-done.3.far, f32[2,3,256,128]{3,2,1,0:T(8,128)S(1)} %copy-done.7), custom_call_target="tpu_custom_call" | custom-call | bytes 1024 | tf_op jit(solution)/shard_map/merge/pallas_call | solution.py:591
  87.8 1.5 %collective-permute-start.6 = (bf16[2,640,128]{2,1,0:T(8,128)(2,1)S(1)}, bf16[2,640,128]{2,1,0:T(8,128)(2,1)S(1)}, u32[]{:S(2)}, u32[]{:S(2)}) collective-permute-start(bf16[2,640,128]{2,1,0:T(8,128)(2,1)S(1)} %merge.1.m_a), channel_id=1, source_target_pairs={{0,2},{1,3},{2,0},{3,1},{4,6},{5,7},{6,4},{7,5},{8,10},{9,11},{10,... | collective-permute-start | bytes 983048 | tf_op jit(solution)/shard_map/ppermute | solution.py:390
  89.4 1.6 %copy-done.2 = bf16[2,256,2048]{2,1,0:T(8,128)(2,1)S(1)} copy-done((bf16[2,256,2048]{2,1,0:T(8,128)(2,1)S(1)}, bf16[2,256,2048]{2,1,0:T(8,128)(2,1)}, u32[]{:S(2)}) %copy-start.2) | copy-done | bytes 2097176
  91.0 3.3 %project_chip.1.after.refs_1_ = f32[2,256,2048]{2,1,0:T(8,128)S(1)} custom-call(bf16[2,640,128]{2,1,0:T(8,128)(2,1)S(1)} %merge.1.m_a, bf16[2,640,128]{2,1,0:T(8,128)(2,1)S(1)} %collective-permute-done.10.m_b, bf16[320,2048]{1,0:T(8,128)(2,1)S(1)} %copy-done.12, bf16[320,2048]{1,0:T(8,128)(2,1)} %collective-permute-done.11.refs_1_, ...), custom_call_target="tpu_custom_call" | custom-call | bytes 1024 | tf_op jit(solution)/shard_map/project_chip/pallas_call | solution.py:611
  94.3 1.8 %stage.1.refs_0_ = bf16[640,2048]{1,0:T(8,128)(2,1)S(1)} custom-call(bf16[320,2048]{1,0:T(8,128)(2,1)} %collective-permute-done.8.w_a, bf16[320,2048]{1,0:T(8,128)(2,1)} %collective-permute-done.9.w_b, f32[2,256,2048]{2,1,0:T(8,128)S(1)} %project_chip.1.after.refs_1_), custom_call_target="tpu_custom_call" | custom-call | bytes 1024 | tf_op jit(solution)/shard_map/stage/pallas_call | solution.py:624
  96.1 1.8 %collective-permute-done.7.refs_0_ = bf16[2,5,288,128]{3,2,1,0:T(8,128)(2,1)} collective-permute-done((bf16[2,5,288,128]{3,2,1,0:T(8,128)(2,1)}, bf16[2,5,288,128]{3,2,1,0:T(8,128)(2,1)}, u32[]{:S(2)}, u32[]{:S(2)}) %collective-permute-start.7) | collective-permute-done | bytes 737312 | tf_op jit(solution)/shard_map/ppermute | solution.py:477
  99.3 1.6 %collective-permute-done.12.m_b = bf16[2,640,128]{2,1,0:T(8,128)(2,1)S(1)} collective-permute-done((bf16[2,640,128]{2,1,0:T(8,128)(2,1)S(1)}, bf16[2,640,128]{2,1,0:T(8,128)(2,1)S(1)}, u32[]{:S(2)}, u32[]{:S(2)}) %collective-permute-start.12) | collective-permute-done | bytes 327712 | tf_op jit(solution)/shard_map/ppermute | solution.py:390
  100.9 3.0 %project_rest.1 = bf16[2,256,2048]{2,1,0:T(8,128)(2,1)} custom-call(bf16[2,640,128]{2,1,0:T(8,128)(2,1)S(1)} %collective-permute-done.6.m_a, bf16[2,640,128]{2,1,0:T(8,128)(2,1)S(1)} %collective-permute-done.12.m_b, bf16[640,2048]{1,0:T(8,128)(2,1)S(1)} %stage.1.refs_0_, f32[2,256,2048]{2,1,0:T(8,128)S(1)} %project_chip.1.after.refs_1_), custom_call_target="tpu_custom_call" | custom-call | bytes 1024 | tf_op jit(solution)/shard_map/project_rest/pallas_call | solution.py:611
  (61 shorter events, 9.4 us)
Async XLA Ops:
  0.6 1.7 %copy-start = (bf16[1,5,2048,128]{3,2,1,0:T(8,128)(2,1)S(1)}, bf16[1,5,2048,128]{3,2,1,0:T(8,128)(2,1)}, u32[]{:S(2)}) copy-start(bf16[1,5,2048,128]{3,2,1,0:T(8,128)(2,1)} %param.19) | copy-start | bytes 7864324
  2.4 14.7 %collective-permute-start = (bf16[5,288,128]{2,1,0:T(8,128)(2,1)S(1)}, bf16[5,288,128]{2,1,0:T(8,128)(2,1)}, u32[]{:S(2)}, u32[]{:S(2)}) collective-permute-start(bf16[5,288,128]{2,1,0:T(8,128)(2,1)S(1)} %dynamic-slice_bitcast_fusion.1), channel_id=1, source_target_pairs={{0,4},{4,0},{8,12},{12,8},{16,20},{20,16},{24,28},{28,24},{1,5},{5... | collective-permute-start | bytes 1105928 | tf_op jit(solution)/shard_map/ppermute | solution.py:390
  10.5 14.0 %copy-start.18 = (s32[16]{0:T(128)S(1)}, s32[16]{0:T(128)}, u32[]{:S(2)}) copy-start(s32[16]{0:T(128)} %clen.1) | copy-start | bytes 196
  10.5 14.0 %copy-start.19 = (s32[16]{0:T(128)S(1)}, s32[16]{0:T(128)}, u32[]{:S(2)}) copy-start(s32[16]{0:T(128)} %cont.1) | copy-start | bytes 196
  10.6 14.0 %copy-start.20 = (s32[16]{0:T(128)S(1)}, s32[16]{0:T(128)}, u32[]{:S(2)}) copy-start(s32[16]{0:T(128)} %param.21) | copy-start | bytes 196
  10.6 15.9 %all-to-all-start = ((bf16[8,2,80,128]{3,2,1,0:T(8,128)(2,1)}), bf16[8,2,80,128]{3,2,1,0:T(8,128)(2,1)S(1)}, u32[]{:S(2)}, u32[]{:S(2)}) async-start(bf16[8,2,80,128]{3,2,1,0:T(8,128)(2,1)} %query.1.q), calls=%async_computation | async-start | bytes 655360 | tf_op jit(solution)/shard_map/all_to_all | solution.py:394
  15.6 45.0 %collective-permute-start.8 = (bf16[320,2048]{1,0:T(8,128)(2,1)}, bf16[320,2048]{1,0:T(8,128)(2,1)}, u32[]{:S(2)}, u32[]{:S(2)}) collective-permute-start(bf16[320,2048]{1,0:T(8,128)(2,1)} %refs_0_.1), channel_id=1, source_target_pairs={{0,2},{1,3},{2,0},{3,1},{4,6},{5,7},{6,4},{7,5},{8,10},{9,11},{10,... | collective-permute-start | bytes 3932168 | tf_op jit(solution)/shard_map/ppermute | solution.py:390
  17.1 14.2 %copy-start.15 = (f32[2048]{0:T(1024)S(1)}, f32[2048]{0:T(1024)}, u32[]{:S(2)}) copy-start(f32[2048]{0:T(1024)} %param.13) | copy-start | bytes 24580
  17.1 14.2 %copy-start.16 = (f32[64]{0:T(128)S(1)}, f32[64]{0:T(128)}, u32[]{:S(2)}) copy-start(f32[64]{0:T(128)} %param.18) | copy-start | bytes 772
  19.1 26.0 %collective-permute-start.2 = (bf16[2,5,288,128]{3,2,1,0:T(8,128)(2,1)}, bf16[2,5,288,128]{3,2,1,0:T(8,128)(2,1)}, u32[]{:S(2)}, u32[]{:S(2)}) collective-permute-start(bf16[2,5,288,128]{3,2,1,0:T(8,128)(2,1)} %pad_maximum_fusion.refs_0_), channel_id=1, source_target_pairs={{8,16},{12,20},{16,8},{20,12},{9,17},{13,21},{17,9},{21,13},{10,18... | collective-permute-start | bytes 2211848 | tf_op jit(solution)/shard_map/ppermute | solution.py:477
  20.6 24.5 %collective-permute-start.1 = (bf16[2,5,288,128]{3,2,1,0:T(8,128)(2,1)}, bf16[2,5,288,128]{3,2,1,0:T(8,128)(2,1)}, u32[]{:S(2)}, u32[]{:S(2)}) collective-permute-start(bf16[2,5,288,128]{3,2,1,0:T(8,128)(2,1)} %pad_maximum_fusion.refs_0_), channel_id=1, source_target_pairs={{0,8},{4,12},{8,0},{12,4},{16,24},{20,28},{24,16},{28,20},{1,9},{5... | collective-permute-start | bytes 2211848 | tf_op jit(solution)/shard_map/ppermute | solution.py:477
  24.6 14.9 %copy-start.13 = (s32[3,16]{1,0:T(4,128)}, s32[3,16]{1,0:T(4,128)S(1)}, u32[]{:S(2)}) copy-start(s32[3,16]{1,0:T(4,128)S(1)} %pad_add_fusion.meta) | copy-start | bytes 580
  27.8 17.3 %all-to-all-start.1 = ((bf16[8,80,128]{2,1,0:T(8,128)(2,1)}), bf16[8,80,128]{2,1,0:T(8,128)(2,1)S(1)}, u32[]{:S(2)}, u32[]{:S(2)}) async-start(bf16[8,80,128]{2,1,0:T(8,128)(2,1)} %route_query.1), calls=%async_computation.1 | async-start | bytes 327680 | tf_op jit(solution)/shard_map/all_to_all | solution.py:394
  32.8 1.7 %copy-start.8 = (bf16[2048,640]{1,0:T(8,128)(2,1)S(1)}, bf16[2048,640]{1,0:T(8,128)(2,1)}, u32[]{:S(2)}) copy-start(bf16[2048,640]{1,0:T(8,128)(2,1)} %w.1) | copy-start | bytes 7864324
  40.5 20.6 %copy-start.3 = (bf16[2,5,256,128]{3,2,1,0:T(8,128)(2,1)}, bf16[2,5,256,128]{3,2,1,0:T(8,128)(2,1)S(1)}, u32[]{:S(2)}) copy-start(bf16[2,5,256,128]{3,2,1,0:T(8,128)(2,1)S(1)} %fresh.1.refs_5_.refs_1_) | copy-start | bytes 1966084
  45.1 4.0 %copy-start.17 = (bf16[8,80,128]{2,1,0:T(8,128)(2,1)}, bf16[8,80,128]{2,1,0:T(8,128)(2,1)S(1)}, u32[]{:S(2)}) copy-start(bf16[8,80,128]{2,1,0:T(8,128)(2,1)S(1)} %all-to-all-done.1.q) | copy-start | bytes 491524
  45.1 23.2 %collective-permute-start.3 = (bf16[2,5,288,128]{3,2,1,0:T(8,128)(2,1)}, bf16[2,5,288,128]{3,2,1,0:T(8,128)(2,1)}, u32[]{:S(2)}, u32[]{:S(2)}) collective-permute-start(bf16[2,5,288,128]{3,2,1,0:T(8,128)(2,1)} %collective-permute-done.1.refs_1_), channel_id=1, source_target_pairs={{8,16},{12,20},{16,8},{20,12},{9,17},{13,21},{17,9},{21,13},{10,18... | collective-permute-start | bytes 2211848 | tf_op jit(solution)/shard_map/ppermute | solution.py:477
  46.7 21.7 %collective-permute-start.4 = (bf16[2,5,288,128]{3,2,1,0:T(8,128)(2,1)}, bf16[2,5,288,128]{3,2,1,0:T(8,128)(2,1)}, u32[]{:S(2)}, u32[]{:S(2)}) collective-permute-start(bf16[2,5,288,128]{3,2,1,0:T(8,128)(2,1)} %collective-permute-done.2.refs_2_), channel_id=1, source_target_pairs={{0,8},{4,12},{8,0},{12,4},{16,24},{20,28},{24,16},{28,20},{1,9},{5... | collective-permute-start | bytes 2211848 | tf_op jit(solution)/shard_map/ppermute | solution.py:477
  48.7 17.0 %collective-permute-start.5 = (bf16[2,5,256,128]{3,2,1,0:T(8,128)(2,1)S(1)}, bf16[2,5,256,128]{3,2,1,0:T(8,128)(2,1)}, u32[]{:S(2)}, u32[]{:S(2)}) collective-permute-start(bf16[2,5,256,128]{3,2,1,0:T(8,128)(2,1)S(1)} %fresh.1.refs_5_.refs_1_), channel_id=1, source_target_pairs={{0,4},{4,0},{8,12},{12,8},{16,20},{20,16},{24,28},{28,24},{1,5},{5... | collective-permute-start | bytes 1966088 | tf_op jit(solution)/shard_map/ppermute | solution.py:390
  55.8 12.6 %copy-start.14 = (s32[3,16]{1,0:T(4,128)S(1)}, s32[3,16]{1,0:T(4,128)}, u32[]{:S(2)}) copy-start(s32[3,16]{1,0:T(4,128)} %copy-done.13) | copy-start | bytes 580
  55.8 12.6 %all-to-all-start.2 = ((bf16[8,96,128]{2,1,0:T(8,128)(2,1)}), bf16[8,96,128]{2,1,0:T(8,128)(2,1)S(1)}, u32[]{:S(2)}, u32[]{:S(2)}) async-start(bf16[8,96,128]{2,1,0:T(8,128)(2,1)} %attend_row.1), calls=%async_computation.2 | async-start | bytes 393216 | tf_op jit(solution)/shard_map/all_to_all | solution.py:394
  60.6 28.7 %collective-permute-start.11 = (bf16[320,2048]{1,0:T(8,128)(2,1)}, bf16[320,2048]{1,0:T(8,128)(2,1)}, u32[]{:S(2)}, u32[]{:S(2)}) collective-permute-start(bf16[320,2048]{1,0:T(8,128)(2,1)} %refs_0_.1), channel_id=1, source_target_pairs={{0,1},{1,0},{2,3},{3,2},{4,5},{5,4},{6,7},{7,6},{8,9},{9,8},{10,11... | collective-permute-start | bytes 3932168 | tf_op jit(solution)/shard_map/ppermute | solution.py:390
  60.6 33.7 %collective-permute-start.9 = (bf16[320,2048]{1,0:T(8,128)(2,1)}, bf16[320,2048]{1,0:T(8,128)(2,1)}, u32[]{:S(2)}, u32[]{:S(2)}) collective-permute-start(bf16[320,2048]{1,0:T(8,128)(2,1)} %collective-permute-done.8.w_a), channel_id=1, source_target_pairs={{0,1},{1,0},{2,3},{3,2},{4,5},{5,4},{6,7},{7,6},{8,9},{9,8},{10,11... | collective-permute-start | bytes 3932168 | tf_op jit(solution)/shard_map/ppermute | solution.py:390
  68.4 5.5 %copy-start.9 = (bf16[8,96,128]{2,1,0:T(8,128)(2,1)}, bf16[8,96,128]{2,1,0:T(8,128)(2,1)S(1)}, u32[]{:S(2)}) copy-start(bf16[8,96,128]{2,1,0:T(8,128)(2,1)S(1)} %all-to-all-done.2.src.refs_7_) | copy-start | bytes 589828
  69.8 15.9 %all-to-all-start.3 = ((bf16[8,2,96,128]{3,2,1,0:T(8,128)(2,1)}), bf16[8,2,96,128]{3,2,1,0:T(8,128)(2,1)}, u32[]{:S(2)}, u32[]{:S(2)}) async-start(bf16[8,2,96,128]{3,2,1,0:T(8,128)(2,1)} %bitcast.11), calls=%async_computation.3 | async-start | bytes 786432 | tf_op jit(solution)/shard_map/all_to_all | solution.py:394
  73.9 24.1 %collective-permute-start.7 = (bf16[2,5,288,128]{3,2,1,0:T(8,128)(2,1)}, bf16[2,5,288,128]{3,2,1,0:T(8,128)(2,1)}, u32[]{:S(2)}, u32[]{:S(2)}) collective-permute-start(bf16[2,5,288,128]{3,2,1,0:T(8,128)(2,1)} %collective-permute-done.3.refs_3_), channel_id=1, source_target_pairs={{0,8},{4,12},{8,0},{12,4},{16,24},{20,28},{24,16},{28,20},{1,9},{5... | collective-permute-start | bytes 2211848 | tf_op jit(solution)/shard_map/ppermute | solution.py:477
  77.8 7.9 %copy-start.7 = (f32[2,3,256,128]{3,2,1,0:T(8,128)S(1)}, f32[2,3,256,128]{3,2,1,0:T(8,128)}, u32[]{:S(2)}) copy-start(f32[2,3,256,128]{3,2,1,0:T(8,128)} %attend_new.1.near) | copy-start | bytes 2359300
  85.7 3.7 %copy-start.12 = (bf16[320,2048]{1,0:T(8,128)(2,1)S(1)}, bf16[320,2048]{1,0:T(8,128)(2,1)}, u32[]{:S(2)}) copy-start(bf16[320,2048]{1,0:T(8,128)(2,1)} %refs_0_.1) | copy-start | bytes 3932164
  87.7 1.7 %collective-permute-start.10 = (bf16[2,640,128]{2,1,0:T(8,128)(2,1)S(1)}, bf16[2,640,128]{2,1,0:T(8,128)(2,1)S(1)}, u32[]{:S(2)}, u32[]{:S(2)}) collective-permute-start(bf16[2,640,128]{2,1,0:T(8,128)(2,1)S(1)} %merge.1.m_a), channel_id=1, source_target_pairs={{0,1},{1,0},{2,3},{3,2},{4,5},{5,4},{6,7},{7,6},{8,9},{9,8},{10,11... | collective-permute-start | bytes 983048 | tf_op jit(solution)/shard_map/ppermute | solution.py:390
  87.8 11.4 %collective-permute-start.6 = (bf16[2,640,128]{2,1,0:T(8,128)(2,1)S(1)}, bf16[2,640,128]{2,1,0:T(8,128)(2,1)S(1)}, u32[]{:S(2)}, u32[]{:S(2)}) collective-permute-start(bf16[2,640,128]{2,1,0:T(8,128)(2,1)S(1)} %merge.1.m_a), channel_id=1, source_target_pairs={{0,2},{1,3},{2,0},{3,1},{4,6},{5,7},{6,4},{7,5},{8,10},{9,11},{10,... | collective-permute-start | bytes 983048 | tf_op jit(solution)/shard_map/ppermute | solution.py:390
  94.3 3.6 %copy-start.5 = (bf16[2,5,256,128]{3,2,1,0:T(8,128)(2,1)S(1)}, bf16[2,5,256,128]{3,2,1,0:T(8,128)(2,1)}, u32[]{:S(2)}) copy-start(bf16[2,5,256,128]{3,2,1,0:T(8,128)(2,1)} %copy-done.3) | copy-start | bytes 1966084
  99.2 1.7 %collective-permute-start.12 = (bf16[2,640,128]{2,1,0:T(8,128)(2,1)S(1)}, bf16[2,640,128]{2,1,0:T(8,128)(2,1)S(1)}, u32[]{:S(2)}, u32[]{:S(2)}) collective-permute-start(bf16[2,640,128]{2,1,0:T(8,128)(2,1)S(1)} %collective-permute-done.6.m_a), channel_id=1, source_target_pairs={{0,1},{1,0},{2,3},{3,2},{4,5},{5,4},{6,7},{7,6},{8,9},{9,8},{10,11... | collective-permute-start | bytes 983048 | tf_op jit(solution)/shard_map/ppermute | solution.py:390
  (6 other events, 7.2 us)
